TPU v7x, 512 devices: a whole 4x4x16 slice. The times are simulated.
512 devices in a mesh: gx: 32 (over z, core), gy: 16 (over x, y).
Axes of the slice: x: 4, y: 4, z: 16, core: 2. Of those that a mesh axis runs over, the one named last changes fastest.
Arguments:
- density: float32 [512, 128, 128], P('gx', 'gy'), may hold values from 0.05 to 0.95
- displacement: float32 [3, 512, 128, 128], P(None, 'gx', 'gy'), may hold values from -2 to 2
- passive: int32 [512, 128, 128], P('gx', 'gy'), may hold values from 0 to 2
Outputs:
- new_density: float32 [512, 128, 128], P('gx', 'gy')
- sensitivity: float32 [512, 128, 128], P('gx', 'gy')
All inputs are finite; a program needn't handle non-finite values.
Results may differ from a plain program's by a relative error of at most 0.0003.
Values sent between devices are 32-bit elements; how exact they have to be, the bound alone decides.
No kernel may reach another device: no remote copies, remote signals or barrier semaphores. Data moves between devices by JAX's collectives and lax.ppermute only.
A program may use at most 64 MiB of HBM per device.

v0:
```python
import math

import jax
import jax.numpy as jnp
import numpy as np
from jax import lax
from jax.sharding import PartitionSpec as P

BISECT = 8


BRACKET = 8.0
MOVE_LIMIT = 0.2
VOLUME_SHARE = 0.35
DERIVATIVE = 3.0 * (1.0 - 1e-09)
EDGE_WEIGHT = 1.5 - math.sqrt(2.0)


def extended_2(block, sides, width):
    for axis, dim in sides:
        count = lax.axis_size(axis)
        forward = [(i, i + 1) for i in range(count - 1)]
        backward = [(target, source) for source, target in forward]
        low = lax.ppermute(
            lax.slice_in_dim(block, block.shape[dim] - width, None, axis=dim), axis, forward
        )
        high = lax.ppermute(lax.slice_in_dim(block, 0, width, axis=dim), axis, backward)
        block = jnp.concatenate([low, block, high], axis=dim)
    return block


def passed_along(block, axis, distance):
    devices = range(lax.axis_size(axis))
    route = [(i - distance, i) for i in devices if i - distance in devices]
    return lax.ppermute(block, axis, route)


def element_stiffness():
    poisson = 0.3
    lame_first = poisson / ((1.0 + poisson) * (1.0 - 2.0 * poisson))
    shear_modulus = 0.5 / (1.0 + poisson)
    elastic = np.zeros((6, 6))
    elastic[:3, :3] = lame_first
    for entry in range(3):
        elastic[entry, entry] = lame_first + 2.0 * shear_modulus
        elastic[entry + 3, entry + 3] = shear_modulus
    points = [0.5 - 0.5 / math.sqrt(3.0), 0.5 + 0.5 / math.sqrt(3.0)]
    stiffness = np.zeros((24, 24))
    for point_x in points:
        for point_y in points:
            for point_z in points:
                strain = np.zeros((6, 24))
                for a in (0, 1):
                    for b in (0, 1):
                        for c in (0, 1):
                            corner = 4 * a + 2 * b + c
                            value_x = point_x if a else 1.0 - point_x
                            value_y = point_y if b else 1.0 - point_y
                            value_z = point_z if c else 1.0 - point_z
                            slope_x = (1.0 if a else -1.0) * value_y * value_z
                            slope_y = value_x * (1.0 if b else -1.0) * value_z
                            slope_z = value_x * value_y * (1.0 if c else -1.0)
                            strain[0, 3 * corner] = slope_x
                            strain[1, 3 * corner + 1] = slope_y
                            strain[2, 3 * corner + 2] = slope_z
                            strain[3, 3 * corner] = slope_y
                            strain[3, 3 * corner + 1] = slope_x
                            strain[4, 3 * corner + 1] = slope_z
                            strain[4, 3 * corner + 2] = slope_y
                            strain[5, 3 * corner] = slope_z
                            strain[5, 3 * corner + 2] = slope_x
                stiffness = stiffness + 0.125 * strain.T @ elastic @ strain
    return stiffness.astype(np.float32)


def block_matrices():
    placed = []
    for shift_x in (-1, 0, 1):
        for shift_y in (-1, 0, 1):
            for shift_z in (-1, 0, 1):
                matrix = np.zeros((64, 64), np.float32)
                for source in range(64):
                    for target_cell in range(64):
                        delta_x = 4 * shift_x + source // 16 - target_cell // 16
                        delta_y = 4 * shift_y + source // 4 % 4 - target_cell // 4 % 4
                        delta_z = 4 * shift_z + source % 4 - target_cell % 4
                        squared = delta_x * delta_x + delta_y * delta_y + delta_z * delta_z
                        if squared <= 2:
                            matrix[source, target_cell] = 1.5 - math.sqrt(squared)
                if np.any(matrix != 0.0):
                    placed.append(((shift_x, shift_y, shift_z), matrix))
    return placed


def weight_sums(index_x, index_y, index_z, count_x, count_y, count_z):
    along_x = (index_x > 0).astype(jnp.float32) + (index_x < count_x - 1).astype(jnp.float32)
    along_y = (index_y > 0).astype(jnp.float32) + (index_y < count_y - 1).astype(jnp.float32)
    along_z = (index_z > 0).astype(jnp.float32) + (index_z < count_z - 1).astype(jnp.float32)
    return (
        1.5
        + 0.5 * (along_x + along_y + along_z)
        + EDGE_WEIGHT * (along_x * along_y + along_x * along_z + along_y * along_z)
    )


def block_filter(extended):
    channels, wide_x, wide_y, planes = extended.shape
    padded = jnp.pad(extended, ((0, 0), (0, 0), (0, 0), (4, 4)))
    blocks_x = wide_x // 4
    blocks_y = wide_y // 4
    blocks_z = (planes + 8) // 4
    grouped = padded.reshape(channels, blocks_x, 4, blocks_y, 4, blocks_z, 4)
    grouped = grouped.transpose(0, 1, 3, 5, 2, 4, 6).reshape(
        channels, blocks_x, blocks_y, blocks_z, 64
    )
    inner_x = blocks_x - 2
    inner_y = blocks_y - 2
    inner_z = blocks_z - 2
    summed = jnp.zeros((channels, inner_x, inner_y, inner_z, 64), jnp.float32)
    for offset, matrix in block_matrices():
        sliced = grouped[
            :,
            1 + offset[0] : 1 + offset[0] + inner_x,
            1 + offset[1] : 1 + offset[1] + inner_y,
            1 + offset[2] : 1 + offset[2] + inner_z,
        ]
        summed = summed + jnp.dot(sliced, jnp.asarray(matrix), precision=lax.Precision.HIGHEST)
    summed = summed.reshape(channels, inner_x, inner_y, inner_z, 4, 4, 4).transpose(
        0, 1, 4, 2, 5, 3, 6
    )
    return summed.reshape(channels, inner_x * 4, inner_y * 4, inner_z * 4)


def per_device(density, displacement, passive):
    cols_x, cols_y, planes = density.shape
    total_x = cols_x * lax.axis_size("gx")
    total_y = cols_y * lax.axis_size("gy")
    start_x = lax.axis_index("gx") * cols_x
    start_y = lax.axis_index("gy") * cols_y
    index_x = (start_x + jnp.arange(cols_x, dtype=jnp.int32))[:, None, None]
    index_y = (start_y + jnp.arange(cols_y, dtype=jnp.int32))[None, :, None]
    index_z = jnp.arange(planes, dtype=jnp.int32)[None, None, :]
    sums = weight_sums(index_x, index_y, index_z, total_x, total_y, planes)
    nearby = extended_2(density, (("gx", 0), ("gy", 1)), 4)
    physical = block_filter(nearby[None])[0] / sums
    physical = jnp.where(passive == 1, 1.0, jnp.where(passive == 2, 0.0, physical))
    upper_x = passed_along(displacement[:, 0:1], "gx", -1)
    node_field = jnp.concatenate([displacement, upper_x], axis=1)
    upper_y = passed_along(node_field[:, :, 0:1], "gy", -1)
    node_field = jnp.concatenate([node_field, upper_y], axis=2)
    node_field = jnp.pad(node_field, ((0, 0), (0, 0), (0, 0), (0, 1)))
    stiffness = jnp.asarray(element_stiffness())

    def slab_energy(first):
        section = lax.dynamic_slice_in_dim(node_field, first, 9, 1)
        corners = [
            section[:, a : a + 8, b : b + cols_y, c : c + planes]
            for a in (0, 1)
            for b in (0, 1)
            for c in (0, 1)
        ]
        stacked = jnp.stack(corners, 0).reshape(24, 8 * cols_y * planes)
        mapped = jnp.dot(stiffness, stacked, precision=lax.Precision.HIGHEST)
        return jnp.sum(stacked * mapped, axis=0).reshape(8, cols_y, planes)

    starts = jnp.arange(cols_x // 8, dtype=jnp.int32) * 8
    energy = lax.map(slab_energy, starts).reshape(cols_x, cols_y, planes)
    raw_field = -DERIVATIVE * physical * physical * energy
    spread = raw_field / sums
    spread_rim = extended_2(spread, (("gx", 0), ("gy", 1)), 4)
    wide_x = (start_x - 4 + jnp.arange(cols_x + 8, dtype=jnp.int32))[:, None, None]
    wide_y = (start_y - 4 + jnp.arange(cols_y + 8, dtype=jnp.int32))[None, :, None]
    inside = (wide_x >= 0) & (wide_x < total_x) & (wide_y >= 0) & (wide_y < total_y)
    wide_sums = weight_sums(wide_x, wide_y, index_z, total_x, total_y, planes)
    inverse_rim = jnp.where(inside, 1.0 / wide_sums, 0.0)
    filtered = block_filter(jnp.stack([spread_rim, inverse_rim], 0))
    sensitivity = filtered[0]
    volume_weight = filtered[1]
    scaled = density * jnp.sqrt(-sensitivity / volume_weight)
    lower = jnp.where(
        passive == 0, jnp.maximum(density - MOVE_LIMIT, 0.0), jnp.where(passive == 1, 1.0, 0.0)
    )
    upper = jnp.where(
        passive == 0, jnp.minimum(density + MOVE_LIMIT, 1.0), jnp.where(passive == 1, 1.0, 0.0)
    )
    target = VOLUME_SHARE * total_x * total_y * planes
    lower_end = jnp.asarray(-BRACKET, jnp.float32)
    upper_end = jnp.asarray(BRACKET, jnp.float32)
    for bisection_step in range(BISECT):
        middle = 0.5 * (lower_end + upper_end)
        volume = lax.psum(
            jnp.sum(jnp.minimum(jnp.maximum(scaled * jnp.exp(-0.5 * middle), lower), upper)),
            ("gx", "gy"),
        )
        exceeds = volume > target
        lower_end = jnp.where(exceeds, middle, lower_end)
        upper_end = jnp.where(exceeds, upper_end, middle)
    middle = 0.5 * (lower_end + upper_end)
    new_density = jnp.minimum(jnp.maximum(scaled * jnp.exp(-0.5 * middle), lower), upper)
    return (new_density, sensitivity)


def solution(mesh):
    return jax.shard_map(
        per_device,
        mesh=mesh,
        in_specs=(P("gx", "gy", None), P(None, "gx", "gy", None), P("gx", "gy", None)),
        out_specs=(P("gx", "gy", None), P("gx", "gy", None)),
        check_vma=False,
    )
```

profile of v0, /device:TPU:1, one launch (start us, length us, event | category | flops | bytes accessed | tf_op | source)
XLA Modules:
  0.0 942.7 jit_solution(3248934166519166403)
XLA Ops:
  0.6 0.7 slice.199
  1.4 8.7 collective-permute-start.4
  10.1 0.7 fusion.44
  10.8 1.9 collective-permute-start.1
  12.8 3.6 collective-permute-start
  16.9 0.9 constant_dynamic-update-slice_fusion.4
  17.9 1.3 collective-permute-start.5
  19.2 0.8 constant_dynamic-update-slice_fusion.1
  20.1 4.0 collective-permute-start.2
  24.1 1.3 collective-permute-start.3
  25.5 8.2 while.11
  28.7 0.8 fusion.106
  32.8 0.8 fusion.106
  33.9 4.3 reshape.490
  38.2 6.0 copy.49
  45.6 0.7 convolution_add_fusion.34
  46.3 0.7 convolution_add_fusion.33
  47.0 0.7 convolution_add_fusion.32
  48.3 0.7 convolution_add_fusion.30
  49.0 0.7 convolution_add_fusion.29
  50.4 0.7 convolution_add_fusion.27
  53.8 0.7 convolution_add_fusion.22
  56.4 0.7 convolution_add_fusion.18
  57.2 0.8 copy.70
  58.1 1.6 squeeze_reshape.3
  59.9 2.5 collective-permute-start.6
  62.3 1.9 collective-permute-start.7
  64.4 3.0 collective-permute-done.7
  67.4 4.3 collective-permute-start.8
  71.7 1.3 collective-permute-start.9
  73.3 3.3 collective-permute-done.9
  76.9 7.3 reshape.513
  84.2 9.7 %copy.71 = f32[2,6,4,34,4,4,4]{3,6,5,4,2,1,0:T(4,128)S(1)} copy(f32[2,6,4,34,4,4,4]{6,3,5,2,4,1,0:T(8,128)} %bitcast.336) | data formatting | bytes 835584 | tf_op jit(solution)/shard_map/transpose | solution.py:113
  94.0 1.2 fusion.28
  95.1 1.0 convolution_add_fusion.17
  96.1 1.2 convolution_add_fusion.16
  97.3 1.2 convolution_add_fusion.15
  98.5 1.2 convolution_add_fusion.14
  99.7 1.0 convolution_add_fusion.13
  100.7 1.2 convolution_add_fusion.12
  101.9 1.2 convolution_add_fusion.11
  103.1 1.0 convolution_add_fusion.10
  104.1 1.2 convolution_add_fusion.9
  105.3 1.2 convolution_add_fusion.8
  106.4 1.0 convolution_add_fusion.7
  107.5 1.2 convolution_add_fusion.6
  108.6 1.4 convolution_add_fusion.5
  110.0 1.2 convolution_add_fusion.4
  111.2 1.0 convolution_add_fusion.3
  112.2 1.2 convolution_add_fusion.2
  113.4 1.2 convolution_add_fusion.1
  114.5 1.2 convolution_add_fusion
  115.9 0.8 copy.92
  116.8 1.6 squeeze.10
  118.4 0.8 copy.93
  119.3 1.6 squeeze.11
  121.6 112.3 %psum.56 = f32[]{:T(128)} all-reduce(f32[]{:T(128)} %get-tuple-element.53), channel_id=1, replica_groups=mesh['gx'=32,'gy'=16] {'gx','gy'}, use_global_device_ids=true, to_apply=%region_4.5 | all-reduce | flops 1 | bytes 8 | tf_op jit(solution)/shard_map/psum | solution.py:191
  235.2 99.2 %psum.57 = f32[]{:T(128)} all-reduce(f32[]{:T(128)} %minimum_reduce_fusion.6), channel_id=1, replica_groups=mesh['gx'=32,'gy'=16] {'gx','gy'}, use_global_device_ids=true, to_apply=%region_6.7 | all-reduce | flops 1 | bytes 8 | tf_op jit(solution)/shard_map/psum | solution.py:191
  335.6 100.5 %psum.58 = f32[]{:T(128)} all-reduce(f32[]{:T(128)} %minimum_reduce_fusion.5), channel_id=1, replica_groups=mesh['gx'=32,'gy'=16] {'gx','gy'}, use_global_device_ids=true, to_apply=%region_8.9 | all-reduce | flops 1 | bytes 8 | tf_op jit(solution)/shard_map/psum | solution.py:191
  437.5 99.3 %psum.59 = f32[]{:T(128)} all-reduce(f32[]{:T(128)} %minimum_reduce_fusion.4), channel_id=1, replica_groups=mesh['gx'=32,'gy'=16] {'gx','gy'}, use_global_device_ids=true, to_apply=%region_10.11 | all-reduce | flops 1 | bytes 8 | tf_op jit(solution)/shard_map/psum | solution.py:191
  538.1 100.2 %psum.60 = f32[]{:T(128)} all-reduce(f32[]{:T(128)} %minimum_reduce_fusion.3), channel_id=1, replica_groups=mesh['gx'=32,'gy'=16] {'gx','gy'}, use_global_device_ids=true, to_apply=%region_12.13 | all-reduce | flops 1 | bytes 8 | tf_op jit(solution)/shard_map/psum | solution.py:191
  639.6 99.3 %psum.61 = f32[]{:T(128)} all-reduce(f32[]{:T(128)} %minimum_reduce_fusion.2), channel_id=1, replica_groups=mesh['gx'=32,'gy'=16] {'gx','gy'}, use_global_device_ids=true, to_apply=%region_14.15 | all-reduce | flops 1 | bytes 8 | tf_op jit(solution)/shard_map/psum | solution.py:191
  740.3 100.1 %psum.62 = f32[]{:T(128)} all-reduce(f32[]{:T(128)} %minimum_reduce_fusion.1), channel_id=1, replica_groups=mesh['gx'=32,'gy'=16] {'gx','gy'}, use_global_device_ids=true, to_apply=%region_16.17 | all-reduce | flops 1 | bytes 8 | tf_op jit(solution)/shard_map/psum | solution.py:191
  841.7 99.4 %psum.63 = f32[]{:T(128)} all-reduce(f32[]{:T(128)} %minimum_reduce_fusion), channel_id=1, replica_groups=mesh['gx'=32,'gy'=16] {'gx','gy'}, use_global_device_ids=true, to_apply=%region_18.19 | all-reduce | flops 1 | bytes 8 | tf_op jit(solution)/shard_map/psum | solution.py:191
  (166 shorter events, 17.2 us)
Async XLA Ops:
  0.6 24.9 %copy-start.1 = (f32[24,24]{1,0:T(8,128)S(1)}, f32[24,24]{1,0:T(8,128)}, u32[]{:S(2)}) copy-start(f32[24,24]{1,0:T(8,128)} %constant.153.clone..sunk.2) | copy-start | bytes 6916
  1.4 16.5 %collective-permute-start.4 = (f32[3,1,8,128]{3,2,1,0:T(8,128)S(1)}, f32[3,1,8,128]{3,2,1,0:T(8,128)S(1)}, u32[]{:S(2)}, u32[]{:S(2)}) collective-permute-start(f32[3,1,8,128]{3,2,1,0:T(8,128)S(1)} %slice.199), channel_id=1, source_target_pairs={{16,0},{32,16},{48,32},{64,48},{80,64},{96,80},{112,96},{128,112},... | collective-permute-start | bytes 36872 | tf_op jit(solution)/shard_map/ppermute | solution.py:35
  10.8 9.2 collective-permute-start.1
  12.8 6.4 collective-permute-start
  17.9 7.5 collective-permute-start.5
  20.1 13.6 %collective-permute-start.2 = (f32[24,4,128]{2,1,0:T(4,128)S(1)}, f32[24,4,128]{2,1,0:T(4,128)S(1)}, u32[]{:S(2)}, u32[]{:S(2)}) collective-permute-start(f32[24,4,128]{2,1,0:T(4,128)S(1)} %get-tuple-element.61), channel_id=1, source_target_pairs={{0,1},{1,2},{2,3},{3,4},{4,5},{5,6},{6,7},{7,8},{8,9},{9,10},{10,1... | collective-permute-start | bytes 147464 | tf_op jit(solution)/shard_map/ppermute | solution.py:24
  24.1 9.6 %collective-permute-start.3 = (f32[24,4,128]{2,1,0:T(4,128)S(1)}, f32[24,4,128]{2,1,0:T(4,128)S(1)}, u32[]{:S(2)}, u32[]{:S(2)}) collective-permute-start(f32[24,4,128]{2,1,0:T(4,128)S(1)} %get-tuple-element.62), channel_id=1, source_target_pairs={{1,0},{2,1},{3,2},{4,3},{5,4},{6,5},{7,6},{8,7},{9,8},{10,9},{11,1... | collective-permute-start | bytes 147464 | tf_op jit(solution)/shard_map/ppermute | solution.py:27
  38.2 6.1 copy-start.41
  38.2 6.8 copy-start.40
  38.2 7.4 copy-start.39
  38.2 8.1 copy-start.38
  44.3 2.7 copy-start.37
  44.3 3.4 copy-start.36
  44.3 4.0 copy-start.35
  45.0 4.0 copy-start.34
  45.6 4.1 copy-start.33
  46.3 4.0 copy-start.32
  47.0 4.0 copy-start.31
  47.7 4.0 copy-start.30
  48.3 4.0 copy-start.29
  49.0 4.0 copy-start.28
  49.7 4.0 copy-start.27
  50.3 4.1 copy-start.26
  51.0 4.0 copy-start.25
  51.7 4.0 copy-start.24
  52.4 4.1 copy-start.23
  58.1 1.7 copy-start.3
  59.9 4.5 collective-permute-start.6
  62.3 5.1 collective-permute-start.7
  67.4 5.8 collective-permute-start.8
  71.7 4.8 collective-permute-start.9
  84.2 9.7 %copy-start.22 = (f32[64,64,1,1,1]{1,0,4,3,2:T(8,128)S(1)}, f32[64,64,1,1,1]{1,0,4,3,2:T(8,128)}, u32[]{:S(2)}) copy-start(f32[64,64,1,1,1]{1,0,4,3,2:T(8,128)} %constant.182) | copy-start | bytes 49156
  84.2 10.9 %copy-start.21 = (f32[64,64,1,1,1]{1,0,4,3,2:T(8,128)S(1)}, f32[64,64,1,1,1]{1,0,4,3,2:T(8,128)}, u32[]{:S(2)}) copy-start(f32[64,64,1,1,1]{1,0,4,3,2:T(8,128)} %constant.183) | copy-start | bytes 49156
  93.9 2.2 copy-start.20
  93.9 3.4 copy-start.19
  95.1 3.4 copy-start.18
  96.1 3.5 copy-start.17
  97.3 3.4 copy-start.16
  98.5 3.4 copy-start.15
  99.7 3.4 copy-start.14
  100.7 3.4 copy-start.13
  101.9 3.4 copy-start.12
  103.0 3.4 copy-start.11
  104.1 3.4 copy-start.10
  105.2 3.4 copy-start.9
  106.4 3.6 copy-start.8
  107.4 3.7 copy-start.7
  108.6 3.6 copy-start.6
  110.0 3.4 copy-start.5
  111.2 3.3 copy-start.4
  118.4 2.5 copy-start.2
  119.3 1.7 copy-start
where the time goes:
time: 948 us; the launch traced here: 943 us
  blocking collectives  810 us (85%)
  local copies, waits for them, and re-layouts  41.4 us (4%)
  matrix products  35.2 us (4%)
  starting transfers between devices  30.8 us (3%)
    psum x8, blocking collectives, per_device(): lax.psum(jnp.sum(jnp.minimum(jnp.maximum(scaled * jnp.exp(-0.5 * middle),...  810 us
    dot_general x38, matrix products, block_filter(): jnp.dot(sliced, jnp.asarray(matrix), precision=lax.Precision.HIGHEST)  33.6 us
  transfers between devices with their start and end apart: 10, of which 2 were waited for; matrix products, arithmetic and copies ran while one was open for 1% of the time, Pallas kernels for 0%

commit v1 on v0

v1 whole, which is shorter than its diff:
```python
import functools
import math

import jax
import jax.numpy as jnp
import numpy as np
from jax import lax
from jax.experimental import pallas as pl
from jax.experimental.pallas import tpu as pltpu
from jax.sharding import PartitionSpec as P

BISECT = 8
BRACKET = 8.0
MOVE_LIMIT = 0.2
VOLUME_SHARE = 0.35
DERIVATIVE = 3.0 * (1.0 - 1e-09)
EDGE_WEIGHT = 1.5 - math.sqrt(2.0)
POISSON = 0.3
LAME = POISSON / ((1.0 + POISSON) * (1.0 - 2.0 * POISSON))
SHEAR = 0.5 / (1.0 + POISSON)

NXL = 16
NYL = 8
NZ = 128
TRIALS = 2 ** BISECT - 1
SLOTS = TRIALS + 1
STEP = 2.0 * BRACKET / 2 ** BISECT

VMEM = pl.BlockSpec(memory_space=pltpu.VMEM)
SMEM = pl.BlockSpec(memory_space=pltpu.SMEM)


def trial_factors():
    middles = -BRACKET + STEP * np.arange(1, SLOTS + 1, dtype=np.float64)
    return np.exp(-0.5 * middles).astype(np.float32)


def pack_y(density, displacement, passive, to_low, to_high):
    for row in (0, 1):
        to_low[pl.ds(row * NXL, NXL), :] = density[:, row, :]
        to_high[pl.ds(row * NXL, NXL), :] = density[:, NYL - 2 + row, :]
    for c in range(3):
        for row in (0, 1):
            to_low[pl.ds((2 + 2 * c + row) * NXL, NXL), :] = displacement[c, :, row, :]
        to_high[pl.ds((2 + c) * NXL, NXL), :] = displacement[c, :, NYL - 1, :]
    to_low[pl.ds(8 * NXL, NXL), :] = passive[:, 0, :].astype(jnp.float32)
    to_high[pl.ds(5 * NXL, NXL), :] = passive[:, NYL - 1, :].astype(jnp.float32)


def pack_x(density, displacement, passive, y_high, y_low, to_low, to_high):
    for k in (0, 1):
        to_low[pl.ds(8 * k, 8), :] = density[k]
        to_high[pl.ds(8 * k, 8), :] = density[NXL - 2 + k]
    for c in range(3):
        for k in (0, 1):
            to_low[pl.ds(8 * (2 + 2 * c + k), 8), :] = displacement[c, k]
        to_high[pl.ds(8 * (2 + c), 8), :] = displacement[c, NXL - 1]
    to_low[pl.ds(64, 8), :] = passive[0].astype(jnp.float32)
    to_high[pl.ds(40, 8), :] = passive[NXL - 1].astype(jnp.float32)
    for base, first, out in ((72, 0, to_low), (48, NXL - 2, to_high)):
        for kind in range(9):
            out[pl.ds(base + 2 * kind, 2), :] = y_high[pl.ds(NXL * kind + first, 2), :]
        for kind in range(6):
            out[pl.ds(base + 18 + 2 * kind, 2), :] = y_low[pl.ds(NXL * kind + first, 2), :]
        out[pl.ds(base + 30, 2), :] = jnp.zeros((2, NZ), jnp.float32)


def z_sum(f, first, last):
    return jnp.where(first, 0.0, pltpu.roll(f, 1, 1)) + jnp.where(
        last, 0.0, pltpu.roll(f, NZ - 1, 1)
    )


def filter_terms(low, mid, high, first, last):
    across = z_sum(mid, first, last)
    along = low + high
    both = across + along
    side = 0.5 * mid + EDGE_WEIGHT * both
    rest = 1.5 * mid + 0.5 * both + EDGE_WEIGHT * z_sum(along, first, last)
    return side, rest


def corner_sums(here, above, last):
    total = here + above
    slope = above - here
    total_next = jnp.where(last, 0.0, pltpu.roll(total, NZ - 1, 1))
    slope_next = jnp.where(last, 0.0, pltpu.roll(slope, NZ - 1, 1))
    return (total + total_next, total_next - total, slope + slope_next, slope_next - slope)


def element_energy(before, after):
    modes = []
    for c in range(3):
        for k in range(4):
            low, high = before[4 * c + k], after[4 * c + k]
            modes.append((low + high, high - low))
    u, v, w = (
        {(a, k // 2, k % 2): modes[4 * c + k][a] for a in (0, 1) for k in range(4)}
        for c in range(3)
    )

    def sq(x):
        return x * x

    trace = sq(u[1, 0, 0] + v[0, 1, 0] + w[0, 0, 1]) + (1.0 / 3.0) * (
        sq(v[1, 1, 0] + w[1, 0, 1]) + sq(u[1, 1, 0] + w[0, 1, 1]) + sq(u[1, 0, 1] + v[0, 1, 1])
    )
    normal = sq(u[1, 0, 0]) + sq(v[0, 1, 0]) + sq(w[0, 0, 1])
    linear = (
        sq(v[1, 1, 0])
        + sq(w[1, 0, 1])
        + sq(u[1, 1, 0])
        + sq(w[0, 1, 1])
        + sq(u[1, 0, 1])
        + sq(v[0, 1, 1])
    )
    bilinear = sq(u[1, 1, 1]) + sq(v[1, 1, 1]) + sq(w[1, 1, 1])
    shear = (
        sq(u[0, 1, 0] + v[1, 0, 0]) + sq(u[0, 0, 1] + w[1, 0, 0]) + sq(v[0, 0, 1] + w[0, 1, 0])
    )
    twist = (
        sq(u[0, 1, 1] + v[1, 0, 1]) + sq(u[0, 1, 1] + w[1, 1, 0]) + sq(v[1, 0, 1] + w[1, 1, 0])
    )
    return (
        (LAME / 16.0) * trace
        + (SHEAR / 8.0) * normal
        + (SHEAR / 16.0) * (linear + shear)
        + ((LAME + 4.0 * SHEAR) / 144.0) * bilinear
        + (SHEAR / 48.0) * twist
    )


def update(
    factors,
    density,
    displacement,
    passive,
    y_high,
    y_low,
    x_high,
    x_low,
    sensitivity,
    scaled,
    sums_out,
    dens,
    disp,
    kind_of,
    spread,
    inverse,
    lower,
    upper,
    partial,
    *,
    copies,
):
    last_x = lax.axis_index("gx") == lax.axis_size("gx") - 1
    first_x = lax.axis_index("gx") == 0
    start_y = lax.axis_index("gy") * NYL
    total_y = lax.axis_size("gy") * NYL

    dens[pl.ds(2, NXL), pl.ds(2, NYL), :] = density[...]
    disp[:, pl.ds(1, NXL), pl.ds(1, NYL), :] = displacement[...]
    kind_of[pl.ds(1, NXL), pl.ds(1, NYL), :] = passive[...].astype(jnp.float32)
    for k in (0, 1):
        dens[pl.ds(2, NXL), NYL + 2 + k, :] = y_high[pl.ds(k * NXL, NXL), :]
        dens[pl.ds(2, NXL), k, :] = y_low[pl.ds(k * NXL, NXL), :]
        dens[NXL + 2 + k, pl.ds(2, NYL), :] = x_high[pl.ds(8 * k, 8), :]
        dens[k, pl.ds(2, NYL), :] = x_low[pl.ds(8 * k, 8), :]
        for row in (0, 1):
            dens[NXL + 2 + k, pl.ds(NYL + 2 + row, 1), :] = x_high[pl.ds(72 + 2 * row + k, 1), :]
            dens[NXL + 2 + k, pl.ds(row, 1), :] = x_high[pl.ds(90 + 2 * row + k, 1), :]
            dens[k, pl.ds(NYL + 2 + row, 1), :] = x_low[pl.ds(48 + 2 * row + k, 1), :]
            dens[k, pl.ds(row, 1), :] = x_low[pl.ds(66 + 2 * row + k, 1), :]
    for c in range(3):
        for k in (0, 1):
            at = 2 + 2 * c + k
            disp[c, pl.ds(1, NXL), NYL + 1 + k, :] = y_high[pl.ds(at * NXL, NXL), :]
            disp[c, NXL + 1 + k, pl.ds(1, NYL), :] = x_high[pl.ds(8 * at, 8), :]
            for row in (0, 1):
                disp[c, NXL + 1 + k, pl.ds(NYL + 1 + row, 1), :] = x_high[
                    pl.ds(72 + 2 * (2 + 2 * c + row) + k, 1), :
                ]
            disp[c, NXL + 1 + k, pl.ds(0, 1), :] = x_high[pl.ds(90 + 2 * (2 + c) + k, 1), :]
            disp[c, 0, pl.ds(NYL + 1 + k, 1), :] = x_low[pl.ds(48 + 2 * at + 1, 1), :]
        disp[c, pl.ds(1, NXL), 0, :] = y_low[pl.ds((2 + c) * NXL, NXL), :]
        disp[c, 0, pl.ds(1, NYL), :] = x_low[pl.ds(8 * (2 + c), 8), :]
        disp[c, 0, pl.ds(0, 1), :] = x_low[pl.ds(66 + 2 * (2 + c) + 1, 1), :]
    kind_of[pl.ds(1, NXL), NYL + 1, :] = y_high[pl.ds(8 * NXL, NXL), :]
    kind_of[pl.ds(1, NXL), 0, :] = y_low[pl.ds(5 * NXL, NXL), :]
    kind_of[NXL + 1, pl.ds(1, NYL), :] = x_high[pl.ds(64, 8), :]
    kind_of[0, pl.ds(1, NYL), :] = x_low[pl.ds(40, 8), :]
    kind_of[NXL + 1, pl.ds(NYL + 1, 1), :] = x_high[pl.ds(72 + 16, 1), :]
    kind_of[NXL + 1, pl.ds(0, 1), :] = x_high[pl.ds(90 + 10, 1), :]
    kind_of[0, pl.ds(NYL + 1, 1), :] = x_low[pl.ds(48 + 17, 1), :]
    kind_of[0, pl.ds(0, 1), :] = x_low[pl.ds(66 + 11, 1), :]

    lane = lax.broadcasted_iota(jnp.int32, (8, NZ), 1)
    first = lane == 0
    last = lane == NZ - 1
    along_z = jnp.where(first | last, 1.0, 2.0)

    for v in (0, 1):
        index_y = start_y - 1 + 8 * v + lax.broadcasted_iota(jnp.int32, (8, NZ), 0)
        inside = (index_y >= 0) & (index_y < total_y)
        along_y = jnp.where((index_y == 0) | (index_y == total_y - 1), 1.0, 2.0)
        base = 1.5 + 0.5 * (along_y + along_z) + EDGE_WEIGHT * along_y * along_z
        slope = 0.5 + EDGE_WEIGHT * (along_y + along_z)
        for slot, along_x in ((0, 2.0), (1, 1.0)):
            inverse[slot, pl.ds(8 * v, 8), :] = jnp.where(
                inside, 1.0 / (base + along_x * slope), 0.0
            )

    for v in (0, 1):
        rows = pl.ds(8 * v, 8)

        def density_terms(plane):
            return filter_terms(
                dens[plane, rows, :],
                dens[plane, pl.ds(8 * v + 1, 8), :],
                dens[plane, pl.ds(8 * v + 2, 8), :],
                first,
                last,
            )

        def node_plane(plane):
            return sum(
                (
                    corner_sums(
                        disp[c, plane, rows, :], disp[c, plane, pl.ds(8 * v + 1, 8), :], last
                    )
                    for c in range(3)
                ),
                (),
            )

        def rim_plane(j, carry):
            side_before, side_here, rest_here, nodes = carry
            side_after, rest_after = density_terms(j + 2)
            nodes_after = node_plane(j + 1)
            inner = inverse[0, rows, :]
            edge = inverse[1, rows, :]
            weight = jnp.where(
                ((j == 1) & first_x) | ((j == NXL) & last_x),
                edge,
                jnp.where(((j == 0) & first_x) | ((j == NXL + 1) & last_x), 0.0, inner),
            )
            physical = (rest_here + side_before + side_after) * weight
            kind = kind_of[j, rows, :]
            physical = jnp.where(kind == 1.0, 1.0, jnp.where(kind == 2.0, 0.0, physical))
            energy = element_energy(nodes, nodes_after)
            spread[j, rows, :] = -DERIVATIVE * physical * physical * energy * weight
            return side_here, side_after, rest_after, nodes_after

        side_0, _ = density_terms(0)
        side_1, rest_1 = density_terms(1)
        lax.fori_loop(0, NXL + 2, rim_plane, (side_0, side_1, rest_1, node_plane(0)))

    weights = []
    for slot in (0, 1):
        weights.append(
            filter_terms(
                inverse[slot, pl.ds(0, 8), :],
                inverse[slot, pl.ds(1, 8), :],
                inverse[slot, pl.ds(2, 8), :],
                first,
                last,
            )
        )
    (side_inner, rest_inner), (side_edge, rest_edge) = weights

    def spread_terms(plane):
        return filter_terms(
            spread[plane, pl.ds(0, 8), :],
            spread[plane, pl.ds(1, 8), :],
            spread[plane, pl.ds(2, 8), :],
            first,
            last,
        )

    def side_of(plane):
        return jnp.where(
            ((plane == 1) & first_x) | ((plane == NXL) & last_x),
            side_edge,
            jnp.where(
                ((plane == 0) & first_x) | ((plane == NXL + 1) & last_x), 0.0, side_inner
            ),
        )

    def out_plane(x, carry):
        side_before, side_here, rest_here = carry
        side_after, rest_after = spread_terms(x + 2)
        sens = rest_here + side_before + side_after
        rest_weight = jnp.where(
            ((x == 0) & first_x) | ((x == NXL - 1) & last_x), rest_edge, rest_inner
        )
        weight = rest_weight + side_of(x) + side_of(x + 2)
        here = density[x]
        kind = passive[x]
        sensitivity[x] = sens
        scaled[x] = here * jnp.sqrt(-sens / weight)
        fixed = jnp.where(kind == 1, 1.0, 0.0)
        lower[x] = jnp.where(kind == 0, jnp.maximum(here - MOVE_LIMIT, 0.0), fixed)
        upper[x] = jnp.where(kind == 0, jnp.minimum(here + MOVE_LIMIT, 1.0), fixed)
        return side_here, side_after, rest_after

    side_0, _ = spread_terms(0)
    side_1, rest_1 = spread_terms(1)
    lax.fori_loop(0, NXL, out_plane, (side_0, side_1, rest_1))

    def volume_group(g, carry):
        scales = [factors[8 * g + k] for k in range(8)]
        totals = [jnp.zeros((8, NZ), jnp.float32) for _ in range(8)]
        for x in range(NXL):
            values, floor, ceiling = scaled[x], lower[x], upper[x]
            for k in range(8):
                totals[k] += jnp.minimum(jnp.maximum(values * scales[k], floor), ceiling)
        for k in range(8):
            partial[pl.ds(pl.multiple_of(64 * g + 8 * k, 8), 8), :] = totals[k]
        return carry

    lax.fori_loop(0, SLOTS // 8, volume_group, 0)
    rows_of = [partial[pl.ds(s, SLOTS, stride=8), :] for s in range(8)]
    lines = ((rows_of[0] + rows_of[1]) + (rows_of[2] + rows_of[3])) + (
        (rows_of[4] + rows_of[5]) + (rows_of[6] + rows_of[7])
    )
    volumes = lax.dot_general(
        jnp.ones((8, NZ), jnp.float32),
        lines,
        (((1,), (1,)), ((), ())),
        precision=lax.Precision.HIGHEST,
        preferred_element_type=jnp.float32,
    )
    for copy in range(copies):
        for half in (0, 1):
            sums_out[copy, pl.ds(half, 1), :] = volumes[0:1, half * NZ : (half + 1) * NZ]


def add_copies(received, out, *, copies):
    total = jnp.sum(received[...], axis=0)
    for copy in range(copies):
        out[copy] = total


def finish(received, scaled, density, passive, new_density, *, target):
    volumes = jnp.sum(received[...], axis=0)
    slot = lax.broadcasted_iota(jnp.int32, (2, NZ), 0) * NZ + lax.broadcasted_iota(
        jnp.int32, (2, NZ), 1
    )
    above = jnp.sum(jnp.where((volumes > target) & (slot < TRIALS), 1.0, 0.0))
    middle = -BRACKET + STEP * above + 0.5 * STEP
    factor = jnp.exp(jnp.full((8, NZ), -0.5, jnp.float32) * middle)
    here = density[...]
    kind = passive[...]
    fixed = jnp.where(kind == 1, 1.0, 0.0)
    lower = jnp.where(kind == 0, jnp.maximum(here - MOVE_LIMIT, 0.0), fixed)
    upper = jnp.where(kind == 0, jnp.minimum(here + MOVE_LIMIT, 1.0), fixed)
    new_density[...] = jnp.minimum(jnp.maximum(scaled[...] * factor[None], lower), upper)


def f32(*shape):
    return jax.ShapeDtypeStruct(shape, jnp.float32)


def call(kernel, inputs, outputs, scratch=(), specs=None):
    return pl.pallas_call(
        kernel,
        out_shape=outputs,
        in_specs=specs or [VMEM] * inputs,
        out_specs=jax.tree.map(lambda _: VMEM, outputs),
        scratch_shapes=list(scratch),
    )


def shifted(block, axis, distance):
    devices = range(lax.axis_size(axis))
    route = [(i - distance, i) for i in devices if i - distance in devices]
    return lax.ppermute(block, axis, route)


def per_device(density, displacement, passive):
    count_x, count_y = lax.axis_size("gx"), lax.axis_size("gy")
    assert density.shape == (NXL, NYL, NZ)
    to_low, to_high = call(pack_y, 3, (f32(9 * NXL, NZ), f32(6 * NXL, NZ)))(
        density, displacement, passive
    )
    y_high = shifted(to_low, "gy", -1)
    y_low = shifted(to_high, "gy", 1)
    to_low, to_high = call(pack_x, 5, (f32(104, NZ), f32(80, NZ)))(
        density, displacement, passive, y_high, y_low
    )
    x_high = shifted(to_low, "gx", -1)
    x_low = shifted(to_high, "gx", 1)

    block = (NXL, NYL, NZ)
    plane = 2 * count_y
    layers = count_x // 2
    sensitivity, scaled, volumes = call(
        functools.partial(update, copies=plane),
        8,
        (f32(*block), f32(*block), f32(plane, 2, NZ)),
        (
            pltpu.VMEM((NXL + 4, 24, NZ), jnp.float32),
            pltpu.VMEM((3, NXL + 3, 24, NZ), jnp.float32),
            pltpu.VMEM((NXL + 2, 16, NZ), jnp.float32),
            pltpu.VMEM((NXL + 2, 16, NZ), jnp.float32),
            pltpu.VMEM((2, 16, NZ), jnp.float32),
            pltpu.VMEM(block, jnp.float32),
            pltpu.VMEM(block, jnp.float32),
            pltpu.VMEM((8 * SLOTS, NZ), jnp.float32),
        ),
        specs=[SMEM] + [VMEM] * 7,
    )(trial_factors(), density, displacement, passive, y_high, y_low, x_high, x_low)

    across = [
        [(2 * z + core) * count_y + y for core in (0, 1) for y in range(count_y)]
        for z in range(layers)
    ]
    along = [
        [(2 * z + core) * count_y + y for z in range(layers)]
        for core in (0, 1)
        for y in range(count_y)
    ]
    volumes = lax.all_to_all(volumes, ("gx", "gy"), 0, 0, axis_index_groups=across)
    volumes = call(functools.partial(add_copies, copies=layers), 1, f32(layers, 2, NZ))(volumes)
    volumes = lax.all_to_all(volumes, ("gx", "gy"), 0, 0, axis_index_groups=along)
    target = VOLUME_SHARE * (count_x * NXL) * (count_y * NYL) * NZ
    new_density = call(functools.partial(finish, target=target), 4, f32(*block))(
        volumes, scaled, density, passive
    )
    return new_density, sensitivity


def solution(mesh):
    return jax.shard_map(
        per_device,
        mesh=mesh,
        in_specs=(P("gx", "gy", None), P(None, "gx", "gy", None), P("gx", "gy", None)),
        out_specs=(P("gx", "gy", None), P("gx", "gy", None)),
        check_vma=False,
    )
```

time: 948 us -> 81 us (0.09)
  blocking collectives: 810 us -> 41.4 us
  local copies, waits for them, and re-layouts: 41.4 us -> 2.47 us
  matrix products: 35.2 us -> 0 us
  Pallas kernels: 0 us -> 16.1 us
  starting transfers between devices: 30.8 us -> 17.1 us
    psum x8 -> x0, blocking collectives: 810 us -> none  [per_device(): lax.psum(jnp.sum(jnp.minimum(jnp.maximum(scaled * jnp.exp(-0.5 * middle),...]
    all_to_all x0 -> x2, blocking collectives: none -> 41.4 us  [the longest x1 28.2 us: per_device(): lax.all_to_all(volumes, ('gx', 'gy'), 0, 0, axis_index_groups=along)]
    dot_general x40 -> x0, matrix products: 35.2 us -> none  [the longest x38 33.6 us: block_filter(): jnp.dot(sliced, jnp.asarray(matrix), precision=lax.Precision.HIGHEST)]
    transpose x3 -> x0, local copies, waits for them, and re-layouts: 16.5 us -> none  [the longest x2 15.7 us: block_filter(): grouped.transpose(0, 1, 3, 5, 2, 4, 6)]
    pallas_call x0 -> x5, Pallas kernels: none -> 16.1 us  [the longest x1 9.62 us: per_device(): call(functools.partial(update, copies=plane), 8, (f32(*block), f32(*block...]
    ppermute x10 -> x4, starting transfers between devices: 30.8 us -> 17.1 us  [shifted(): return lax.ppermute(block, axis, route)]
    reshape x4 -> x0, local copies, waits for them, and re-layouts: 12 us -> none  [the longest x2 11.7 us: block_filter(): grouped = padded.reshape(channels, blocks_x, 4, blocks_y, 4, blocks_z, 4)]
  transfers between devices with their start and end apart: 10 -> 4, of which waited for: 2 -> 2; matrix products, arithmetic and copies ran while one was open for 1% -> 0% of each run, Pallas kernels for 0% -> 0%
where the time goes in v1:
time: 81 us; the launch traced here: 80.5 us
  blocking collectives  41.4 us (51%)
  starting transfers between devices  17.1 us (21%)
  Pallas kernels  16.1 us (20%)
  waiting for transfers between devices  2.87 us (4%)
  local copies, waits for them, and re-layouts  2.47 us (3%)
    all_to_all x1, blocking collectives, per_device(): lax.all_to_all(volumes, ('gx', 'gy'), 0, 0, axis_index_groups=along)  28.2 us
    ppermute x4, starting transfers between devices, shifted(): return lax.ppermute(block, axis, route)  17.1 us
    all_to_all x1, blocking collectives, per_device(): lax.all_to_all(volumes, ('gx', 'gy'), 0, 0, axis_index_groups=across)  13.2 us
    pallas_call x1, Pallas kernels, per_device(): call(functools.partial(update, copies=plane), 8, (f32(*block), f32(*block...  9.62 us
    ppermute x4, waiting for transfers between devices, shifted(): return lax.ppermute(block, axis, route)  2.87 us
    unnamed x8, local copies, waits for them, and re-layouts  2.47 us
    pallas_call x1, Pallas kernels, per_device(): call(functools.partial(finish, target=target), 4, f32(*block))  1.7 us
    pallas_call x1, Pallas kernels, per_device(): call(pack_y, 3, (f32(9 * NXL, NZ), f32(6 * NXL, NZ)))  1.68 us
  transfers between devices with their start and end apart: 4, of which 2 were waited for; matrix products, arithmetic and copies ran while one was open for 0% of the time, Pallas kernels for 0%

profile of v1, /device:TPU:1, one launch (start us, length us, event | category | flops | bytes accessed | tf_op | source)
XLA Modules:
  0.0 80.5 jit_solution(16208511798834952466)
XLA Ops:
  0.6 1.7 %shard_map.59 = (f32[144,128]{1,0:T(8,128)}, f32[96,128]{1,0:T(8,128)}) custom-call(f32[16,8,128]{2,1,0:T(8,128)} %density.7, f32[3,16,8,128]{3,2,1,0:T(8,128)} %displacement.5, s32[16,8,128]{2,1,0:T(8,128)} %passive.7), custom_call_target="tpu_custom_call" | custom-call | tf_op jit(solution)/shard_map/pallas_call | solution.py:383
  2.3 1.3 %collective-permute-start = (f32[144,128]{1,0:T(8,128)}, f32[144,128]{1,0:T(8,128)S(1)}, u32[]{:S(2)}, u32[]{:S(2)}) collective-permute-start(f32[144,128]{1,0:T(8,128)} %get-tuple-element.9), channel_id=1, source_target_pairs={{1,0},{2,1},{3,2},{4,3},{5,4},{6,5},{7,6},{8,7},{9,8},{10,9},{11,1... | collective-permute-start | bytes 221192 | tf_op jit(solution)/shard_map/ppermute | solution.py:377
  3.6 4.6 %collective-permute-start.1 = (f32[96,128]{1,0:T(8,128)}, f32[96,128]{1,0:T(8,128)S(1)}, u32[]{:S(2)}, u32[]{:S(2)}) collective-permute-start(f32[96,128]{1,0:T(8,128)} %get-tuple-element.10), channel_id=1, source_target_pairs={{0,1},{1,2},{2,3},{3,4},{4,5},{5,6},{6,7},{7,8},{8,9},{9,10},{10,1... | collective-permute-start | bytes 147464 | tf_op jit(solution)/shard_map/ppermute | solution.py:377
  8.3 1.5 %collective-permute-done.1.y_low = f32[96,128]{1,0:T(8,128)S(1)} collective-permute-done((f32[96,128]{1,0:T(8,128)}, f32[96,128]{1,0:T(8,128)S(1)}, u32[]{:S(2)}, u32[]{:S(2)}) %collective-permute-start.1) | collective-permute-done | bytes 49184 | tf_op jit(solution)/shard_map/ppermute | solution.py:377
  9.7 0.0 copy-start.1
  9.7 0.0 collective-permute-done.y_high
  9.7 0.6 copy-done.1
  10.3 0.0 copy-start
  10.3 0.6 copy-done
  11.0 1.7 %shard_map.60 = (f32[104,128]{1,0:T(8,128)}, f32[80,128]{1,0:T(8,128)}) custom-call(f32[16,8,128]{2,1,0:T(8,128)} %density.7, f32[3,16,8,128]{3,2,1,0:T(8,128)} %displacement.5, s32[16,8,128]{2,1,0:T(8,128)} %passive.7, f32[144,128]{1,0:T(8,128)} %copy-done, f32[96,128]{1,0:T(8,128)} %copy-done.1), custom_call_target="tpu_custom_call" | custom-call | tf_op jit(solution)/shard_map/pallas_call | solution.py:388
  12.6 9.2 %collective-permute-start.2 = (f32[104,128]{1,0:T(8,128)}, f32[104,128]{1,0:T(8,128)S(1)}, u32[]{:S(2)}, u32[]{:S(2)}) collective-permute-start(f32[104,128]{1,0:T(8,128)} %get-tuple-element.11), channel_id=1, source_target_pairs={{16,0},{32,16},{48,32},{64,48},{80,64},{96,80},{112,96},{128,112},... | collective-permute-start | bytes 159752 | tf_op jit(solution)/shard_map/ppermute | solution.py:377
  21.8 1.9 %collective-permute-start.3 = (f32[80,128]{1,0:T(8,128)}, f32[80,128]{1,0:T(8,128)S(1)}, u32[]{:S(2)}, u32[]{:S(2)}) collective-permute-start(f32[80,128]{1,0:T(8,128)} %get-tuple-element.12), channel_id=1, source_target_pairs={{0,16},{16,32},{32,48},{48,64},{64,80},{80,96},{96,112},{112,128},... | collective-permute-start | bytes 122888 | tf_op jit(solution)/shard_map/ppermute | solution.py:377
  23.8 1.4 %collective-permute-done.3.x_low = f32[80,128]{1,0:T(8,128)S(1)} collective-permute-done((f32[80,128]{1,0:T(8,128)}, f32[80,128]{1,0:T(8,128)S(1)}, u32[]{:S(2)}, u32[]{:S(2)}) %collective-permute-start.3) | collective-permute-done | bytes 40992 | tf_op jit(solution)/shard_map/ppermute | solution.py:377
  25.2 0.0 copy-start.3
  25.2 0.0 collective-permute-done.2.x_high
  25.2 0.6 copy-done.3
  25.8 0.0 copy-start.2
  25.8 0.6 copy-done.2
  26.4 9.6 %shard_map.61 = (f32[16,8,128]{2,1,0:T(8,128)}, f32[16,8,128]{2,1,0:T(8,128)}, f32[32,2,128]{2,1,0:T(2,128)}) custom-call(f32[256]{0:T(256)} %constant.2.clone.factors, f32[16,8,128]{2,1,0:T(8,128)} %density.7, f32[3,16,8,128]{3,2,1,0:T(8,128)} %displacement.5, s32[16,8,128]{2,1,0:T(8,128)} %passive.7, f32[144,128]{1,0:T(8,128)} %copy-done, ...), custom_call_target="tpu_custom_call" | custom-call | tf_op jit(solution)/shard_map/pallas_call | solution.py:397
  36.0 13.2 %all_to_all.10.received = f32[32,2,128]{2,1,0:T(2,128)} all-to-all(f32[32,2,128]{2,1,0:T(2,128)} %get-tuple-element.13), channel_id=1, replica_groups={{0,1,2,3,4,5,6,7,8,9,10,11,12,13,14,15,16,17,18,19,20,21,22,23,24,25,26..., dimensions={0} | all-to-all | bytes 65536 | tf_op jit(solution)/shard_map/all_to_all | solution.py:423
  49.2 1.4 %shard_map.62 = f32[16,2,128]{2,1,0:T(2,128)} custom-call(f32[32,2,128]{2,1,0:T(2,128)} %all_to_all.10.received), custom_call_target="tpu_custom_call" | custom-call | tf_op jit(solution)/shard_map/pallas_call | solution.py:424
  50.6 28.2 %all_to_all.11.received = f32[16,2,128]{2,1,0:T(2,128)} all-to-all(f32[16,2,128]{2,1,0:T(2,128)} %shard_map.62), channel_id=1, replica_groups={{0,32,64,96,128,160,192,224,256,288,320,352,384,416,448,480},{1,33,65,9..., dimensions={0} | all-to-all | bytes 32768 | tf_op jit(solution)/shard_map/all_to_all | solution.py:425
  78.8 1.7 %shard_map.63 = f32[16,8,128]{2,1,0:T(8,128)} custom-call(f32[16,2,128]{2,1,0:T(2,128)} %all_to_all.11.received, f32[16,8,128]{2,1,0:T(8,128)} %get-tuple-element.14.scaled, f32[16,8,128]{2,1,0:T(8,128)} %density.7, s32[16,8,128]{2,1,0:T(8,128)} %passive.7), custom_call_target="tpu_custom_call" | custom-call | tf_op jit(solution)/shard_map/pallas_call | solution.py:427
Async XLA Ops:
  2.3 7.4 %collective-permute-start = (f32[144,128]{1,0:T(8,128)}, f32[144,128]{1,0:T(8,128)S(1)}, u32[]{:S(2)}, u32[]{:S(2)}) collective-permute-start(f32[144,128]{1,0:T(8,128)} %get-tuple-element.9), channel_id=1, source_target_pairs={{1,0},{2,1},{3,2},{4,3},{5,4},{6,5},{7,6},{8,7},{9,8},{10,9},{11,1... | collective-permute-start | bytes 221192 | tf_op jit(solution)/shard_map/ppermute | solution.py:377
  3.6 6.1 %collective-permute-start.1 = (f32[96,128]{1,0:T(8,128)}, f32[96,128]{1,0:T(8,128)S(1)}, u32[]{:S(2)}, u32[]{:S(2)}) collective-permute-start(f32[96,128]{1,0:T(8,128)} %get-tuple-element.10), channel_id=1, source_target_pairs={{0,1},{1,2},{2,3},{3,4},{4,5},{5,6},{6,7},{7,8},{8,9},{9,10},{10,1... | collective-permute-start | bytes 147464 | tf_op jit(solution)/shard_map/ppermute | solution.py:377
  9.7 0.6 copy-start.1
  10.3 0.6 copy-start
  12.6 12.5 %collective-permute-start.2 = (f32[104,128]{1,0:T(8,128)}, f32[104,128]{1,0:T(8,128)S(1)}, u32[]{:S(2)}, u32[]{:S(2)}) collective-permute-start(f32[104,128]{1,0:T(8,128)} %get-tuple-element.11), channel_id=1, source_target_pairs={{16,0},{32,16},{48,32},{64,48},{80,64},{96,80},{112,96},{128,112},... | collective-permute-start | bytes 159752 | tf_op jit(solution)/shard_map/ppermute | solution.py:377
  21.8 3.3 %collective-permute-start.3 = (f32[80,128]{1,0:T(8,128)}, f32[80,128]{1,0:T(8,128)S(1)}, u32[]{:S(2)}, u32[]{:S(2)}) collective-permute-start(f32[80,128]{1,0:T(8,128)} %get-tuple-element.12), channel_id=1, source_target_pairs={{0,16},{16,32},{32,48},{48,64},{64,80},{80,96},{96,112},{112,128},... | collective-permute-start | bytes 122888 | tf_op jit(solution)/shard_map/ppermute | solution.py:377
  25.2 0.6 copy-start.3
  25.8 0.6 copy-start.2

commit v2 on v1

--- a/solution.py
+++ b/solution.py
@@ -35,7 +35,23 @@
     return np.exp(-0.5 * middles).astype(np.float32)
 
 
-def pack_y(density, displacement, passive, to_low, to_high):
+def pack_y(
+    density_far, displacement_far, passive_far, density, displacement, passive, to_low, to_high, sems
+):
+    copies = [
+        pltpu.make_async_copy(far, local, sems.at[i])
+        for i, (far, local) in enumerate(
+            (
+                (density_far, density),
+                (displacement_far, displacement),
+                (passive_far, passive),
+            )
+        )
+    ]
+    for copy in copies:
+        copy.start()
+    for copy in copies:
+        copy.wait()
     for row in (0, 1):
         to_low[pl.ds(row * NXL, NXL), :] = density[:, row, :]
         to_high[pl.ds(row * NXL, NXL), :] = density[:, NYL - 2 + row, :]
@@ -361,6 +377,18 @@
     return jax.ShapeDtypeStruct(shape, jnp.float32)
 
 
+def near(*shape):
+    return pltpu.VMEM(shape, jnp.float32)
+
+
+def far(array):
+    return pltpu.with_memory_space_constraint(array, pltpu.HBM)
+
+
+def held(array):
+    return pltpu.with_memory_space_constraint(array, pltpu.VMEM)
+
+
 def call(kernel, inputs, outputs, scratch=(), specs=None):
     return pl.pallas_call(
         kernel,
@@ -368,6 +396,7 @@
         in_specs=specs or [VMEM] * inputs,
         out_specs=jax.tree.map(lambda _: VMEM, outputs),
         scratch_shapes=list(scratch),
+        compiler_params=pltpu.CompilerParams(vmem_limit_bytes=16 << 20),
     )
 
 
@@ -380,24 +409,34 @@
 def per_device(density, displacement, passive):
     count_x, count_y = lax.axis_size("gx"), lax.axis_size("gy")
     assert density.shape == (NXL, NYL, NZ)
-    to_low, to_high = call(pack_y, 3, (f32(9 * NXL, NZ), f32(6 * NXL, NZ)))(
-        density, displacement, passive
-    )
-    y_high = shifted(to_low, "gy", -1)
-    y_low = shifted(to_high, "gy", 1)
-    to_low, to_high = call(pack_x, 5, (f32(104, NZ), f32(80, NZ)))(
+    block = (NXL, NYL, NZ)
+    density, displacement, passive, to_low, to_high = call(
+        pack_y,
+        3,
+        (
+            near(*block),
+            near(3, *block),
+            pltpu.VMEM(block, jnp.int32),
+            near(9 * NXL, NZ),
+            near(6 * NXL, NZ),
+        ),
+        [pltpu.SemaphoreType.DMA((3,))],
+        specs=[pl.BlockSpec(memory_space=pltpu.HBM)] * 3,
+    )(far(density), far(displacement), far(passive))
+    y_high = held(shifted(to_low, "gy", -1))
+    y_low = held(shifted(to_high, "gy", 1))
+    to_low, to_high = call(pack_x, 5, (near(104, NZ), near(80, NZ)))(
         density, displacement, passive, y_high, y_low
     )
-    x_high = shifted(to_low, "gx", -1)
-    x_low = shifted(to_high, "gx", 1)
-
-    block = (NXL, NYL, NZ)
+    x_high = held(shifted(to_low, "gx", -1))
+    x_low = held(shifted(to_high, "gx", 1))
+
     plane = 2 * count_y
     layers = count_x // 2
     sensitivity, scaled, volumes = call(
         functools.partial(update, copies=plane),
         8,
-        (f32(*block), f32(*block), f32(plane, 2, NZ)),
+        (f32(*block), near(*block), near(plane, 2, NZ)),
         (
             pltpu.VMEM((NXL + 4, 24, NZ), jnp.float32),
             pltpu.VMEM((3, NXL + 3, 24, NZ), jnp.float32),
@@ -421,11 +460,11 @@
         for y in range(count_y)
     ]
     volumes = lax.all_to_all(volumes, ("gx", "gy"), 0, 0, axis_index_groups=across)
-    volumes = call(functools.partial(add_copies, copies=layers), 1, f32(layers, 2, NZ))(volumes)
+    volumes = call(functools.partial(add_copies, copies=layers), 1, near(layers, 2, NZ))(held(volumes))
     volumes = lax.all_to_all(volumes, ("gx", "gy"), 0, 0, axis_index_groups=along)
     target = VOLUME_SHARE * (count_x * NXL) * (count_y * NYL) * NZ
     new_density = call(functools.partial(finish, target=target), 4, f32(*block))(
-        volumes, scaled, density, passive
+        held(volumes), scaled, density, passive
     )
     return new_density, sensitivity
 

time: 81 us -> 72 us (0.89)
  Pallas kernels: 16.1 us -> 10.7 us
  local copies, waits for them, and re-layouts: 2.47 us -> 0.01 us
    pallas_call x4, Pallas kernels: 14.3 us -> 9.88 us  [the longest x1 8.76 us: per_device(): call(functools.partial(update, copies=plane), 8, (f32(*block), near(*bloc...]
    unnamed x8 -> x2, local copies, waits for them, and re-layouts: 2.47 us -> 0.01 us
    pallas_call x1, Pallas kernels: 1.7 us -> 0.78 us  [per_device(): call(functools.partial(finish, target=target), 4, f32(*block))]
where the time goes in v2:
time: 72 us; the launch traced here: 71.7 us
  blocking collectives  40.9 us (57%)
  starting transfers between devices  17.1 us (24%)
  Pallas kernels  10.7 us (15%)
  waiting for transfers between devices  2.35 us (3%)
    all_to_all x1, blocking collectives, per_device(): lax.all_to_all(volumes, ('gx', 'gy'), 0, 0, axis_index_groups=along)  28 us
    ppermute x4, starting transfers between devices, shifted(): return lax.ppermute(block, axis, route)  17.1 us
    all_to_all x1, blocking collectives, per_device(): lax.all_to_all(volumes, ('gx', 'gy'), 0, 0, axis_index_groups=across)  12.9 us
    pallas_call x1, Pallas kernels, per_device(): call(functools.partial(update, copies=plane), 8, (f32(*block), near(*bloc...  8.76 us
    ppermute x4, waiting for transfers between devices, shifted(): return lax.ppermute(block, axis, route)  2.35 us
  transfers between devices with their start and end apart: 4, of which 2 were waited for; matrix products, arithmetic and copies ran while one was open for 0% of the time, Pallas kernels for 0%

profile of v2, /device:TPU:1, one launch (start us, length us, event | category | flops | bytes accessed | tf_op | source)
XLA Modules:
  0.0 71.7 jit_solution(3473796357634219034)
XLA Ops:
  0.6 1.1 %shard_map.59 = (f32[16,8,128]{2,1,0:T(8,128)S(1)}, f32[3,16,8,128]{3,2,1,0:T(8,128)S(1)}, s32[16,8,128]{2,1,0:T(8,128)S(1)}, f32[144,128]{1,0:T(8,128)S(1)}, f32[96,128]{1,0:T(8,128)S(1)}) custom-call(f32[16,8,128]{2,1,0:T(8,128)} %density_far.1, f32[3,16,8,128]{3,2,1,0:T(8,128)} %displacement_far.1, s32[16,8,128]{2,1,0:T(8,128)} %passive_far.1), custom_call_target="tpu_custom_call" | custom-call | tf_op jit(solution)/shard_map/pallas_call | solution.py:413
  1.7 1.3 %collective-permute-start = (f32[144,128]{1,0:T(8,128)S(1)}, f32[144,128]{1,0:T(8,128)S(1)}, u32[]{:S(2)}, u32[]{:S(2)}) collective-permute-start(f32[144,128]{1,0:T(8,128)S(1)} %get-tuple-element.15), channel_id=1, source_target_pairs={{1,0},{2,1},{3,2},{4,3},{5,4},{6,5},{7,6},{8,7},{9,8},{10,9},{11,1... | collective-permute-start | bytes 221192 | tf_op jit(solution)/shard_map/ppermute | solution.py:406
  3.0 4.6 %collective-permute-start.1 = (f32[96,128]{1,0:T(8,128)S(1)}, f32[96,128]{1,0:T(8,128)S(1)}, u32[]{:S(2)}, u32[]{:S(2)}) collective-permute-start(f32[96,128]{1,0:T(8,128)S(1)} %get-tuple-element.16), channel_id=1, source_target_pairs={{0,1},{1,2},{2,3},{3,4},{4,5},{5,6},{6,7},{7,8},{8,9},{9,10},{10,1... | collective-permute-start | bytes 147464 | tf_op jit(solution)/shard_map/ppermute | solution.py:406
  7.7 1.2 %collective-permute-done.1.y_low = f32[96,128]{1,0:T(8,128)S(1)} collective-permute-done((f32[96,128]{1,0:T(8,128)S(1)}, f32[96,128]{1,0:T(8,128)S(1)}, u32[]{:S(2)}, u32[]{:S(2)}) %collective-permute-start.1) | collective-permute-done | bytes 49184 | tf_op jit(solution)/shard_map/ppermute | solution.py:406
  8.8 0.0 collective-permute-done.y_high
  8.8 0.0 copy-start
  8.9 9.2 %collective-permute-start.2 = (f32[104,128]{1,0:T(8,128)S(1)}, f32[104,128]{1,0:T(8,128)S(1)}, u32[]{:S(2)}, u32[]{:S(2)}) collective-permute-start(f32[104,128]{1,0:T(8,128)S(1)} %get-tuple-element.17), channel_id=1, source_target_pairs={{16,0},{32,16},{48,32},{64,48},{80,64},{96,80},{112,96},{128,112},... | collective-permute-start | bytes 159752 | tf_op jit(solution)/shard_map/ppermute | solution.py:406
  18.1 1.9 %collective-permute-start.3 = (f32[80,128]{1,0:T(8,128)S(1)}, f32[80,128]{1,0:T(8,128)S(1)}, u32[]{:S(2)}, u32[]{:S(2)}) collective-permute-start(f32[80,128]{1,0:T(8,128)S(1)} %get-tuple-element.18), channel_id=1, source_target_pairs={{0,16},{16,32},{32,48},{48,64},{64,80},{80,96},{96,112},{112,128},... | collective-permute-start | bytes 122888 | tf_op jit(solution)/shard_map/ppermute | solution.py:406
  20.0 1.2 %collective-permute-done.3.x_low = f32[80,128]{1,0:T(8,128)S(1)} collective-permute-done((f32[80,128]{1,0:T(8,128)S(1)}, f32[80,128]{1,0:T(8,128)S(1)}, u32[]{:S(2)}, u32[]{:S(2)}) %collective-permute-start.3) | collective-permute-done | bytes 40992 | tf_op jit(solution)/shard_map/ppermute | solution.py:406
  21.2 0.0 collective-permute-done.2.x_high
  21.2 0.0 copy-done
  21.2 8.8 %shard_map.61 = (f32[16,8,128]{2,1,0:T(8,128)}, f32[16,8,128]{2,1,0:T(8,128)S(1)}, f32[32,2,128]{2,1,0:T(2,128)S(1)}) custom-call(f32[256]{0:T(256)S(1)} %copy-done, f32[16,8,128]{2,1,0:T(8,128)S(1)} %get-tuple-element.12.density, f32[3,16,8,128]{3,2,1,0:T(8,128)S(1)} %get-tuple-element.13.displacement, s32[16,8,128]{2,1,0:T(8,128)S(1)} %get-tuple-element.14.passive, ...), custom_call_target="tpu_custom_call" | custom-call | tf_op jit(solution)/shard_map/pallas_call | solution.py:436
  30.0 12.9 %all_to_all.10.received = f32[32,2,128]{2,1,0:T(2,128)S(1)} all-to-all(f32[32,2,128]{2,1,0:T(2,128)S(1)} %get-tuple-element.19), channel_id=1, replica_groups={{0,1,2,3,4,5,6,7,8,9,10,11,12,13,14,15,16,17,18,19,20,21,22,23,24,25,26..., dimensions={0} | all-to-all | bytes 65536 | tf_op jit(solution)/shard_map/all_to_all | solution.py:462
  42.9 28.0 %all_to_all.11.received = f32[16,2,128]{2,1,0:T(2,128)S(1)} all-to-all(f32[16,2,128]{2,1,0:T(2,128)S(1)} %shard_map.62), channel_id=1, replica_groups={{0,32,64,96,128,160,192,224,256,288,320,352,384,416,448,480},{1,33,65,9..., dimensions={0} | all-to-all | bytes 32768 | tf_op jit(solution)/shard_map/all_to_all | solution.py:464
  70.9 0.8 %shard_map.63 = f32[16,8,128]{2,1,0:T(8,128)} custom-call(f32[16,2,128]{2,1,0:T(2,128)S(1)} %all_to_all.11.received, f32[16,8,128]{2,1,0:T(8,128)S(1)} %get-tuple-element.20.scaled, f32[16,8,128]{2,1,0:T(8,128)S(1)} %get-tuple-element.12.density, s32[16,8,128]{2,1,0:T(8,128)S(1)} %get-tuple-element.14.passive), custom_call_target="tpu_custom_call" | custom-call | tf_op jit(solution)/shard_map/pallas_call | solution.py:466
  (2 shorter events, 0.1 us)
Async XLA Ops:
  1.7 7.1 %collective-permute-start = (f32[144,128]{1,0:T(8,128)S(1)}, f32[144,128]{1,0:T(8,128)S(1)}, u32[]{:S(2)}, u32[]{:S(2)}) collective-permute-start(f32[144,128]{1,0:T(8,128)S(1)} %get-tuple-element.15), channel_id=1, source_target_pairs={{1,0},{2,1},{3,2},{4,3},{5,4},{6,5},{7,6},{8,7},{9,8},{10,9},{11,1... | collective-permute-start | bytes 221192 | tf_op jit(solution)/shard_map/ppermute | solution.py:406
  3.0 5.8 %collective-permute-start.1 = (f32[96,128]{1,0:T(8,128)S(1)}, f32[96,128]{1,0:T(8,128)S(1)}, u32[]{:S(2)}, u32[]{:S(2)}) collective-permute-start(f32[96,128]{1,0:T(8,128)S(1)} %get-tuple-element.16), channel_id=1, source_target_pairs={{0,1},{1,2},{2,3},{3,4},{4,5},{5,6},{6,7},{7,8},{8,9},{9,10},{10,1... | collective-permute-start | bytes 147464 | tf_op jit(solution)/shard_map/ppermute | solution.py:406
  8.8 12.4 %copy-start = (f32[256]{0:T(256)S(1)}, f32[256]{0:T(256)}, u32[]{:S(2)}) copy-start(f32[256]{0:T(256)} %constant.2.clone.factors) | copy-start | bytes 3076
  8.9 12.3 %collective-permute-start.2 = (f32[104,128]{1,0:T(8,128)S(1)}, f32[104,128]{1,0:T(8,128)S(1)}, u32[]{:S(2)}, u32[]{:S(2)}) collective-permute-start(f32[104,128]{1,0:T(8,128)S(1)} %get-tuple-element.17), channel_id=1, source_target_pairs={{16,0},{32,16},{48,32},{64,48},{80,64},{96,80},{112,96},{128,112},... | collective-permute-start | bytes 159752 | tf_op jit(solution)/shard_map/ppermute | solution.py:406
  18.1 3.1 %collective-permute-start.3 = (f32[80,128]{1,0:T(8,128)S(1)}, f32[80,128]{1,0:T(8,128)S(1)}, u32[]{:S(2)}, u32[]{:S(2)}) collective-permute-start(f32[80,128]{1,0:T(8,128)S(1)} %get-tuple-element.18), channel_id=1, source_target_pairs={{0,16},{16,32},{32,48},{48,64},{64,80},{80,96},{96,112},{112,128},... | collective-permute-start | bytes 122888 | tf_op jit(solution)/shard_map/ppermute | solution.py:406

commit v3 on v2

v3 whole, which is shorter than its diff:
```python
import functools
import math

import jax
import jax.numpy as jnp
from jax import lax
from jax.experimental import pallas as pl
from jax.experimental.pallas import tpu as pltpu
from jax.sharding import PartitionSpec as P

BISECT = 8
BRACKET = 8.0
MOVE_LIMIT = 0.2
VOLUME_SHARE = 0.35
DERIVATIVE = 3.0 * (1.0 - 1e-09)
EDGE_WEIGHT = 1.5 - math.sqrt(2.0)
POISSON = 0.3
LAME = POISSON / ((1.0 + POISSON) * (1.0 - 2.0 * POISSON))
SHEAR = 0.5 / (1.0 + POISSON)

NXL = 16
NYL = 8
NZ = 128
TRIALS = 2 ** BISECT - 1
SLOTS = TRIALS + 1
STEP = 2.0 * BRACKET / 2 ** BISECT
GROUP = 16

VMEM = pl.BlockSpec(memory_space=pltpu.VMEM)


def pack_y(
    density_far, displacement_far, passive_far, density, displacement, passive, to_low, to_high, sems
):
    copies = [
        pltpu.make_async_copy(far, local, sems.at[i])
        for i, (far, local) in enumerate(
            (
                (density_far, density),
                (displacement_far, displacement),
                (passive_far, passive),
            )
        )
    ]
    for copy in copies:
        copy.start()
    for copy in copies:
        copy.wait()
    for row in (0, 1):
        to_low[pl.ds(row * NXL, NXL), :] = density[:, row, :]
        to_high[pl.ds(row * NXL, NXL), :] = density[:, NYL - 2 + row, :]
    for c in range(3):
        for row in (0, 1):
            to_low[pl.ds((2 + 2 * c + row) * NXL, NXL), :] = displacement[c, :, row, :]
        to_high[pl.ds((2 + c) * NXL, NXL), :] = displacement[c, :, NYL - 1, :]
    to_low[pl.ds(8 * NXL, NXL), :] = passive[:, 0, :].astype(jnp.float32)
    to_high[pl.ds(5 * NXL, NXL), :] = passive[:, NYL - 1, :].astype(jnp.float32)


def pack_x(density, displacement, passive, y_high, y_low, after, to_low, to_high):
    del after
    for k in (0, 1):
        to_low[pl.ds(8 * k, 8), :] = density[k]
        to_high[pl.ds(8 * k, 8), :] = density[NXL - 2 + k]
    for c in range(3):
        for k in (0, 1):
            to_low[pl.ds(8 * (2 + 2 * c + k), 8), :] = displacement[c, k]
        to_high[pl.ds(8 * (2 + c), 8), :] = displacement[c, NXL - 1]
    to_low[pl.ds(64, 8), :] = passive[0].astype(jnp.float32)
    to_high[pl.ds(40, 8), :] = passive[NXL - 1].astype(jnp.float32)
    for base, first, out in ((72, 0, to_low), (48, NXL - 2, to_high)):
        for kind in range(9):
            out[pl.ds(base + 2 * kind, 2), :] = y_high[pl.ds(NXL * kind + first, 2), :]
        for kind in range(6):
            out[pl.ds(base + 18 + 2 * kind, 2), :] = y_low[pl.ds(NXL * kind + first, 2), :]
        out[pl.ds(base + 30, 2), :] = jnp.zeros((2, NZ), jnp.float32)


def lane_ends(height):
    lane = lax.broadcasted_iota(jnp.int32, (height, NZ), 1)
    return lane == 0, lane == NZ - 1


def z_sum(f, first, last):
    return jnp.where(first, 0.0, pltpu.roll(f, 1, 1)) + jnp.where(
        last, 0.0, pltpu.roll(f, NZ - 1, 1)
    )


def filter_terms(low, mid, high, first, last):
    across = z_sum(mid, first, last)
    along = low + high
    both = across + along
    side = 0.5 * mid + EDGE_WEIGHT * both
    rest = 1.5 * mid + 0.5 * both + EDGE_WEIGHT * z_sum(along, first, last)
    return side, rest


def corner_sums(here, above, last):
    total = here + above
    slope = above - here
    total_next = jnp.where(last, 0.0, pltpu.roll(total, NZ - 1, 1))
    slope_next = jnp.where(last, 0.0, pltpu.roll(slope, NZ - 1, 1))
    return (total + total_next, total_next - total, slope + slope_next, slope_next - slope)


def element_energy(before, after):
    modes = []
    for c in range(3):
        for k in range(4):
            low, high = before[4 * c + k], after[4 * c + k]
            modes.append((low + high, high - low))
    u, v, w = (
        {(a, k // 2, k % 2): modes[4 * c + k][a] for a in (0, 1) for k in range(4)}
        for c in range(3)
    )

    def sq(x):
        return x * x

    trace = sq(u[1, 0, 0] + v[0, 1, 0] + w[0, 0, 1]) + (1.0 / 3.0) * (
        sq(v[1, 1, 0] + w[1, 0, 1]) + sq(u[1, 1, 0] + w[0, 1, 1]) + sq(u[1, 0, 1] + v[0, 1, 1])
    )
    normal = sq(u[1, 0, 0]) + sq(v[0, 1, 0]) + sq(w[0, 0, 1])
    linear = (
        sq(v[1, 1, 0])
        + sq(w[1, 0, 1])
        + sq(u[1, 1, 0])
        + sq(w[0, 1, 1])
        + sq(u[1, 0, 1])
        + sq(v[0, 1, 1])
    )
    bilinear = sq(u[1, 1, 1]) + sq(v[1, 1, 1]) + sq(w[1, 1, 1])
    shear = (
        sq(u[0, 1, 0] + v[1, 0, 0]) + sq(u[0, 0, 1] + w[1, 0, 0]) + sq(v[0, 0, 1] + w[0, 1, 0])
    )
    twist = (
        sq(u[0, 1, 1] + v[1, 0, 1]) + sq(u[0, 1, 1] + w[1, 1, 0]) + sq(v[1, 0, 1] + w[1, 1, 0])
    )
    return (
        (LAME / 16.0) * trace
        + (SHEAR / 8.0) * normal
        + (SHEAR / 16.0) * (linear + shear)
        + ((LAME + 4.0 * SHEAR) / 144.0) * bilinear
        + (SHEAR / 48.0) * twist
    )


def interior_energy(displacement, energy, inverse, weights, factors):
    start_y = lax.axis_index("gy") * NYL
    total_y = lax.axis_size("gy") * NYL
    first, last = lane_ends(NYL)

    def nodes(plane):
        here = []
        for c in range(3):
            f = displacement[c, plane]
            here.extend(corner_sums(f, pltpu.roll(f, NYL - 1, 0), last))
        return tuple(here)

    def plane_energy(x, before):
        after = nodes(x + 1)
        energy[x] = element_energy(before, after)
        return after

    lax.fori_loop(0, NXL - 1, plane_energy, nodes(0))
    energy[NXL - 1] = jnp.zeros((NYL, NZ), jnp.float32)
    trial = lax.broadcasted_iota(jnp.int32, (SLOTS, NZ), 0).astype(jnp.float32)
    factors[...] = jnp.exp(-0.5 * (-BRACKET + STEP * (trial + 1.0)))

    along_z = jnp.where(first | last, 1.0, 2.0)
    for v in (0, 1):
        index_y = start_y - 1 + 8 * v + lax.broadcasted_iota(jnp.int32, (8, NZ), 0)
        inside = (index_y >= 0) & (index_y < total_y)
        along_y = jnp.where((index_y == 0) | (index_y == total_y - 1), 1.0, 2.0)
        base = 1.5 + 0.5 * (along_y + along_z) + EDGE_WEIGHT * along_y * along_z
        slope = 0.5 + EDGE_WEIGHT * (along_y + along_z)
        for slot, along_x in ((0, 2.0), (1, 1.0)):
            inverse[slot, pl.ds(8 * v, 8), :] = jnp.where(
                inside, 1.0 / (base + along_x * slope), 0.0
            )
    for slot in (0, 1):
        side, rest = filter_terms(
            inverse[slot, pl.ds(0, 8), :],
            inverse[slot, pl.ds(1, 8), :],
            inverse[slot, pl.ds(2, 8), :],
            first,
            last,
        )
        weights[2 * slot] = side
        weights[2 * slot + 1] = rest


def spread_of(filtered, weight, kind, energy):
    physical = filtered * weight
    physical = jnp.where(kind == 1.0, 1.0, jnp.where(kind == 2.0, 0.0, physical))
    return -DERIVATIVE * physical * physical * energy * weight


def around(ref, plane, first, last):
    return filter_terms(
        ref[plane, pl.ds(7, 8), :],
        ref[plane, pl.ds(8, 8), :],
        ref[plane, pl.ds(9, 8), :],
        first,
        last,
    )


def add_volumes(planes, factors, scaled, lower, upper, start, partial):
    def volume_group(g, carry):
        base = pl.multiple_of(8 * GROUP * g, 8 * GROUP)
        scales = [
            jnp.broadcast_to(factors[pl.ds(GROUP * g + k, 1), :], (8, NZ)) for k in range(GROUP)
        ]
        if start is None:
            totals = [jnp.zeros((8, NZ), jnp.float32) for _ in range(GROUP)]
        else:
            totals = [start[pl.ds(base + 8 * k, 8), :] for k in range(GROUP)]
        for place, x in planes:
            values, floor, ceiling = scaled[place], lower[x], upper[x]
            for k in range(GROUP):
                totals[k] += jnp.minimum(jnp.maximum(values * scales[k], floor), ceiling)
        for k in range(GROUP):
            partial[pl.ds(base + 8 * k, 8), :] = totals[k]
        return carry

    lax.fori_loop(0, SLOTS // GROUP, volume_group, 0)


def middle(
    factors,
    density,
    passive,
    own_energy,
    inverse,
    weights,
    y_high,
    y_low,
    to_low,
    to_high,
    spread,
    sensitivity,
    scaled,
    lower,
    upper,
    partial,
    dens,
    energy,
):
    def rows(ref, kind):
        return ref[pl.ds(kind * NXL, NXL), :]

    first, last = lane_ends(NXL)

    def row_nodes(ref, step, at):
        return [rows(ref, at + step * c) for c in range(3)]

    def row_energy(here, above):
        before, after = [], []
        for c in range(3):
            sums = corner_sums(here[c], above[c], last)
            before.extend(sums)
            after.extend(pltpu.roll(f, NXL - 1, 0) for f in sums)
        return element_energy(before, after)

    nodes_8 = row_nodes(y_high, 2, 2)
    energy_low = row_energy(row_nodes(y_low, 1, 2), row_nodes(to_low, 2, 2))
    energy_7 = row_energy(row_nodes(to_high, 1, 2), nodes_8)
    energy_high = row_energy(nodes_8, row_nodes(y_high, 2, 3))

    dens[:, pl.ds(8, NYL), :] = density[...]
    dens[:, 7, :] = rows(y_low, 1)
    dens[:, 16, :] = rows(y_high, 0)
    energy[...] = own_energy[...]
    energy[:, 7, :] = energy_7

    for row, low, mid, high, kind, row_energies in (
        (0, rows(y_low, 0), rows(y_low, 1), rows(to_low, 0), rows(y_low, 5), energy_low),
        (9, rows(to_high, 1), rows(y_high, 0), rows(y_high, 1), rows(y_high, 8), energy_high),
    ):
        side, rest = filter_terms(low, mid, high, first, last)
        filtered = rest + pltpu.roll(side, 1, 0) + pltpu.roll(side, NXL - 1, 0)
        weight = jnp.broadcast_to(inverse[0, pl.ds(row, 1), :], (NXL, NZ))
        spread[:, row + 7, :] = spread_of(filtered, weight, kind, row_energies)

    first, last = lane_ends(NYL)
    weight = inverse[0, pl.ds(1, 8), :]

    def spread_plane(x, carry):
        side_before, side_here, rest_here = carry
        side_after, rest_after = around(dens, x + 1, first, last)
        spread[x, pl.ds(8, 8), :] = spread_of(
            rest_here + side_before + side_after,
            weight,
            passive[x].astype(jnp.float32),
            energy[x],
        )
        return side_here, side_after, rest_after

    side_0, _ = around(dens, 0, first, last)
    lax.fori_loop(
        1, NXL - 1, spread_plane, (side_0,) + around(dens, 1, first, last), unroll=2
    )

    scale = 1.0 / (weights[1] + 2.0 * weights[0])

    def out_plane(x, carry):
        side_before, side_here, rest_here = carry
        side_after, rest_after = around(spread, x + 1, first, last)
        sens = rest_here + side_before + side_after
        sensitivity[x] = sens
        scaled[x] = density[x] * jnp.sqrt(-sens * scale)
        return side_here, side_after, rest_after

    side_1, _ = around(spread, 1, first, last)
    lax.fori_loop(
        2, NXL - 2, out_plane, (side_1,) + around(spread, 2, first, last), unroll=2
    )

    here = density[...]
    kind = passive[...]
    fixed = jnp.where(kind == 1, 1.0, 0.0)
    lower[...] = jnp.where(kind == 0, jnp.maximum(here - MOVE_LIMIT, 0.0), fixed)
    upper[...] = jnp.where(kind == 0, jnp.minimum(here + MOVE_LIMIT, 1.0), fixed)
    add_volumes(
        [(x, x) for x in range(2, NXL - 2)], factors, scaled, lower, upper, None, partial
    )


def edges(
    factors,
    density,
    displacement,
    passive,
    y_high,
    y_low,
    x_high,
    x_low,
    inverse,
    weights,
    spread,
    lower,
    upper,
    start,
    sensitivity,
    scaled,
    sums_out,
    dens,
    disp,
    kind_of,
    rim,
    partial,
    *,
    copies,
):
    first, last = lane_ends(NYL)
    at_end = (
        lax.axis_index("gx") == 0,
        lax.axis_index("gx") == lax.axis_size("gx") - 1,
    )
    for side, (own, far, slabs, low_rows, pick) in enumerate(
        ((0, x_low, 48, 66, 1), (NXL - 2, x_high, 72, 90, 0))
    ):
        for k in (0, 1):
            own_at, far_at = (2 + k, k) if side == 0 else (k, 2 + k)
            dens[side, own_at, pl.ds(2, NYL), :] = density[own + k]
            dens[side, far_at, pl.ds(2, NYL), :] = far[pl.ds(8 * k, 8), :]
            for row in (0, 1):
                dens[side, own_at, pl.ds(NYL + 2 + row, 1), :] = y_high[
                    pl.ds(row * NXL + own + k, 1), :
                ]
                dens[side, own_at, pl.ds(row, 1), :] = y_low[pl.ds(row * NXL + own + k, 1), :]
                dens[side, far_at, pl.ds(NYL + 2 + row, 1), :] = far[
                    pl.ds(slabs + 2 * row + k, 1), :
                ]
                dens[side, far_at, pl.ds(row, 1), :] = far[pl.ds(low_rows + 2 * row + k, 1), :]
        for c in range(3):
            mine = ((1, 0), (2, 1)) if side == 0 else ((0, NXL - 1),)
            theirs = ((0, 2 + c, 1),) if side == 0 else ((1, 2 + 2 * c, 0), (2, 3 + 2 * c, 1))
            for at, x in mine:
                disp[side, c, at, pl.ds(1, NYL), :] = displacement[c, x]
                disp[side, c, at, pl.ds(0, 1), :] = y_low[pl.ds((2 + c) * NXL + x, 1), :]
                for row in (0, 1):
                    disp[side, c, at, pl.ds(NYL + 1 + row, 1), :] = y_high[
                        pl.ds((2 + 2 * c + row) * NXL + x, 1), :
                    ]
            for at, slab, k in theirs:
                disp[side, c, at, pl.ds(1, NYL), :] = far[pl.ds(8 * slab, 8), :]
                disp[side, c, at, pl.ds(0, 1), :] = far[pl.ds(low_rows + 2 * (2 + c) + k, 1), :]
                for row in (0, 1):
                    disp[side, c, at, pl.ds(NYL + 1 + row, 1), :] = far[
                        pl.ds(slabs + 2 * (2 + 2 * c + row) + k, 1), :
                    ]
        own_at, far_at, x = (1, 0, 0) if side == 0 else (0, 1, NXL - 1)
        kind_of[side, own_at, pl.ds(1, NYL), :] = passive[x].astype(jnp.float32)
        kind_of[side, own_at, pl.ds(0, 1), :] = y_low[pl.ds(5 * NXL + x, 1), :]
        kind_of[side, own_at, pl.ds(NYL + 1, 1), :] = y_high[pl.ds(8 * NXL + x, 1), :]
        kind_of[side, far_at, pl.ds(1, NYL), :] = far[pl.ds(40 if side == 0 else 64, 8), :]
        kind_of[side, far_at, pl.ds(0, 1), :] = far[pl.ds(low_rows + 10 + pick, 1), :]
        kind_of[side, far_at, pl.ds(NYL + 1, 1), :] = far[pl.ds(slabs + 16 + pick, 1), :]

        for v in (0, 1):
            rows = pl.ds(8 * v, 8)
            terms = [
                filter_terms(
                    dens[side, p, rows, :],
                    dens[side, p, pl.ds(8 * v + 1, 8), :],
                    dens[side, p, pl.ds(8 * v + 2, 8), :],
                    first,
                    last,
                )
                for p in range(4)
            ]
            nodes = []
            for p in range(3):
                sums = []
                for c in range(3):
                    sums.extend(
                        corner_sums(
                            disp[side, c, p, rows, :],
                            disp[side, c, p, pl.ds(8 * v + 1, 8), :],
                            last,
                        )
                    )
                nodes.append(sums)
            inner = inverse[0, rows, :]
            by_place = (
                jnp.where(at_end[side], 0.0, inner),
                jnp.where(at_end[side], inverse[1, rows, :], inner),
            )
            for k in (0, 1):
                weight = by_place[k] if side == 0 else by_place[1 - k]
                rim[side, (k if side == 0 else 2 + k), pl.ds(7 + 8 * v, 8), :] = spread_of(
                    terms[k + 1][1] + terms[k][0] + terms[k + 2][0],
                    weight,
                    kind_of[side, k, rows, :],
                    element_energy(nodes[k], nodes[k + 1]),
                )
        for k in (0, 1):
            rim[side, (2 + k if side == 0 else k), :, :] = spread[1 + k if side == 0 else 13 + k]

    side_inner, rest_inner, side_edge, rest_edge = (weights[i] for i in range(4))
    for side in (0, 1):
        outer_side = jnp.where(at_end[side], 0.0, side_inner)
        next_side = jnp.where(at_end[side], side_edge, side_inner)
        outer = jnp.where(at_end[side], rest_edge, rest_inner) + outer_side + side_inner
        inner = rest_inner + next_side + side_inner
        terms = [around(rim.at[side], p, first, last) for p in range(4)]
        for k in (0, 1):
            x = k if side == 0 else NXL - 2 + k
            sens = terms[k + 1][1] + terms[k][0] + terms[k + 2][0]
            weight = outer if k == side else inner
            sensitivity[2 * side + k] = sens
            scaled[2 * side + k] = density[x] * jnp.sqrt(-sens / weight)

    add_volumes(
        [(0, 0), (1, 1), (2, NXL - 2), (3, NXL - 1)],
        factors,
        scaled,
        lower,
        upper,
        start,
        partial,
    )
    rows_of = [partial[pl.ds(s, SLOTS, stride=8), :] for s in range(8)]
    lines = ((rows_of[0] + rows_of[1]) + (rows_of[2] + rows_of[3])) + (
        (rows_of[4] + rows_of[5]) + (rows_of[6] + rows_of[7])
    )
    volumes = lax.dot_general(
        jnp.ones((8, NZ), jnp.float32),
        lines,
        (((1,), (1,)), ((), ())),
        precision=lax.Precision.HIGHEST,
        preferred_element_type=jnp.float32,
    )
    odd = lax.broadcasted_iota(jnp.int32, (8, NZ), 0) > 0
    pair = jnp.where(odd, volumes[:, NZ:], volumes[:, :NZ])[0:2]
    for copy in range(copies):
        sums_out[copy] = pair


def add_copies(received, out, *, copies):
    total = jnp.sum(received[...], axis=0)
    for copy in range(copies):
        out[copy] = total


def finish(
    received,
    scaled,
    scaled_edge,
    lower,
    upper,
    sensitivity,
    sensitivity_edge,
    new_density,
    sensitivity_out,
    sems,
    *,
    target,
):
    inner = pl.ds(2, NXL - 4)
    ends = ((pl.ds(0, 2), pl.ds(0, 2)), (pl.ds(2, 2), pl.ds(NXL - 2, 2)))
    copies = [pltpu.make_async_copy(sensitivity.at[inner], sensitivity_out.at[inner], sems.at[0])]
    for i, (place, planes) in enumerate(ends):
        copies.append(
            pltpu.make_async_copy(
                sensitivity_edge.at[place], sensitivity_out.at[planes], sems.at[1 + i]
            )
        )
    for copy in copies:
        copy.start()
    volumes = jnp.sum(received[...], axis=0)
    slot = lax.broadcasted_iota(jnp.int32, (2, NZ), 0) * NZ + lax.broadcasted_iota(
        jnp.int32, (2, NZ), 1
    )
    above = jnp.sum(jnp.where((volumes > target) & (slot < TRIALS), 1.0, 0.0))
    middle_end = -BRACKET + STEP * above + 0.5 * STEP
    factor = jnp.exp(jnp.full((8, NZ), -0.5, jnp.float32) * middle_end)[None]
    for ref, place, planes in ((scaled, inner, inner),) + tuple(
        (scaled_edge, place, planes) for place, planes in ends
    ):
        new_density[planes] = jnp.minimum(
            jnp.maximum(ref[place] * factor, lower[planes]), upper[planes]
        )
    for copy in copies:
        copy.wait()


def f32(*shape):
    return jax.ShapeDtypeStruct(shape, jnp.float32)


def near(*shape, dtype=jnp.float32):
    return pltpu.VMEM(shape, dtype)


def far(array):
    return pltpu.with_memory_space_constraint(array, pltpu.HBM)


def held(array):
    return pltpu.with_memory_space_constraint(array, pltpu.VMEM)


def call(kernel, outputs, inputs, scratch=(), specs=None, out_specs=None, cost=0):
    return pl.pallas_call(
        kernel,
        out_shape=outputs,
        in_specs=specs or [VMEM] * len(inputs),
        out_specs=out_specs or jax.tree.map(lambda _: VMEM, outputs),
        scratch_shapes=list(scratch),
        cost_estimate=pl.CostEstimate(
            flops=cost * 4000, bytes_accessed=cost * 1000, transcendentals=0
        ),
        compiler_params=pltpu.CompilerParams(vmem_limit_bytes=16 << 20),
    )(*inputs)


def shifted(block, axis, distance):
    devices = range(lax.axis_size(axis))
    route = [(i - distance, i) for i in devices if i - distance in devices]
    return lax.ppermute(block, axis, route)


def per_device(density, displacement, passive):
    count_x, count_y = lax.axis_size("gx"), lax.axis_size("gy")
    assert density.shape == (NXL, NYL, NZ)
    block = (NXL, NYL, NZ)
    density, displacement, passive, y_to_low, y_to_high = call(
        pack_y,
        (
            near(*block),
            near(3, *block),
            near(*block, dtype=jnp.int32),
            near(9 * NXL, NZ),
            near(6 * NXL, NZ),
        ),
        (far(density), far(displacement), far(passive)),
        [pltpu.SemaphoreType.DMA((3,))],
        specs=[pl.BlockSpec(memory_space=pltpu.HBM)] * 3,
        cost=1000,
    )
    y_high = held(shifted(y_to_low, "gy", -1))
    y_low = held(shifted(y_to_high, "gy", 1))
    own_energy, inverse, weights, factors = call(
        interior_energy,
        (near(*block), near(2, 16, NZ), near(4, NYL, NZ), near(SLOTS, NZ)),
        (displacement,),
        cost=1000,
    )
    to_low, to_high = call(
        pack_x,
        (near(104, NZ), near(80, NZ)),
        (density, displacement, passive, y_high, y_low, weights),
        cost=500,
    )
    x_high = held(shifted(to_low, "gx", -1))
    x_low = held(shifted(to_high, "gx", 1))
    spread, sensitivity, scaled, lower, upper, partial = call(
        middle,
        (near(NXL, 24, NZ),) + (near(*block),) * 4 + (near(8 * SLOTS, NZ),),
        (
            factors,
            density,
            passive,
            own_energy,
            inverse,
            weights,
            y_high,
            y_low,
            y_to_low,
            y_to_high,
        ),
        [pltpu.VMEM((NXL, 24, NZ), jnp.float32), pltpu.VMEM(block, jnp.float32)],
        cost=5000,
    )
    plane = 2 * count_y
    layers = count_x // 2
    sensitivity_edge, scaled_edge, volumes = call(
        functools.partial(edges, copies=plane),
        (near(4, NYL, NZ), near(4, NYL, NZ), near(plane, 2, NZ)),
        (
            factors,
            density,
            displacement,
            passive,
            y_high,
            y_low,
            x_high,
            x_low,
            inverse,
            weights,
            spread,
            lower,
            upper,
            partial,
        ),
        [
            pltpu.VMEM((2, 4, 24, NZ), jnp.float32),
            pltpu.VMEM((2, 3, 3, 24, NZ), jnp.float32),
            pltpu.VMEM((2, 2, 16, NZ), jnp.float32),
            pltpu.VMEM((2, 4, 24, NZ), jnp.float32),
            pltpu.VMEM((8 * SLOTS, NZ), jnp.float32),
        ],
        cost=3000,
    )

    across = [
        [(2 * z + core) * count_y + y for core in (0, 1) for y in range(count_y)]
        for z in range(layers)
    ]
    along = [
        [(2 * z + core) * count_y + y for z in range(layers)]
        for core in (0, 1)
        for y in range(count_y)
    ]
    volumes = lax.all_to_all(volumes, ("gx", "gy"), 0, 0, axis_index_groups=across)
    volumes = call(
        functools.partial(add_copies, copies=layers),
        near(layers, 2, NZ),
        (held(volumes),),
        cost=300,
    )
    volumes = lax.all_to_all(volumes, ("gx", "gy"), 0, 0, axis_index_groups=along)
    target = VOLUME_SHARE * (count_x * NXL) * (count_y * NYL) * NZ
    new_density, sensitivity = call(
        functools.partial(finish, target=target),
        (f32(*block), f32(*block)),
        (held(volumes), scaled, scaled_edge, lower, upper, sensitivity, sensitivity_edge),
        [pltpu.SemaphoreType.DMA((3,))],
        out_specs=(VMEM, pl.BlockSpec(memory_space=pltpu.HBM)),
        cost=500,
    )
    return new_density, sensitivity


def solution(mesh):
    return jax.shard_map(
        per_device,
        mesh=mesh,
        in_specs=(P("gx", "gy", None), P(None, "gx", "gy", None), P("gx", "gy", None)),
        out_specs=(P("gx", "gy", None), P("gx", "gy", None)),
        check_vma=False,
    )
```

time: 72 us -> 65 us (0.903)
  waiting for transfers between devices: 2.35 us -> 0.01 us
  Pallas kernels: 10.7 us -> 8.5 us
  blocking collectives: 40.9 us -> 38.9 us
    ppermute x4, waiting for transfers between devices: 2.35 us -> 0.01 us  [shifted(): return lax.ppermute(block, axis, route)]
    pallas_call x5 -> x7, Pallas kernels: 10.7 us -> 8.5 us  [call(): pl.pallas_call(kernel, out_shape=outputs, in_specs=specs or [VMEM] * len(...]
    all_to_all x1, blocking collectives: 28 us -> 25.9 us  [per_device(): lax.all_to_all(volumes, ('gx', 'gy'), 0, 0, axis_index_groups=along)]
  transfers between devices with their start and end apart: 4 -> 4, of which waited for: 2 -> 0; matrix products, arithmetic and copies ran while one was open for 0% -> 0% of each run, Pallas kernels for 0% -> 7%
where the time goes in v3:
time: 65 us; the launch traced here: 64.8 us
  blocking collectives  38.9 us (60%)
  starting transfers between devices  16.7 us (26%)
  Pallas kernels  8.5 us (13%)
  between operations  0.73 us (1%)
    all_to_all x1, blocking collectives, per_device(): lax.all_to_all(volumes, ('gx', 'gy'), 0, 0, axis_index_groups=along)  25.9 us
    ppermute x4, starting transfers between devices, shifted(): return lax.ppermute(block, axis, route)  16.7 us
    all_to_all x1, blocking collectives, per_device(): lax.all_to_all(volumes, ('gx', 'gy'), 0, 0, axis_index_groups=across)  13 us
    pallas_call x7, Pallas kernels, call(): pl.pallas_call(kernel, out_shape=outputs, in_specs=specs or [VMEM] * len(...  8.5 us
  transfers between devices with their start and end apart: 4, of which 0 were waited for; matrix products, arithmetic and copies ran while one was open for 0% of the time, Pallas kernels for 7%

profile of v3, /device:TPU:1, one launch (start us, length us, event | category | flops | bytes accessed | tf_op | source)
XLA Modules:
  0.0 64.8 jit_solution(5561916122892180069)
XLA Ops:
  0.6 1.1 %shard_map.50 = (f32[16,8,128]{2,1,0:T(8,128)S(1)}, f32[3,16,8,128]{3,2,1,0:T(8,128)S(1)}, s32[16,8,128]{2,1,0:T(8,128)S(1)}, f32[144,128]{1,0:T(8,128)S(1)}, f32[96,128]{1,0:T(8,128)S(1)}) custom-call(f32[16,8,128]{2,1,0:T(8,128)} %density_far.1, f32[3,16,8,128]{3,2,1,0:T(8,128)} %displacement_far.1, s32[16,8,128]{2,1,0:T(8,128)} %passive_far.1), custom_call_target="tpu_custom_call" | custom-call | flops 4000000 | bytes 1000000 | tf_op jit(solution)/shard_map/pallas_call | solution.py:548
  1.7 1.3 %collective-permute-start = (f32[144,128]{1,0:T(8,128)S(1)}, f32[144,128]{1,0:T(8,128)S(1)}, u32[]{:S(2)}, u32[]{:S(2)}) collective-permute-start(f32[144,128]{1,0:T(8,128)S(1)} %get-tuple-element.26.to_low), channel_id=1, source_target_pairs={{1,0},{2,1},{3,2},{4,3},{5,4},{6,5},{7,6},{8,7},{9,8},{10,9},{11,1... | collective-permute-start | bytes 221192 | tf_op jit(solution)/shard_map/ppermute | solution.py:564
  3.0 4.6 %collective-permute-start.1 = (f32[96,128]{1,0:T(8,128)S(1)}, f32[96,128]{1,0:T(8,128)S(1)}, u32[]{:S(2)}, u32[]{:S(2)}) collective-permute-start(f32[96,128]{1,0:T(8,128)S(1)} %get-tuple-element.27.to_high), channel_id=1, source_target_pairs={{0,1},{1,2},{2,3},{3,4},{4,5},{5,6},{6,7},{7,8},{8,9},{9,10},{10,1... | collective-permute-start | bytes 147464 | tf_op jit(solution)/shard_map/ppermute | solution.py:564
  7.7 1.5 %shard_map.51 = (f32[16,8,128]{2,1,0:T(8,128)S(1)}, f32[2,16,128]{2,1,0:T(8,128)S(1)}, f32[4,8,128]{2,1,0:T(8,128)S(1)}, f32[256,128]{1,0:T(8,128)S(1)}) custom-call(f32[3,16,8,128]{3,2,1,0:T(8,128)S(1)} %get-tuple-element.22.displacement), custom_call_target="tpu_custom_call" | custom-call | flops 4000000 | bytes 1000000 | tf_op jit(solution)/shard_map/pallas_call | solution.py:548
  9.2 0.0 collective-permute-done.1.y_low
  9.2 0.0 collective-permute-done.y_high
  9.3 8.8 %collective-permute-start.2 = (f32[104,128]{1,0:T(8,128)S(1)}, f32[104,128]{1,0:T(8,128)S(1)}, u32[]{:S(2)}, u32[]{:S(2)}) collective-permute-start(f32[104,128]{1,0:T(8,128)S(1)} %get-tuple-element.29), channel_id=1, source_target_pairs={{16,0},{32,16},{48,32},{64,48},{80,64},{96,80},{112,96},{128,112},... | collective-permute-start | bytes 159752 | tf_op jit(solution)/shard_map/ppermute | solution.py:564
  18.1 1.9 %collective-permute-start.3 = (f32[80,128]{1,0:T(8,128)S(1)}, f32[80,128]{1,0:T(8,128)S(1)}, u32[]{:S(2)}, u32[]{:S(2)}) collective-permute-start(f32[80,128]{1,0:T(8,128)S(1)} %get-tuple-element.30), channel_id=1, source_target_pairs={{0,16},{16,32},{32,48},{48,64},{64,80},{80,96},{96,112},{112,128},... | collective-permute-start | bytes 122888 | tf_op jit(solution)/shard_map/ppermute | solution.py:564
  20.0 3.2 %shard_map.53 = (f32[16,24,128]{2,1,0:T(8,128)S(1)}, f32[16,8,128]{2,1,0:T(8,128)S(1)}, f32[16,8,128]{2,1,0:T(8,128)S(1)}, f32[16,8,128]{2,1,0:T(8,128)S(1)}, f3...) custom-call(f32[256,128]{1,0:T(8,128)S(1)} %get-tuple-element.23.factors, f32[16,8,128]{2,1,0:T(8,128)S(1)} %get-tuple-element.24.density, ...), custom_call_target="tpu_custom_call" | custom-call | flops 20000000 | bytes 5000000 | tf_op jit(solution)/shard_map/pallas_call | solution.py:548
  23.2 0.0 collective-permute-done.3.x_low
  23.2 0.0 collective-permute-done.2.x_high
  23.2 1.4 %shard_map.54 = (f32[4,8,128]{2,1,0:T(8,128)S(1)}, f32[4,8,128]{2,1,0:T(8,128)S(1)}, f32[32,2,128]{2,1,0:T(2,128)S(1)}) custom-call(f32[256,128]{1,0:T(8,128)S(1)} %get-tuple-element.23.factors, f32[16,8,128]{2,1,0:T(8,128)S(1)} %get-tuple-element.24.density, f32[3,16,8,128]{3,2,1,0:T(8,128)S(1)} %get-tuple-element.22.displacement, ...), custom_call_target="tpu_custom_call" | custom-call | flops 12000000 | bytes 3000000 | tf_op jit(solution)/shard_map/pallas_call | solution.py:548
  24.6 13.0 %all_to_all.10.received = f32[32,2,128]{2,1,0:T(2,128)S(1)} all-to-all(f32[32,2,128]{2,1,0:T(2,128)S(1)} %get-tuple-element.37), channel_id=1, replica_groups={{0,1,2,3,4,5,6,7,8,9,10,11,12,13,14,15,16,17,18,19,20,21,22,23,24,25,26..., dimensions={0} | all-to-all | bytes 65536 | tf_op jit(solution)/shard_map/all_to_all | solution.py:659
  37.6 25.9 %all_to_all.11.received = f32[16,2,128]{2,1,0:T(2,128)S(1)} all-to-all(f32[16,2,128]{2,1,0:T(2,128)S(1)} %shard_map.55), channel_id=1, replica_groups={{0,32,64,96,128,160,192,224,256,288,320,352,384,416,448,480},{1,33,65,9..., dimensions={0} | all-to-all | bytes 32768 | tf_op jit(solution)/shard_map/all_to_all | solution.py:666
  63.5 1.3 %shard_map.56 = (f32[16,8,128]{2,1,0:T(8,128)}, f32[16,8,128]{2,1,0:T(8,128)}) custom-call(f32[16,2,128]{2,1,0:T(2,128)S(1)} %all_to_all.11.received, f32[16,8,128]{2,1,0:T(8,128)S(1)} %get-tuple-element.38.scaled, f32[4,8,128]{2,1,0:T(8,128)S(1)} %get-tuple-element.39.scaled_edge, f32[16,8,128]{2,1,0:T(8,128)S(1)} %get-tuple-element.34.lower, ...), custom_call_target="tpu_custom_call" | custom-call | flops 2000000 | bytes 500000 | tf_op jit(solution)/shard_map/pallas_call | solution.py:548
  (2 shorter events, 0.1 us)
Async XLA Ops:
  1.7 7.5 %collective-permute-start = (f32[144,128]{1,0:T(8,128)S(1)}, f32[144,128]{1,0:T(8,128)S(1)}, u32[]{:S(2)}, u32[]{:S(2)}) collective-permute-start(f32[144,128]{1,0:T(8,128)S(1)} %get-tuple-element.26.to_low), channel_id=1, source_target_pairs={{1,0},{2,1},{3,2},{4,3},{5,4},{6,5},{7,6},{8,7},{9,8},{10,9},{11,1... | collective-permute-start | bytes 221192 | tf_op jit(solution)/shard_map/ppermute | solution.py:564
  3.0 6.2 %collective-permute-start.1 = (f32[96,128]{1,0:T(8,128)S(1)}, f32[96,128]{1,0:T(8,128)S(1)}, u32[]{:S(2)}, u32[]{:S(2)}) collective-permute-start(f32[96,128]{1,0:T(8,128)S(1)} %get-tuple-element.27.to_high), channel_id=1, source_target_pairs={{0,1},{1,2},{2,3},{3,4},{4,5},{5,6},{6,7},{7,8},{8,9},{9,10},{10,1... | collective-permute-start | bytes 147464 | tf_op jit(solution)/shard_map/ppermute | solution.py:564
  9.3 14.0 %collective-permute-start.2 = (f32[104,128]{1,0:T(8,128)S(1)}, f32[104,128]{1,0:T(8,128)S(1)}, u32[]{:S(2)}, u32[]{:S(2)}) collective-permute-start(f32[104,128]{1,0:T(8,128)S(1)} %get-tuple-element.29), channel_id=1, source_target_pairs={{16,0},{32,16},{48,32},{64,48},{80,64},{96,80},{112,96},{128,112},... | collective-permute-start | bytes 159752 | tf_op jit(solution)/shard_map/ppermute | solution.py:564
  18.1 5.1 %collective-permute-start.3 = (f32[80,128]{1,0:T(8,128)S(1)}, f32[80,128]{1,0:T(8,128)S(1)}, u32[]{:S(2)}, u32[]{:S(2)}) collective-permute-start(f32[80,128]{1,0:T(8,128)S(1)} %get-tuple-element.30), channel_id=1, source_target_pairs={{0,16},{16,32},{32,48},{48,64},{64,80},{80,96},{96,112},{112,128},... | collective-permute-start | bytes 122888 | tf_op jit(solution)/shard_map/ppermute | solution.py:564

commit v4 on v3

--- a/solution.py
+++ b/solution.py
@@ -29,8 +29,12 @@
 VMEM = pl.BlockSpec(memory_space=pltpu.VMEM)
 
 
+def is_even(axis):
+    return lax.rem(lax.axis_index(axis), 2) == 0
+
+
 def pack_y(
-    density_far, displacement_far, passive_far, density, displacement, passive, to_low, to_high, sems
+    density_far, displacement_far, passive_far, density, displacement, passive, send_a, send_b, sems
 ):
     copies = [
         pltpu.make_async_copy(far, local, sems.at[i])
@@ -46,34 +50,54 @@
         copy.start()
     for copy in copies:
         copy.wait()
-    for row in (0, 1):
-        to_low[pl.ds(row * NXL, NXL), :] = density[:, row, :]
-        to_high[pl.ds(row * NXL, NXL), :] = density[:, NYL - 2 + row, :]
-    for c in range(3):
+
+    def fill(to_low, to_high):
         for row in (0, 1):
-            to_low[pl.ds((2 + 2 * c + row) * NXL, NXL), :] = displacement[c, :, row, :]
-        to_high[pl.ds((2 + c) * NXL, NXL), :] = displacement[c, :, NYL - 1, :]
-    to_low[pl.ds(8 * NXL, NXL), :] = passive[:, 0, :].astype(jnp.float32)
-    to_high[pl.ds(5 * NXL, NXL), :] = passive[:, NYL - 1, :].astype(jnp.float32)
-
-
-def pack_x(density, displacement, passive, y_high, y_low, after, to_low, to_high):
+            to_low[pl.ds(row * NXL, NXL), :] = density[:, row, :]
+            to_high[pl.ds(row * NXL, NXL), :] = density[:, NYL - 2 + row, :]
+        for c in range(3):
+            for row in (0, 1):
+                to_low[pl.ds((2 + 2 * c + row) * NXL, NXL), :] = displacement[c, :, row, :]
+            to_high[pl.ds((2 + c) * NXL, NXL), :] = displacement[c, :, NYL - 1, :]
+        to_low[pl.ds(8 * NXL, NXL), :] = passive[:, 0, :].astype(jnp.float32)
+        to_high[pl.ds(5 * NXL, NXL), :] = passive[:, NYL - 1, :].astype(jnp.float32)
+        to_high[pl.ds(6 * NXL, 3 * NXL), :] = jnp.zeros((3 * NXL, NZ), jnp.float32)
+
+    even = is_even("gy")
+    pl.when(even)(lambda: fill(send_b, send_a))
+    pl.when(jnp.logical_not(even))(lambda: fill(send_a, send_b))
+
+
+def pack_x(
+    density, displacement, passive, received_a, received_b, after, y_high, y_low, send_a, send_b
+):
     del after
-    for k in (0, 1):
-        to_low[pl.ds(8 * k, 8), :] = density[k]
-        to_high[pl.ds(8 * k, 8), :] = density[NXL - 2 + k]
-    for c in range(3):
+    even = is_even("gy")
+    y_high[...] = jnp.where(even, received_a[...], received_b[...])
+    low = pl.ds(0, 6 * NXL)
+    y_low[...] = jnp.where(even, received_b[low, :], received_a[low, :])
+
+    def fill(to_low, to_high):
         for k in (0, 1):
-            to_low[pl.ds(8 * (2 + 2 * c + k), 8), :] = displacement[c, k]
-        to_high[pl.ds(8 * (2 + c), 8), :] = displacement[c, NXL - 1]
-    to_low[pl.ds(64, 8), :] = passive[0].astype(jnp.float32)
-    to_high[pl.ds(40, 8), :] = passive[NXL - 1].astype(jnp.float32)
-    for base, first, out in ((72, 0, to_low), (48, NXL - 2, to_high)):
-        for kind in range(9):
-            out[pl.ds(base + 2 * kind, 2), :] = y_high[pl.ds(NXL * kind + first, 2), :]
-        for kind in range(6):
-            out[pl.ds(base + 18 + 2 * kind, 2), :] = y_low[pl.ds(NXL * kind + first, 2), :]
-        out[pl.ds(base + 30, 2), :] = jnp.zeros((2, NZ), jnp.float32)
+            to_low[pl.ds(8 * k, 8), :] = density[k]
+            to_high[pl.ds(8 * k, 8), :] = density[NXL - 2 + k]
+        for c in range(3):
+            for k in (0, 1):
+                to_low[pl.ds(8 * (2 + 2 * c + k), 8), :] = displacement[c, k]
+            to_high[pl.ds(8 * (2 + c), 8), :] = displacement[c, NXL - 1]
+        to_low[pl.ds(64, 8), :] = passive[0].astype(jnp.float32)
+        to_high[pl.ds(40, 8), :] = passive[NXL - 1].astype(jnp.float32)
+        for base, first, out in ((72, 0, to_low), (48, NXL - 2, to_high)):
+            for kind in range(9):
+                out[pl.ds(base + 2 * kind, 2), :] = y_high[pl.ds(NXL * kind + first, 2), :]
+            for kind in range(6):
+                out[pl.ds(base + 18 + 2 * kind, 2), :] = y_low[pl.ds(NXL * kind + first, 2), :]
+            out[pl.ds(base + 30, 2), :] = jnp.zeros((2, NZ), jnp.float32)
+        to_high[pl.ds(80, 24), :] = jnp.zeros((24, NZ), jnp.float32)
+
+    even_x = is_even("gx")
+    pl.when(even_x)(lambda: fill(send_b, send_a))
+    pl.when(jnp.logical_not(even_x))(lambda: fill(send_a, send_b))
 
 
 def lane_ends(height):
@@ -237,8 +261,8 @@
     weights,
     y_high,
     y_low,
-    to_low,
-    to_high,
+    sent_a,
+    sent_b,
     spread,
     sensitivity,
     scaled,
@@ -251,6 +275,14 @@
     def rows(ref, kind):
         return ref[pl.ds(kind * NXL, NXL), :]
 
+    even = is_even("gy")
+
+    def sent_low(kind):
+        return jnp.where(even, rows(sent_b, kind), rows(sent_a, kind))
+
+    def sent_high(kind):
+        return jnp.where(even, rows(sent_a, kind), rows(sent_b, kind))
+
     first, last = lane_ends(NXL)
 
     def row_nodes(ref, step, at):
@@ -265,8 +297,8 @@
         return element_energy(before, after)
 
     nodes_8 = row_nodes(y_high, 2, 2)
-    energy_low = row_energy(row_nodes(y_low, 1, 2), row_nodes(to_low, 2, 2))
-    energy_7 = row_energy(row_nodes(to_high, 1, 2), nodes_8)
+    energy_low = row_energy(row_nodes(y_low, 1, 2), [sent_low(2 + 2 * c) for c in range(3)])
+    energy_7 = row_energy([sent_high(2 + c) for c in range(3)], nodes_8)
     energy_high = row_energy(nodes_8, row_nodes(y_high, 2, 3))
 
     dens[:, pl.ds(8, NYL), :] = density[...]
@@ -276,8 +308,8 @@
     energy[:, 7, :] = energy_7
 
     for row, low, mid, high, kind, row_energies in (
-        (0, rows(y_low, 0), rows(y_low, 1), rows(to_low, 0), rows(y_low, 5), energy_low),
-        (9, rows(to_high, 1), rows(y_high, 0), rows(y_high, 1), rows(y_high, 8), energy_high),
+        (0, rows(y_low, 0), rows(y_low, 1), sent_low(0), rows(y_low, 5), energy_low),
+        (9, sent_high(1), rows(y_high, 0), rows(y_high, 1), rows(y_high, 8), energy_high),
     ):
         side, rest = filter_terms(low, mid, high, first, last)
         filtered = rest + pltpu.roll(side, 1, 0) + pltpu.roll(side, NXL - 1, 0)
@@ -335,8 +367,8 @@
     passive,
     y_high,
     y_low,
-    x_high,
-    x_low,
+    received_a,
+    received_b,
     inverse,
     weights,
     spread,
@@ -351,9 +383,14 @@
     kind_of,
     rim,
     partial,
+    x_high,
+    x_low,
     *,
     copies,
 ):
+    even = is_even("gx")
+    x_high[...] = jnp.where(even, received_a[...], received_b[...])
+    x_low[...] = jnp.where(even, received_b[...], received_a[...])
     first, last = lane_ends(NYL)
     at_end = (
         lax.axis_index("gx") == 0,
@@ -558,46 +595,45 @@
     )(*inputs)
 
 
-def shifted(block, axis, distance):
-    devices = range(lax.axis_size(axis))
-    route = [(i - distance, i) for i in devices if i - distance in devices]
-    return lax.ppermute(block, axis, route)
+def swapped(block, axis, start):
+    pairs = [(i, i + 1) for i in range(start, lax.axis_size(axis) - 1, 2)]
+    return lax.ppermute(block, axis, pairs + [(j, i) for i, j in pairs])
 
 
 def per_device(density, displacement, passive):
     count_x, count_y = lax.axis_size("gx"), lax.axis_size("gy")
     assert density.shape == (NXL, NYL, NZ)
     block = (NXL, NYL, NZ)
-    density, displacement, passive, y_to_low, y_to_high = call(
+    density, displacement, passive, sent_a, sent_b = call(
         pack_y,
         (
             near(*block),
             near(3, *block),
             near(*block, dtype=jnp.int32),
             near(9 * NXL, NZ),
-            near(6 * NXL, NZ),
+            near(9 * NXL, NZ),
         ),
         (far(density), far(displacement), far(passive)),
         [pltpu.SemaphoreType.DMA((3,))],
         specs=[pl.BlockSpec(memory_space=pltpu.HBM)] * 3,
         cost=1000,
     )
-    y_high = held(shifted(y_to_low, "gy", -1))
-    y_low = held(shifted(y_to_high, "gy", 1))
+    received_a = held(swapped(sent_a, "gy", 0))
+    received_b = held(swapped(sent_b, "gy", 1))
     own_energy, inverse, weights, factors = call(
         interior_energy,
         (near(*block), near(2, 16, NZ), near(4, NYL, NZ), near(SLOTS, NZ)),
         (displacement,),
         cost=1000,
     )
-    to_low, to_high = call(
+    y_high, y_low, to_a, to_b = call(
         pack_x,
-        (near(104, NZ), near(80, NZ)),
-        (density, displacement, passive, y_high, y_low, weights),
+        (near(9 * NXL, NZ), near(6 * NXL, NZ), near(104, NZ), near(104, NZ)),
+        (density, displacement, passive, received_a, received_b, weights),
         cost=500,
     )
-    x_high = held(shifted(to_low, "gx", -1))
-    x_low = held(shifted(to_high, "gx", 1))
+    received_a = held(swapped(to_a, "gx", 0))
+    received_b = held(swapped(to_b, "gx", 1))
     spread, sensitivity, scaled, lower, upper, partial = call(
         middle,
         (near(NXL, 24, NZ),) + (near(*block),) * 4 + (near(8 * SLOTS, NZ),),
@@ -610,8 +646,8 @@
             weights,
             y_high,
             y_low,
-            y_to_low,
-            y_to_high,
+            sent_a,
+            sent_b,
         ),
         [pltpu.VMEM((NXL, 24, NZ), jnp.float32), pltpu.VMEM(block, jnp.float32)],
         cost=5000,
@@ -628,8 +664,8 @@
             passive,
             y_high,
             y_low,
-            x_high,
-            x_low,
+            received_a,
+            received_b,
             inverse,
             weights,
             spread,
@@ -643,6 +679,8 @@
             pltpu.VMEM((2, 2, 16, NZ), jnp.float32),
             pltpu.VMEM((2, 4, 24, NZ), jnp.float32),
             pltpu.VMEM((8 * SLOTS, NZ), jnp.float32),
+            pltpu.VMEM((104, NZ), jnp.float32),
+            pltpu.VMEM((104, NZ), jnp.float32),
         ],
         cost=3000,
     )

time: 65 us -> 65.6 us (level)
  blocking collectives: 38.9 us -> 40.5 us
  starting transfers between devices: 16.7 us -> 15.3 us
    all_to_all x1, blocking collectives: 13 us -> 14.5 us  [per_device(): lax.all_to_all(volumes, ('gx', 'gy'), 0, 0, axis_index_groups=across)]
    ppermute x4, starting transfers between devices: 16.7 us -> 15.3 us  [swapped(): return lax.ppermute(block, axis, pairs + [(j, i) for i, j in pairs])]
  transfers between devices with their start and end apart: 4 -> 4, of which waited for: 0 -> 1; matrix products, arithmetic and copies ran while one was open for 0% -> 0% of each run, Pallas kernels for 7% -> 7%
where the time goes in v4:
time: 65.6 us; the launch traced here: 65.4 us
  blocking collectives  40.5 us (62%)
  starting transfers between devices  15.3 us (23%)
  Pallas kernels  8.56 us (13%)
  between operations  0.72 us (1%)
    all_to_all x1, blocking collectives, per_device(): lax.all_to_all(volumes, ('gx', 'gy'), 0, 0, axis_index_groups=along)  26 us
    ppermute x4, starting transfers between devices, swapped(): return lax.ppermute(block, axis, pairs + [(j, i) for i, j in pairs])  15.3 us
    all_to_all x1, blocking collectives, per_device(): lax.all_to_all(volumes, ('gx', 'gy'), 0, 0, axis_index_groups=across)  14.5 us
    pallas_call x7, Pallas kernels, call(): pl.pallas_call(kernel, out_shape=outputs, in_specs=specs or [VMEM] * len(...  8.56 us
  transfers between devices with their start and end apart: 4, of which 1 were waited for; matrix products, arithmetic and copies ran while one was open for 0% of the time, Pallas kernels for 7%

profile of v4, /device:TPU:1, one launch (start us, length us, event | category | flops | bytes accessed | tf_op | source)
XLA Modules:
  0.0 65.4 jit_solution(10529421122796770311)
XLA Ops:
  0.6 1.1 %shard_map.50 = (f32[16,8,128]{2,1,0:T(8,128)S(1)}, f32[3,16,8,128]{3,2,1,0:T(8,128)S(1)}, s32[16,8,128]{2,1,0:T(8,128)S(1)}, f32[144,128]{1,0:T(8,128)S(1)}, f32[144,128]{1,0:T(8,128)S(1)}) custom-call(f32[16,8,128]{2,1,0:T(8,128)} %density_far.1, f32[3,16,8,128]{3,2,1,0:T(8,128)} %displacement_far.1, s32[16,8,128]{2,1,0:T(8,128)} %passive_far.1), custom_call_target="tpu_custom_call" | custom-call | flops 4000000 | bytes 1000000 | tf_op jit(solution)/shard_map/pallas_call | solution.py:585
  1.7 4.0 %collective-permute-start = (f32[144,128]{1,0:T(8,128)S(1)}, f32[144,128]{1,0:T(8,128)S(1)}, u32[]{:S(2)}, u32[]{:S(2)}) collective-permute-start(f32[144,128]{1,0:T(8,128)S(1)} %get-tuple-element.28.sent_a), channel_id=1, source_target_pairs={{0,1},{2,3},{4,5},{6,7},{8,9},{10,11},{12,13},{14,15},{1,0},{3,2},... | collective-permute-start | bytes 221192 | tf_op jit(solution)/shard_map/ppermute | solution.py:600
  5.7 0.7 %collective-permute-start.1 = (f32[144,128]{1,0:T(8,128)S(1)}, f32[144,128]{1,0:T(8,128)S(1)}, u32[]{:S(2)}, u32[]{:S(2)}) collective-permute-start(f32[144,128]{1,0:T(8,128)S(1)} %get-tuple-element.29.sent_b), channel_id=1, source_target_pairs={{1,2},{3,4},{5,6},{7,8},{9,10},{11,12},{13,14},{2,1},{4,3},{6,5},{... | collective-permute-start | bytes 221192 | tf_op jit(solution)/shard_map/ppermute | solution.py:600
  6.4 1.5 %shard_map.51 = (f32[16,8,128]{2,1,0:T(8,128)S(1)}, f32[2,16,128]{2,1,0:T(8,128)S(1)}, f32[4,8,128]{2,1,0:T(8,128)S(1)}, f32[256,128]{1,0:T(8,128)S(1)}) custom-call(f32[3,16,8,128]{3,2,1,0:T(8,128)S(1)} %get-tuple-element.24.displacement), custom_call_target="tpu_custom_call" | custom-call | flops 4000000 | bytes 1000000 | tf_op jit(solution)/shard_map/pallas_call | solution.py:585
  8.0 0.0 collective-permute-done.received_a
  8.0 0.0 collective-permute-done.1.received_b
  8.0 8.7 %collective-permute-start.2 = (f32[104,128]{1,0:T(8,128)S(1)}, f32[104,128]{1,0:T(8,128)S(1)}, u32[]{:S(2)}, u32[]{:S(2)}) collective-permute-start(f32[104,128]{1,0:T(8,128)S(1)} %get-tuple-element.33), channel_id=1, source_target_pairs={{0,16},{32,48},{64,80},{96,112},{128,144},{160,176},{192,208},{224... | collective-permute-start | bytes 159752 | tf_op jit(solution)/shard_map/ppermute | solution.py:600
  16.8 1.9 %collective-permute-start.3 = (f32[104,128]{1,0:T(8,128)S(1)}, f32[104,128]{1,0:T(8,128)S(1)}, u32[]{:S(2)}, u32[]{:S(2)}) collective-permute-start(f32[104,128]{1,0:T(8,128)S(1)} %get-tuple-element.34), channel_id=1, source_target_pairs={{16,32},{48,64},{80,96},{112,128},{144,160},{176,192},{208,224},{2... | collective-permute-start | bytes 159752 | tf_op jit(solution)/shard_map/ppermute | solution.py:600
  18.7 3.2 %shard_map.53 = (f32[16,24,128]{2,1,0:T(8,128)S(1)}, f32[16,8,128]{2,1,0:T(8,128)S(1)}, f32[16,8,128]{2,1,0:T(8,128)S(1)}, f32[16,8,128]{2,1,0:T(8,128)S(1)}, f3...) custom-call(f32[256,128]{1,0:T(8,128)S(1)} %get-tuple-element.25.factors, f32[16,8,128]{2,1,0:T(8,128)S(1)} %get-tuple-element.26.density, ...), custom_call_target="tpu_custom_call" | custom-call | flops 20000000 | bytes 5000000 | tf_op jit(solution)/shard_map/pallas_call | solution.py:585
  21.9 0.0 collective-permute-done.2.received_a
  21.9 0.3 collective-permute-done.3.received_b
  22.2 1.4 %shard_map.54 = (f32[4,8,128]{2,1,0:T(8,128)S(1)}, f32[4,8,128]{2,1,0:T(8,128)S(1)}, f32[32,2,128]{2,1,0:T(2,128)S(1)}) custom-call(f32[256,128]{1,0:T(8,128)S(1)} %get-tuple-element.25.factors, f32[16,8,128]{2,1,0:T(8,128)S(1)} %get-tuple-element.26.density, f32[3,16,8,128]{3,2,1,0:T(8,128)S(1)} %get-tuple-element.24.displacement, ...), custom_call_target="tpu_custom_call" | custom-call | flops 12000000 | bytes 3000000 | tf_op jit(solution)/shard_map/pallas_call | solution.py:585
  23.6 14.5 %all_to_all.10.received = f32[32,2,128]{2,1,0:T(2,128)S(1)} all-to-all(f32[32,2,128]{2,1,0:T(2,128)S(1)} %get-tuple-element.41), channel_id=1, replica_groups={{0,1,2,3,4,5,6,7,8,9,10,11,12,13,14,15,16,17,18,19,20,21,22,23,24,25,26..., dimensions={0} | all-to-all | bytes 65536 | tf_op jit(solution)/shard_map/all_to_all | solution.py:697
  38.1 26.0 %all_to_all.11.received = f32[16,2,128]{2,1,0:T(2,128)S(1)} all-to-all(f32[16,2,128]{2,1,0:T(2,128)S(1)} %shard_map.55), channel_id=1, replica_groups={{0,32,64,96,128,160,192,224,256,288,320,352,384,416,448,480},{1,33,65,9..., dimensions={0} | all-to-all | bytes 32768 | tf_op jit(solution)/shard_map/all_to_all | solution.py:704
  64.1 1.3 %shard_map.56 = (f32[16,8,128]{2,1,0:T(8,128)}, f32[16,8,128]{2,1,0:T(8,128)}) custom-call(f32[16,2,128]{2,1,0:T(2,128)S(1)} %all_to_all.11.received, f32[16,8,128]{2,1,0:T(8,128)S(1)} %get-tuple-element.42.scaled, f32[4,8,128]{2,1,0:T(8,128)S(1)} %get-tuple-element.43.scaled_edge, f32[16,8,128]{2,1,0:T(8,128)S(1)} %get-tuple-element.38.lower, ...), custom_call_target="tpu_custom_call" | custom-call | flops 2000000 | bytes 500000 | tf_op jit(solution)/shard_map/pallas_call | solution.py:585
  (2 shorter events, 0.1 us)
Async XLA Ops:
  1.7 6.3 %collective-permute-start = (f32[144,128]{1,0:T(8,128)S(1)}, f32[144,128]{1,0:T(8,128)S(1)}, u32[]{:S(2)}, u32[]{:S(2)}) collective-permute-start(f32[144,128]{1,0:T(8,128)S(1)} %get-tuple-element.28.sent_a), channel_id=1, source_target_pairs={{0,1},{2,3},{4,5},{6,7},{8,9},{10,11},{12,13},{14,15},{1,0},{3,2},... | collective-permute-start | bytes 221192 | tf_op jit(solution)/shard_map/ppermute | solution.py:600
  5.7 2.2 %collective-permute-start.1 = (f32[144,128]{1,0:T(8,128)S(1)}, f32[144,128]{1,0:T(8,128)S(1)}, u32[]{:S(2)}, u32[]{:S(2)}) collective-permute-start(f32[144,128]{1,0:T(8,128)S(1)} %get-tuple-element.29.sent_b), channel_id=1, source_target_pairs={{1,2},{3,4},{5,6},{7,8},{9,10},{11,12},{13,14},{2,1},{4,3},{6,5},{... | collective-permute-start | bytes 221192 | tf_op jit(solution)/shard_map/ppermute | solution.py:600
  8.0 13.9 %collective-permute-start.2 = (f32[104,128]{1,0:T(8,128)S(1)}, f32[104,128]{1,0:T(8,128)S(1)}, u32[]{:S(2)}, u32[]{:S(2)}) collective-permute-start(f32[104,128]{1,0:T(8,128)S(1)} %get-tuple-element.33), channel_id=1, source_target_pairs={{0,16},{32,48},{64,80},{96,112},{128,144},{160,176},{192,208},{224... | collective-permute-start | bytes 159752 | tf_op jit(solution)/shard_map/ppermute | solution.py:600
  16.8 5.5 %collective-permute-start.3 = (f32[104,128]{1,0:T(8,128)S(1)}, f32[104,128]{1,0:T(8,128)S(1)}, u32[]{:S(2)}, u32[]{:S(2)}) collective-permute-start(f32[104,128]{1,0:T(8,128)S(1)} %get-tuple-element.34), channel_id=1, source_target_pairs={{16,32},{48,64},{80,96},{112,128},{144,160},{176,192},{208,224},{2... | collective-permute-start | bytes 159752 | tf_op jit(solution)/shard_map/ppermute | solution.py:600

commit v5 on v4

--- a/solution.py
+++ b/solution.py
@@ -25,12 +25,13 @@
 SLOTS = TRIALS + 1
 STEP = 2.0 * BRACKET / 2 ** BISECT
 GROUP = 16
+SIDE = 4
 
 VMEM = pl.BlockSpec(memory_space=pltpu.VMEM)
 
 
-def is_even(axis):
-    return lax.rem(lax.axis_index(axis), 2) == 0
+def is_odd(axis):
+    return lax.rem(lax.axis_index(axis), 2) == 1
 
 
 def pack_y(
@@ -63,19 +64,19 @@
         to_high[pl.ds(5 * NXL, NXL), :] = passive[:, NYL - 1, :].astype(jnp.float32)
         to_high[pl.ds(6 * NXL, 3 * NXL), :] = jnp.zeros((3 * NXL, NZ), jnp.float32)
 
-    even = is_even("gy")
-    pl.when(even)(lambda: fill(send_b, send_a))
-    pl.when(jnp.logical_not(even))(lambda: fill(send_a, send_b))
+    odd = is_odd("gy")
+    pl.when(odd)(lambda: fill(send_b, send_a))
+    pl.when(jnp.logical_not(odd))(lambda: fill(send_a, send_b))
 
 
 def pack_x(
     density, displacement, passive, received_a, received_b, after, y_high, y_low, send_a, send_b
 ):
     del after
-    even = is_even("gy")
-    y_high[...] = jnp.where(even, received_a[...], received_b[...])
+    odd = is_odd("gy")
+    y_high[...] = jnp.where(odd, received_a[...], received_b[...])
     low = pl.ds(0, 6 * NXL)
-    y_low[...] = jnp.where(even, received_b[low, :], received_a[low, :])
+    y_low[...] = jnp.where(odd, received_b[low, :], received_a[low, :])
 
     def fill(to_low, to_high):
         for k in (0, 1):
@@ -95,9 +96,9 @@
             out[pl.ds(base + 30, 2), :] = jnp.zeros((2, NZ), jnp.float32)
         to_high[pl.ds(80, 24), :] = jnp.zeros((24, NZ), jnp.float32)
 
-    even_x = is_even("gx")
-    pl.when(even_x)(lambda: fill(send_b, send_a))
-    pl.when(jnp.logical_not(even_x))(lambda: fill(send_a, send_b))
+    odd_x = is_odd("gx")
+    pl.when(odd_x)(lambda: fill(send_b, send_a))
+    pl.when(jnp.logical_not(odd_x))(lambda: fill(send_a, send_b))
 
 
 def lane_ends(height):
@@ -275,13 +276,13 @@
     def rows(ref, kind):
         return ref[pl.ds(kind * NXL, NXL), :]
 
-    even = is_even("gy")
+    odd = is_odd("gy")
 
     def sent_low(kind):
-        return jnp.where(even, rows(sent_b, kind), rows(sent_a, kind))
+        return jnp.where(odd, rows(sent_b, kind), rows(sent_a, kind))
 
     def sent_high(kind):
-        return jnp.where(even, rows(sent_a, kind), rows(sent_b, kind))
+        return jnp.where(odd, rows(sent_a, kind), rows(sent_b, kind))
 
     first, last = lane_ends(NXL)
 
@@ -372,6 +373,7 @@
     inverse,
     weights,
     spread,
+    inner_sensitivity,
     lower,
     upper,
     start,
@@ -388,9 +390,9 @@
     *,
     copies,
 ):
-    even = is_even("gx")
-    x_high[...] = jnp.where(even, received_a[...], received_b[...])
-    x_low[...] = jnp.where(even, received_b[...], received_a[...])
+    odd = is_odd("gx")
+    x_high[...] = jnp.where(odd, received_a[...], received_b[...])
+    x_low[...] = jnp.where(odd, received_b[...], received_a[...])
     first, last = lane_ends(NYL)
     at_end = (
         lax.axis_index("gx") == 0,
@@ -477,6 +479,8 @@
         for k in (0, 1):
             rim[side, (2 + k if side == 0 else k), :, :] = spread[1 + k if side == 0 else 13 + k]
 
+    inner_planes = pl.ds(2, NXL - 4)
+    sensitivity[inner_planes] = inner_sensitivity[inner_planes]
     side_inner, rest_inner, side_edge, rest_edge = (weights[i] for i in range(4))
     for side in (0, 1):
         outer_side = jnp.where(at_end[side], 0.0, side_inner)
@@ -488,7 +492,7 @@
             x = k if side == 0 else NXL - 2 + k
             sens = terms[k + 1][1] + terms[k][0] + terms[k + 2][0]
             weight = outer if k == side else inner
-            sensitivity[2 * side + k] = sens
+            sensitivity[x] = sens
             scaled[2 * side + k] = density[x] * jnp.sqrt(-sens / weight)
 
     add_volumes(
@@ -511,8 +515,8 @@
         precision=lax.Precision.HIGHEST,
         preferred_element_type=jnp.float32,
     )
-    odd = lax.broadcasted_iota(jnp.int32, (8, NZ), 0) > 0
-    pair = jnp.where(odd, volumes[:, NZ:], volumes[:, :NZ])[0:2]
+    second = lax.broadcasted_iota(jnp.int32, (8, NZ), 0) > 0
+    pair = jnp.where(second, volumes[:, NZ:], volumes[:, :NZ])[0:2]
     for copy in range(copies):
         sums_out[copy] = pair
 
@@ -523,31 +527,7 @@
         out[copy] = total
 
 
-def finish(
-    received,
-    scaled,
-    scaled_edge,
-    lower,
-    upper,
-    sensitivity,
-    sensitivity_edge,
-    new_density,
-    sensitivity_out,
-    sems,
-    *,
-    target,
-):
-    inner = pl.ds(2, NXL - 4)
-    ends = ((pl.ds(0, 2), pl.ds(0, 2)), (pl.ds(2, 2), pl.ds(NXL - 2, 2)))
-    copies = [pltpu.make_async_copy(sensitivity.at[inner], sensitivity_out.at[inner], sems.at[0])]
-    for i, (place, planes) in enumerate(ends):
-        copies.append(
-            pltpu.make_async_copy(
-                sensitivity_edge.at[place], sensitivity_out.at[planes], sems.at[1 + i]
-            )
-        )
-    for copy in copies:
-        copy.start()
+def finish(received, scaled, scaled_edge, lower, upper, new_density, *, target):
     volumes = jnp.sum(received[...], axis=0)
     slot = lax.broadcasted_iota(jnp.int32, (2, NZ), 0) * NZ + lax.broadcasted_iota(
         jnp.int32, (2, NZ), 1
@@ -555,14 +535,15 @@
     above = jnp.sum(jnp.where((volumes > target) & (slot < TRIALS), 1.0, 0.0))
     middle_end = -BRACKET + STEP * above + 0.5 * STEP
     factor = jnp.exp(jnp.full((8, NZ), -0.5, jnp.float32) * middle_end)[None]
-    for ref, place, planes in ((scaled, inner, inner),) + tuple(
-        (scaled_edge, place, planes) for place, planes in ends
+    inner = pl.ds(2, NXL - 4)
+    for ref, place, planes in (
+        (scaled, inner, inner),
+        (scaled_edge, pl.ds(0, 2), pl.ds(0, 2)),
+        (scaled_edge, pl.ds(2, 2), pl.ds(NXL - 2, 2)),
     ):
         new_density[planes] = jnp.minimum(
             jnp.maximum(ref[place] * factor, lower[planes]), upper[planes]
         )
-    for copy in copies:
-        copy.wait()
 
 
 def f32(*shape):
@@ -581,12 +562,12 @@
     return pltpu.with_memory_space_constraint(array, pltpu.VMEM)
 
 
-def call(kernel, outputs, inputs, scratch=(), specs=None, out_specs=None, cost=0):
+def call(kernel, outputs, inputs, scratch=(), specs=None, cost=0):
     return pl.pallas_call(
         kernel,
         out_shape=outputs,
         in_specs=specs or [VMEM] * len(inputs),
-        out_specs=out_specs or jax.tree.map(lambda _: VMEM, outputs),
+        out_specs=jax.tree.map(lambda _: VMEM, outputs),
         scratch_shapes=list(scratch),
         cost_estimate=pl.CostEstimate(
             flops=cost * 4000, bytes_accessed=cost * 1000, transcendentals=0
@@ -598,6 +579,16 @@
 def swapped(block, axis, start):
     pairs = [(i, i + 1) for i in range(start, lax.axis_size(axis) - 1, 2)]
     return lax.ppermute(block, axis, pairs + [(j, i) for i, j in pairs])
+
+
+def reduction_groups(count_x, count_y):
+    across, along = {}, {}
+    for gx in range(count_x):
+        for gy in range(count_y):
+            device = gx * count_y + gy
+            across.setdefault((gx // 2, gy // SIDE), []).append(device)
+            along.setdefault((gx % 2, gy % SIDE), []).append(device)
+    return list(across.values()), list(along.values())
 
 
 def per_device(density, displacement, passive):
@@ -618,8 +609,8 @@
         specs=[pl.BlockSpec(memory_space=pltpu.HBM)] * 3,
         cost=1000,
     )
-    received_a = held(swapped(sent_a, "gy", 0))
-    received_b = held(swapped(sent_b, "gy", 1))
+    received_a = held(swapped(sent_a, "gy", 1))
+    received_b = held(swapped(sent_b, "gy", 0))
     own_energy, inverse, weights, factors = call(
         interior_energy,
         (near(*block), near(2, 16, NZ), near(4, NYL, NZ), near(SLOTS, NZ)),
@@ -632,8 +623,8 @@
         (density, displacement, passive, received_a, received_b, weights),
         cost=500,
     )
-    received_a = held(swapped(to_a, "gx", 0))
-    received_b = held(swapped(to_b, "gx", 1))
+    received_a = held(swapped(to_a, "gx", 1))
+    received_b = held(swapped(to_b, "gx", 0))
     spread, sensitivity, scaled, lower, upper, partial = call(
         middle,
         (near(NXL, 24, NZ),) + (near(*block),) * 4 + (near(8 * SLOTS, NZ),),
@@ -652,11 +643,10 @@
         [pltpu.VMEM((NXL, 24, NZ), jnp.float32), pltpu.VMEM(block, jnp.float32)],
         cost=5000,
     )
-    plane = 2 * count_y
-    layers = count_x // 2
-    sensitivity_edge, scaled_edge, volumes = call(
-        functools.partial(edges, copies=plane),
-        (near(4, NYL, NZ), near(4, NYL, NZ), near(plane, 2, NZ)),
+    first_group, second_group = 2 * SIDE, count_x * count_y // (2 * SIDE)
+    sensitivity, scaled_edge, volumes = call(
+        functools.partial(edges, copies=first_group),
+        (near(*block), near(4, NYL, NZ), near(first_group, 2, NZ)),
         (
             factors,
             density,
@@ -669,6 +659,7 @@
             inverse,
             weights,
             spread,
+            sensitivity,
             lower,
             upper,
             partial,
@@ -685,30 +676,20 @@
         cost=3000,
     )
 
-    across = [
-        [(2 * z + core) * count_y + y for core in (0, 1) for y in range(count_y)]
-        for z in range(layers)
-    ]
-    along = [
-        [(2 * z + core) * count_y + y for z in range(layers)]
-        for core in (0, 1)
-        for y in range(count_y)
-    ]
+    across, along = reduction_groups(count_x, count_y)
     volumes = lax.all_to_all(volumes, ("gx", "gy"), 0, 0, axis_index_groups=across)
     volumes = call(
-        functools.partial(add_copies, copies=layers),
-        near(layers, 2, NZ),
+        functools.partial(add_copies, copies=second_group),
+        near(second_group, 2, NZ),
         (held(volumes),),
         cost=300,
     )
     volumes = lax.all_to_all(volumes, ("gx", "gy"), 0, 0, axis_index_groups=along)
     target = VOLUME_SHARE * (count_x * NXL) * (count_y * NYL) * NZ
-    new_density, sensitivity = call(
+    new_density = call(
         functools.partial(finish, target=target),
-        (f32(*block), f32(*block)),
-        (held(volumes), scaled, scaled_edge, lower, upper, sensitivity, sensitivity_edge),
-        [pltpu.SemaphoreType.DMA((3,))],
-        out_specs=(VMEM, pl.BlockSpec(memory_space=pltpu.HBM)),
+        f32(*block),
+        (held(volumes), scaled, scaled_edge, lower, upper),
         cost=500,
     )
     return new_density, sensitivity

time: 65.6 us -> 65.4 us (level)
  blocking collectives: 40.5 us -> 9.32 us
  starting transfers between devices: 15.3 us -> 32.1 us
  waiting for transfers between devices: 0.29 us -> 13.6 us
    all_to_all x1 -> x0, blocking collectives: 26 us -> none  [per_device(): lax.all_to_all(volumes, ('gx', 'gy'), 0, 0, axis_index_groups=along)]
    all_to_all x0 -> x1, starting transfers between devices: none -> 17.5 us  [per_device(): lax.all_to_all(volumes, ('gx', 'gy'), 0, 0, axis_index_groups=along)]
    all_to_all x0 -> x1, waiting for transfers between devices: none -> 13.4 us  [per_device(): lax.all_to_all(volumes, ('gx', 'gy'), 0, 0, axis_index_groups=along)]
    all_to_all x1, blocking collectives: 14.5 us -> 9.32 us  [per_device(): lax.all_to_all(volumes, ('gx', 'gy'), 0, 0, axis_index_groups=across)]
    ppermute x4, starting transfers between devices: 15.3 us -> 14.6 us  [swapped(): return lax.ppermute(block, axis, pairs + [(j, i) for i, j in pairs])]
  transfers between devices with their start and end apart: 4 -> 5, of which waited for: 1 -> 2; matrix products, arithmetic and copies ran while one was open for 0% -> 1% of each run, Pallas kernels for 7% -> 7%
where the time goes in v5:
time: 65.4 us; the launch traced here: 65 us
  starting transfers between devices  32.1 us (49%)
  waiting for transfers between devices  13.6 us (21%)
  blocking collectives  9.32 us (14%)
  Pallas kernels  8.7 us (13%)
  between operations  0.72 us (1%)
    all_to_all x1, starting transfers between devices, per_device(): lax.all_to_all(volumes, ('gx', 'gy'), 0, 0, axis_index_groups=along)  17.5 us
    ppermute x4, starting transfers between devices, swapped(): return lax.ppermute(block, axis, pairs + [(j, i) for i, j in pairs])  14.6 us
    all_to_all x1, waiting for transfers between devices, per_device(): lax.all_to_all(volumes, ('gx', 'gy'), 0, 0, axis_index_groups=along)  13.4 us
    all_to_all x1, blocking collectives, per_device(): lax.all_to_all(volumes, ('gx', 'gy'), 0, 0, axis_index_groups=across)  9.32 us
    pallas_call x7, Pallas kernels, call(): pl.pallas_call(kernel, out_shape=outputs, in_specs=specs or [VMEM] * len(...  8.7 us
  transfers between devices with their start and end apart: 5, of which 2 were waited for; matrix products, arithmetic and copies ran while one was open for 1% of the time, Pallas kernels for 7%

profile of v5, /device:TPU:1, one launch (start us, length us, event | category | flops | bytes accessed | tf_op | source)
XLA Modules:
  0.0 65.0 jit_solution(9990188486451881220)
XLA Ops:
  0.6 1.1 %shard_map.50 = (f32[16,8,128]{2,1,0:T(8,128)S(1)}, f32[3,16,8,128]{3,2,1,0:T(8,128)S(1)}, s32[16,8,128]{2,1,0:T(8,128)S(1)}, f32[144,128]{1,0:T(8,128)S(1)}, f32[144,128]{1,0:T(8,128)S(1)}) custom-call(f32[16,8,128]{2,1,0:T(8,128)} %density_far.1, f32[3,16,8,128]{3,2,1,0:T(8,128)} %displacement_far.1, s32[16,8,128]{2,1,0:T(8,128)} %passive_far.1), custom_call_target="tpu_custom_call" | custom-call | flops 4000000 | bytes 1000000 | tf_op jit(solution)/shard_map/pallas_call | solution.py:566
  1.7 0.7 %collective-permute-start = (f32[144,128]{1,0:T(8,128)S(1)}, f32[144,128]{1,0:T(8,128)S(1)}, u32[]{:S(2)}, u32[]{:S(2)}) collective-permute-start(f32[144,128]{1,0:T(8,128)S(1)} %get-tuple-element.28.sent_a), channel_id=1, source_target_pairs={{1,2},{3,4},{5,6},{7,8},{9,10},{11,12},{13,14},{2,1},{4,3},{6,5},{... | collective-permute-start | bytes 221192 | tf_op jit(solution)/shard_map/ppermute | solution.py:581
  2.4 6.6 %collective-permute-start.1 = (f32[144,128]{1,0:T(8,128)S(1)}, f32[144,128]{1,0:T(8,128)S(1)}, u32[]{:S(2)}, u32[]{:S(2)}) collective-permute-start(f32[144,128]{1,0:T(8,128)S(1)} %get-tuple-element.29.sent_b), channel_id=1, source_target_pairs={{0,1},{2,3},{4,5},{6,7},{8,9},{10,11},{12,13},{14,15},{1,0},{3,2},... | collective-permute-start | bytes 221192 | tf_op jit(solution)/shard_map/ppermute | solution.py:581
  8.9 1.5 %shard_map.51 = (f32[16,8,128]{2,1,0:T(8,128)S(1)}, f32[2,16,128]{2,1,0:T(8,128)S(1)}, f32[4,8,128]{2,1,0:T(8,128)S(1)}, f32[256,128]{1,0:T(8,128)S(1)}) custom-call(f32[3,16,8,128]{3,2,1,0:T(8,128)S(1)} %get-tuple-element.24.displacement), custom_call_target="tpu_custom_call" | custom-call | flops 4000000 | bytes 1000000 | tf_op jit(solution)/shard_map/pallas_call | solution.py:566
  10.5 0.0 collective-permute-done.received_a
  10.5 0.2 collective-permute-done.1.received_b
  10.7 5.3 %collective-permute-start.2 = (f32[104,128]{1,0:T(8,128)S(1)}, f32[104,128]{1,0:T(8,128)S(1)}, u32[]{:S(2)}, u32[]{:S(2)}) collective-permute-start(f32[104,128]{1,0:T(8,128)S(1)} %get-tuple-element.33), channel_id=1, source_target_pairs={{16,32},{48,64},{80,96},{112,128},{144,160},{176,192},{208,224},{2... | collective-permute-start | bytes 159752 | tf_op jit(solution)/shard_map/ppermute | solution.py:581
  16.0 2.1 %collective-permute-start.3 = (f32[104,128]{1,0:T(8,128)S(1)}, f32[104,128]{1,0:T(8,128)S(1)}, u32[]{:S(2)}, u32[]{:S(2)}) collective-permute-start(f32[104,128]{1,0:T(8,128)S(1)} %get-tuple-element.34), channel_id=1, source_target_pairs={{0,16},{32,48},{64,80},{96,112},{128,144},{160,176},{192,208},{224... | collective-permute-start | bytes 159752 | tf_op jit(solution)/shard_map/ppermute | solution.py:581
  18.1 3.2 %shard_map.53 = (f32[16,24,128]{2,1,0:T(8,128)S(1)}, f32[16,8,128]{2,1,0:T(8,128)S(1)}, f32[16,8,128]{2,1,0:T(8,128)S(1)}, f32[16,8,128]{2,1,0:T(8,128)S(1)}, f3...) custom-call(f32[256,128]{1,0:T(8,128)S(1)} %get-tuple-element.25.factors, f32[16,8,128]{2,1,0:T(8,128)S(1)} %get-tuple-element.26.density, ...), custom_call_target="tpu_custom_call" | custom-call | flops 20000000 | bytes 5000000 | tf_op jit(solution)/shard_map/pallas_call | solution.py:566
  21.3 0.0 collective-permute-done.2.received_a
  21.3 0.0 collective-permute-done.3.received_b
  21.3 1.4 %shard_map.54 = (f32[16,8,128]{2,1,0:T(8,128)S(1)}, f32[4,8,128]{2,1,0:T(8,128)S(1)}, f32[8,2,128]{2,1,0:T(2,128)S(1)}) custom-call(f32[256,128]{1,0:T(8,128)S(1)} %get-tuple-element.25.factors, f32[16,8,128]{2,1,0:T(8,128)S(1)} %get-tuple-element.26.density, f32[3,16,8,128]{3,2,1,0:T(8,128)S(1)} %get-tuple-element.24.displacement, ...), custom_call_target="tpu_custom_call" | custom-call | flops 12000000 | bytes 3000000 | tf_op jit(solution)/shard_map/pallas_call | solution.py:566
  22.7 9.3 %all_to_all.10.received = f32[8,2,128]{2,1,0:T(2,128)S(1)} all-to-all(f32[8,2,128]{2,1,0:T(2,128)S(1)} %get-tuple-element.42), channel_id=1, replica_groups={{0,1,2,3,16,17,18,19},{4,5,6,7,20,21,22,23},{8,9,10,11,24,25,26,27},{12..., dimensions={0} | all-to-all | bytes 16384 | tf_op jit(solution)/shard_map/all_to_all | solution.py:680
  32.0 0.7 %shard_map.55 = f32[64,2,128]{2,1,0:T(2,128)} custom-call(f32[8,2,128]{2,1,0:T(2,128)S(1)} %all_to_all.10.received), custom_call_target="tpu_custom_call" | custom-call | flops 1200000 | bytes 300000 | tf_op jit(solution)/shard_map/pallas_call | solution.py:566
  32.7 17.5 %all-to-all-start.1 = ((f32[64,2,128]{2,1,0:T(2,128)}), f32[64,2,128]{2,1,0:T(2,128)S(1)}, u32[]{:S(2)}, u32[]{:S(2)}) async-start(f32[64,2,128]{2,1,0:T(2,128)} %shard_map.55), calls=%async_computation.1 | async-start | bytes 131072 | tf_op jit(solution)/shard_map/all_to_all | solution.py:687
  50.2 0.6 copy.5
  50.8 13.4 %all-to-all-done.1.received = f32[64,2,128]{2,1,0:T(2,128)S(1)} async-done(((f32[64,2,128]{2,1,0:T(2,128)}), f32[64,2,128]{2,1,0:T(2,128)S(1)}, u32[]{:S(2)}, u32[]{:S(2)}) %all-to-all-start.1) | async-done | bytes 65568 | tf_op jit(solution)/shard_map/all_to_all | solution.py:687
  64.2 0.8 %shard_map.56 = f32[16,8,128]{2,1,0:T(8,128)} custom-call(f32[64,2,128]{2,1,0:T(2,128)S(1)} %all-to-all-done.1.received, f32[16,8,128]{2,1,0:T(8,128)S(1)} %get-tuple-element.43.scaled, f32[4,8,128]{2,1,0:T(8,128)S(1)} %get-tuple-element.44.scaled_edge, f32[16,8,128]{2,1,0:T(8,128)S(1)} %get-tuple-element.39.lower, f32[16,8,128]{2,1,0:T(8,128)S(1)} %get-tuple-element.40.upper), custom_call_target="tpu_custom_call" | custom-call | flops 2000000 | bytes 500000 | tf_op jit(solution)/shard_map/pallas_call | solution.py:566
  (1 shorter events, 0.0 us)
Async XLA Ops:
  1.7 8.8 %collective-permute-start = (f32[144,128]{1,0:T(8,128)S(1)}, f32[144,128]{1,0:T(8,128)S(1)}, u32[]{:S(2)}, u32[]{:S(2)}) collective-permute-start(f32[144,128]{1,0:T(8,128)S(1)} %get-tuple-element.28.sent_a), channel_id=1, source_target_pairs={{1,2},{3,4},{5,6},{7,8},{9,10},{11,12},{13,14},{2,1},{4,3},{6,5},{... | collective-permute-start | bytes 221192 | tf_op jit(solution)/shard_map/ppermute | solution.py:581
  2.4 8.3 %collective-permute-start.1 = (f32[144,128]{1,0:T(8,128)S(1)}, f32[144,128]{1,0:T(8,128)S(1)}, u32[]{:S(2)}, u32[]{:S(2)}) collective-permute-start(f32[144,128]{1,0:T(8,128)S(1)} %get-tuple-element.29.sent_b), channel_id=1, source_target_pairs={{0,1},{2,3},{4,5},{6,7},{8,9},{10,11},{12,13},{14,15},{1,0},{3,2},... | collective-permute-start | bytes 221192 | tf_op jit(solution)/shard_map/ppermute | solution.py:581
  10.7 10.6 %collective-permute-start.2 = (f32[104,128]{1,0:T(8,128)S(1)}, f32[104,128]{1,0:T(8,128)S(1)}, u32[]{:S(2)}, u32[]{:S(2)}) collective-permute-start(f32[104,128]{1,0:T(8,128)S(1)} %get-tuple-element.33), channel_id=1, source_target_pairs={{16,32},{48,64},{80,96},{112,128},{144,160},{176,192},{208,224},{2... | collective-permute-start | bytes 159752 | tf_op jit(solution)/shard_map/ppermute | solution.py:581
  16.0 5.3 %collective-permute-start.3 = (f32[104,128]{1,0:T(8,128)S(1)}, f32[104,128]{1,0:T(8,128)S(1)}, u32[]{:S(2)}, u32[]{:S(2)}) collective-permute-start(f32[104,128]{1,0:T(8,128)S(1)} %get-tuple-element.34), channel_id=1, source_target_pairs={{0,16},{32,48},{64,80},{96,112},{128,144},{160,176},{192,208},{224... | collective-permute-start | bytes 159752 | tf_op jit(solution)/shard_map/ppermute | solution.py:581
  32.7 31.5 %all-to-all-start.1 = ((f32[64,2,128]{2,1,0:T(2,128)}), f32[64,2,128]{2,1,0:T(2,128)S(1)}, u32[]{:S(2)}, u32[]{:S(2)}) async-start(f32[64,2,128]{2,1,0:T(2,128)} %shard_map.55), calls=%async_computation.1 | async-start | bytes 131072 | tf_op jit(solution)/shard_map/all_to_all | solution.py:687

commit v6 on v5

--- a/solution.py
+++ b/solution.py
@@ -527,7 +527,25 @@
         out[copy] = total
 
 
-def finish(received, scaled, scaled_edge, lower, upper, new_density, *, target):
+def finish(
+    received,
+    scaled,
+    scaled_edge,
+    lower,
+    upper,
+    sensitivity,
+    new_density_far,
+    sensitivity_far,
+    new_density,
+    sems,
+    *,
+    target,
+):
+    copies = [
+        pltpu.make_async_copy(sensitivity, sensitivity_far, sems.at[0]),
+        pltpu.make_async_copy(new_density, new_density_far, sems.at[1]),
+    ]
+    copies[0].start()
     volumes = jnp.sum(received[...], axis=0)
     slot = lax.broadcasted_iota(jnp.int32, (2, NZ), 0) * NZ + lax.broadcasted_iota(
         jnp.int32, (2, NZ), 1
@@ -544,6 +562,9 @@
         new_density[planes] = jnp.minimum(
             jnp.maximum(ref[place] * factor, lower[planes]), upper[planes]
         )
+    copies[1].start()
+    for copy in copies:
+        copy.wait()
 
 
 def f32(*shape):
@@ -562,12 +583,12 @@
     return pltpu.with_memory_space_constraint(array, pltpu.VMEM)
 
 
-def call(kernel, outputs, inputs, scratch=(), specs=None, cost=0):
+def call(kernel, outputs, inputs, scratch=(), specs=None, out_specs=None, cost=0):
     return pl.pallas_call(
         kernel,
         out_shape=outputs,
         in_specs=specs or [VMEM] * len(inputs),
-        out_specs=jax.tree.map(lambda _: VMEM, outputs),
+        out_specs=out_specs or jax.tree.map(lambda _: VMEM, outputs),
         scratch_shapes=list(scratch),
         cost_estimate=pl.CostEstimate(
             flops=cost * 4000, bytes_accessed=cost * 1000, transcendentals=0
@@ -582,12 +603,14 @@
 
 
 def reduction_groups(count_x, count_y):
+    chips_x = count_y // SIDE
     across, along = {}, {}
     for gx in range(count_x):
         for gy in range(count_y):
             device = gx * count_y + gy
-            across.setdefault((gx // 2, gy // SIDE), []).append(device)
-            along.setdefault((gx % 2, gy % SIDE), []).append(device)
+            x, y = gy // SIDE, gy % SIDE
+            across.setdefault((gx // 2, x // 2), []).append(device)
+            along.setdefault((gx % 2, y, min(x, chips_x - 1 - x)), []).append(device)
     return list(across.values()), list(along.values())
 
 
@@ -643,7 +666,8 @@
         [pltpu.VMEM((NXL, 24, NZ), jnp.float32), pltpu.VMEM(block, jnp.float32)],
         cost=5000,
     )
-    first_group, second_group = 2 * SIDE, count_x * count_y // (2 * SIDE)
+    across, along = reduction_groups(count_x, count_y)
+    first_group, second_group = len(across[0]), len(along[0])
     sensitivity, scaled_edge, volumes = call(
         functools.partial(edges, copies=first_group),
         (near(*block), near(4, NYL, NZ), near(first_group, 2, NZ)),
@@ -676,7 +700,6 @@
         cost=3000,
     )
 
-    across, along = reduction_groups(count_x, count_y)
     volumes = lax.all_to_all(volumes, ("gx", "gy"), 0, 0, axis_index_groups=across)
     volumes = call(
         functools.partial(add_copies, copies=second_group),
@@ -686,10 +709,12 @@
     )
     volumes = lax.all_to_all(volumes, ("gx", "gy"), 0, 0, axis_index_groups=along)
     target = VOLUME_SHARE * (count_x * NXL) * (count_y * NYL) * NZ
-    new_density = call(
+    new_density, sensitivity = call(
         functools.partial(finish, target=target),
-        f32(*block),
-        (held(volumes), scaled, scaled_edge, lower, upper),
+        (f32(*block), f32(*block)),
+        (held(volumes), scaled, scaled_edge, lower, upper, sensitivity),
+        [pltpu.VMEM(block, jnp.float32), pltpu.SemaphoreType.DMA((2,))],
+        out_specs=(pl.BlockSpec(memory_space=pltpu.HBM),) * 2,
         cost=500,
     )
     return new_density, sensitivity

time: 65.4 us -> 63.6 us (0.972)
  blocking collectives: 9.32 us -> 39.8 us
  starting transfers between devices: 32.1 us -> 14.6 us
  waiting for transfers between devices: 13.6 us -> 0.18 us
    all_to_all x0 -> x1, blocking collectives: none -> 28.6 us  [per_device(): lax.all_to_all(volumes, ('gx', 'gy'), 0, 0, axis_index_groups=along)]
    all_to_all x1 -> x0, starting transfers between devices: 17.5 us -> none  [per_device(): lax.all_to_all(volumes, ('gx', 'gy'), 0, 0, axis_index_groups=along)]
    all_to_all x1 -> x0, waiting for transfers between devices: 13.4 us -> none  [per_device(): lax.all_to_all(volumes, ('gx', 'gy'), 0, 0, axis_index_groups=along)]
    all_to_all x1, blocking collectives: 9.32 us -> 11.2 us  [per_device(): lax.all_to_all(volumes, ('gx', 'gy'), 0, 0, axis_index_groups=across)]
  transfers between devices with their start and end apart: 5 -> 4, of which waited for: 2 -> 1; matrix products, arithmetic and copies ran while one was open for 1% -> 0% of each run, Pallas kernels for 7% -> 8%
where the time goes in v6:
time: 63.6 us; the launch traced here: 63.3 us
  blocking collectives  39.8 us (63%)
  starting transfers between devices  14.6 us (23%)
  Pallas kernels  8.08 us (13%)
  between operations  0.71 us (1%)
    all_to_all x1, blocking collectives, per_device(): lax.all_to_all(volumes, ('gx', 'gy'), 0, 0, axis_index_groups=along)  28.6 us
    ppermute x4, starting transfers between devices, swapped(): return lax.ppermute(block, axis, pairs + [(j, i) for i, j in pairs])  14.6 us
    all_to_all x1, blocking collectives, per_device(): lax.all_to_all(volumes, ('gx', 'gy'), 0, 0, axis_index_groups=across)  11.2 us
    pallas_call x7, Pallas kernels, call(): pl.pallas_call(kernel, out_shape=outputs, in_specs=specs or [VMEM] * len(...  8.08 us
  transfers between devices with their start and end apart: 4, of which 1 were waited for; matrix products, arithmetic and copies ran while one was open for 0% of the time, Pallas kernels for 8%

profile of v6, /device:TPU:1, one launch (start us, length us, event | category | flops | bytes accessed | tf_op | source)
XLA Modules:
  0.0 63.3 jit_solution(1658448928712298863)
XLA Ops:
  0.6 1.1 %shard_map.50 = (f32[16,8,128]{2,1,0:T(8,128)S(1)}, f32[3,16,8,128]{3,2,1,0:T(8,128)S(1)}, s32[16,8,128]{2,1,0:T(8,128)S(1)}, f32[144,128]{1,0:T(8,128)S(1)}, f32[144,128]{1,0:T(8,128)S(1)}) custom-call(f32[16,8,128]{2,1,0:T(8,128)} %density_far.1, f32[3,16,8,128]{3,2,1,0:T(8,128)} %displacement_far.1, s32[16,8,128]{2,1,0:T(8,128)} %passive_far.1), custom_call_target="tpu_custom_call" | custom-call | flops 4000000 | bytes 1000000 | tf_op jit(solution)/shard_map/pallas_call | solution.py:587
  1.7 0.7 %collective-permute-start = (f32[144,128]{1,0:T(8,128)S(1)}, f32[144,128]{1,0:T(8,128)S(1)}, u32[]{:S(2)}, u32[]{:S(2)}) collective-permute-start(f32[144,128]{1,0:T(8,128)S(1)} %get-tuple-element.28.sent_a), channel_id=1, source_target_pairs={{1,2},{3,4},{5,6},{7,8},{9,10},{11,12},{13,14},{2,1},{4,3},{6,5},{... | collective-permute-start | bytes 221192 | tf_op jit(solution)/shard_map/ppermute | solution.py:602
  2.4 6.6 %collective-permute-start.1 = (f32[144,128]{1,0:T(8,128)S(1)}, f32[144,128]{1,0:T(8,128)S(1)}, u32[]{:S(2)}, u32[]{:S(2)}) collective-permute-start(f32[144,128]{1,0:T(8,128)S(1)} %get-tuple-element.29.sent_b), channel_id=1, source_target_pairs={{0,1},{2,3},{4,5},{6,7},{8,9},{10,11},{12,13},{14,15},{1,0},{3,2},... | collective-permute-start | bytes 221192 | tf_op jit(solution)/shard_map/ppermute | solution.py:602
  8.9 1.5 %shard_map.51 = (f32[16,8,128]{2,1,0:T(8,128)S(1)}, f32[2,16,128]{2,1,0:T(8,128)S(1)}, f32[4,8,128]{2,1,0:T(8,128)S(1)}, f32[256,128]{1,0:T(8,128)S(1)}) custom-call(f32[3,16,8,128]{3,2,1,0:T(8,128)S(1)} %get-tuple-element.24.displacement), custom_call_target="tpu_custom_call" | custom-call | flops 4000000 | bytes 1000000 | tf_op jit(solution)/shard_map/pallas_call | solution.py:587
  10.5 0.0 collective-permute-done.received_a
  10.5 0.2 collective-permute-done.1.received_b
  10.7 5.3 %collective-permute-start.2 = (f32[104,128]{1,0:T(8,128)S(1)}, f32[104,128]{1,0:T(8,128)S(1)}, u32[]{:S(2)}, u32[]{:S(2)}) collective-permute-start(f32[104,128]{1,0:T(8,128)S(1)} %get-tuple-element.33), channel_id=1, source_target_pairs={{16,32},{48,64},{80,96},{112,128},{144,160},{176,192},{208,224},{2... | collective-permute-start | bytes 159752 | tf_op jit(solution)/shard_map/ppermute | solution.py:602
  16.0 2.1 %collective-permute-start.3 = (f32[104,128]{1,0:T(8,128)S(1)}, f32[104,128]{1,0:T(8,128)S(1)}, u32[]{:S(2)}, u32[]{:S(2)}) collective-permute-start(f32[104,128]{1,0:T(8,128)S(1)} %get-tuple-element.34), channel_id=1, source_target_pairs={{0,16},{32,48},{64,80},{96,112},{128,144},{160,176},{192,208},{224... | collective-permute-start | bytes 159752 | tf_op jit(solution)/shard_map/ppermute | solution.py:602
  18.1 3.2 %shard_map.53 = (f32[16,24,128]{2,1,0:T(8,128)S(1)}, f32[16,8,128]{2,1,0:T(8,128)S(1)}, f32[16,8,128]{2,1,0:T(8,128)S(1)}, f32[16,8,128]{2,1,0:T(8,128)S(1)}, f3...) custom-call(f32[256,128]{1,0:T(8,128)S(1)} %get-tuple-element.25.factors, f32[16,8,128]{2,1,0:T(8,128)S(1)} %get-tuple-element.26.density, ...), custom_call_target="tpu_custom_call" | custom-call | flops 20000000 | bytes 5000000 | tf_op jit(solution)/shard_map/pallas_call | solution.py:587
  21.3 0.0 collective-permute-done.2.received_a
  21.3 0.0 collective-permute-done.3.received_b
  21.3 1.4 %shard_map.54 = (f32[16,8,128]{2,1,0:T(8,128)S(1)}, f32[4,8,128]{2,1,0:T(8,128)S(1)}, f32[16,2,128]{2,1,0:T(2,128)S(1)}) custom-call(f32[256,128]{1,0:T(8,128)S(1)} %get-tuple-element.25.factors, f32[16,8,128]{2,1,0:T(8,128)S(1)} %get-tuple-element.26.density, f32[3,16,8,128]{3,2,1,0:T(8,128)S(1)} %get-tuple-element.24.displacement, ...), custom_call_target="tpu_custom_call" | custom-call | flops 12000000 | bytes 3000000 | tf_op jit(solution)/shard_map/pallas_call | solution.py:587
  22.7 11.2 %all_to_all.10.received = f32[16,2,128]{2,1,0:T(2,128)S(1)} all-to-all(f32[16,2,128]{2,1,0:T(2,128)S(1)} %get-tuple-element.42), channel_id=1, replica_groups={{0,1,2,3,4,5,6,7,16,17,18,19,20,21,22,23},{8,9,10,11,12,13,14,15,24,25,..., dimensions={0} | all-to-all | bytes 32768 | tf_op jit(solution)/shard_map/all_to_all | solution.py:703
  33.9 28.6 %all_to_all.11.received = f32[32,2,128]{2,1,0:T(2,128)S(1)} all-to-all(f32[32,2,128]{2,1,0:T(2,128)S(1)} %shard_map.55), channel_id=1, replica_groups={{0,12,32,44,64,76,96,108,128,140,160,172,192,204,224,236,256,268,288,30..., dimensions={0} | all-to-all | bytes 65536 | tf_op jit(solution)/shard_map/all_to_all | solution.py:710
  62.5 0.8 %shard_map.56 = (f32[16,8,128]{2,1,0:T(8,128)}, f32[16,8,128]{2,1,0:T(8,128)}) custom-call(f32[32,2,128]{2,1,0:T(2,128)S(1)} %all_to_all.11.received, f32[16,8,128]{2,1,0:T(8,128)S(1)} %get-tuple-element.43.scaled, f32[4,8,128]{2,1,0:T(8,128)S(1)} %get-tuple-element.44.scaled_edge, f32[16,8,128]{2,1,0:T(8,128)S(1)} %get-tuple-element.39.lower, ...), custom_call_target="tpu_custom_call" | custom-call | flops 2000000 | bytes 500000 | tf_op jit(solution)/shard_map/pallas_call | solution.py:587
  (2 shorter events, 0.1 us)
Async XLA Ops:
  1.7 8.8 %collective-permute-start = (f32[144,128]{1,0:T(8,128)S(1)}, f32[144,128]{1,0:T(8,128)S(1)}, u32[]{:S(2)}, u32[]{:S(2)}) collective-permute-start(f32[144,128]{1,0:T(8,128)S(1)} %get-tuple-element.28.sent_a), channel_id=1, source_target_pairs={{1,2},{3,4},{5,6},{7,8},{9,10},{11,12},{13,14},{2,1},{4,3},{6,5},{... | collective-permute-start | bytes 221192 | tf_op jit(solution)/shard_map/ppermute | solution.py:602
  2.4 8.3 %collective-permute-start.1 = (f32[144,128]{1,0:T(8,128)S(1)}, f32[144,128]{1,0:T(8,128)S(1)}, u32[]{:S(2)}, u32[]{:S(2)}) collective-permute-start(f32[144,128]{1,0:T(8,128)S(1)} %get-tuple-element.29.sent_b), channel_id=1, source_target_pairs={{0,1},{2,3},{4,5},{6,7},{8,9},{10,11},{12,13},{14,15},{1,0},{3,2},... | collective-permute-start | bytes 221192 | tf_op jit(solution)/shard_map/ppermute | solution.py:602
  10.7 10.6 %collective-permute-start.2 = (f32[104,128]{1,0:T(8,128)S(1)}, f32[104,128]{1,0:T(8,128)S(1)}, u32[]{:S(2)}, u32[]{:S(2)}) collective-permute-start(f32[104,128]{1,0:T(8,128)S(1)} %get-tuple-element.33), channel_id=1, source_target_pairs={{16,32},{48,64},{80,96},{112,128},{144,160},{176,192},{208,224},{2... | collective-permute-start | bytes 159752 | tf_op jit(solution)/shard_map/ppermute | solution.py:602
  16.0 5.4 %collective-permute-start.3 = (f32[104,128]{1,0:T(8,128)S(1)}, f32[104,128]{1,0:T(8,128)S(1)}, u32[]{:S(2)}, u32[]{:S(2)}) collective-permute-start(f32[104,128]{1,0:T(8,128)S(1)} %get-tuple-element.34), channel_id=1, source_target_pairs={{0,16},{32,48},{64,80},{96,112},{128,144},{160,176},{192,208},{224... | collective-permute-start | bytes 159752 | tf_op jit(solution)/shard_map/ppermute | solution.py:602

commit v7 on v6

--- a/solution.py
+++ b/solution.py
@@ -34,8 +34,52 @@
     return lax.rem(lax.axis_index(axis), 2) == 1
 
 
+def y_rows(density, displacement, passive, out, low):
+    end = NYL - 1
+    for row in (0, 1):
+        out[pl.ds(row * NXL, NXL), :] = density[:, row if low else end - 1 + row, :]
+    for c in range(3):
+        if low:
+            for row in (0, 1):
+                out[pl.ds((2 + 2 * c + row) * NXL, NXL), :] = displacement[c, :, row, :]
+        else:
+            out[pl.ds((2 + c) * NXL, NXL), :] = displacement[c, :, end, :]
+    out[pl.ds((8 if low else 5) * NXL, NXL), :] = passive[:, 0 if low else end, :].astype(
+        jnp.float32
+    )
+    if not low:
+        out[pl.ds(6 * NXL, 3 * NXL), :] = jnp.zeros((3 * NXL, NZ), jnp.float32)
+
+
+def x_planes(density, displacement, passive, y_high, y_low, out, low):
+    first = 0 if low else NXL - 2
+    for k in (0, 1):
+        out[pl.ds(8 * k, 8), :] = density[first + k]
+    for c in range(3):
+        if low:
+            for k in (0, 1):
+                out[pl.ds(8 * (2 + 2 * c + k), 8), :] = displacement[c, k]
+        else:
+            out[pl.ds(8 * (2 + c), 8), :] = displacement[c, NXL - 1]
+    out[pl.ds(64 if low else 40, 8), :] = passive[0 if low else NXL - 1].astype(jnp.float32)
+    base = 72 if low else 48
+    for kind in range(9):
+        out[pl.ds(base + 2 * kind, 2), :] = y_high[pl.ds(NXL * kind + first, 2), :]
+    for kind in range(6):
+        out[pl.ds(base + 18 + 2 * kind, 2), :] = y_low[pl.ds(NXL * kind + first, 2), :]
+    out[pl.ds(base + 30, 2), :] = jnp.zeros((2, NZ), jnp.float32)
+    if not low:
+        out[pl.ds(80, 24), :] = jnp.zeros((24, NZ), jnp.float32)
+
+
+def by_parity(axis, fill, low_if_odd):
+    odd = is_odd(axis)
+    pl.when(odd)(lambda: fill(low_if_odd))
+    pl.when(jnp.logical_not(odd))(lambda: fill(not low_if_odd))
+
+
 def pack_y(
-    density_far, displacement_far, passive_far, density, displacement, passive, send_a, send_b, sems
+    density_far, displacement_far, passive_far, density, displacement, passive, send_a, sems
 ):
     copies = [
         pltpu.make_async_copy(far, local, sems.at[i])
@@ -51,54 +95,24 @@
         copy.start()
     for copy in copies:
         copy.wait()
-
-    def fill(to_low, to_high):
-        for row in (0, 1):
-            to_low[pl.ds(row * NXL, NXL), :] = density[:, row, :]
-            to_high[pl.ds(row * NXL, NXL), :] = density[:, NYL - 2 + row, :]
-        for c in range(3):
-            for row in (0, 1):
-                to_low[pl.ds((2 + 2 * c + row) * NXL, NXL), :] = displacement[c, :, row, :]
-            to_high[pl.ds((2 + c) * NXL, NXL), :] = displacement[c, :, NYL - 1, :]
-        to_low[pl.ds(8 * NXL, NXL), :] = passive[:, 0, :].astype(jnp.float32)
-        to_high[pl.ds(5 * NXL, NXL), :] = passive[:, NYL - 1, :].astype(jnp.float32)
-        to_high[pl.ds(6 * NXL, 3 * NXL), :] = jnp.zeros((3 * NXL, NZ), jnp.float32)
-
-    odd = is_odd("gy")
-    pl.when(odd)(lambda: fill(send_b, send_a))
-    pl.when(jnp.logical_not(odd))(lambda: fill(send_a, send_b))
+    by_parity(
+        "gy", lambda low: y_rows(density, displacement, passive, send_a, low), False
+    )
 
 
 def pack_x(
-    density, displacement, passive, received_a, received_b, after, y_high, y_low, send_a, send_b
+    density, displacement, passive, received_a, received_b, after, y_high, y_low, send_a
 ):
     del after
     odd = is_odd("gy")
     y_high[...] = jnp.where(odd, received_a[...], received_b[...])
-    low = pl.ds(0, 6 * NXL)
-    y_low[...] = jnp.where(odd, received_b[low, :], received_a[low, :])
-
-    def fill(to_low, to_high):
-        for k in (0, 1):
-            to_low[pl.ds(8 * k, 8), :] = density[k]
-            to_high[pl.ds(8 * k, 8), :] = density[NXL - 2 + k]
-        for c in range(3):
-            for k in (0, 1):
-                to_low[pl.ds(8 * (2 + 2 * c + k), 8), :] = displacement[c, k]
-            to_high[pl.ds(8 * (2 + c), 8), :] = displacement[c, NXL - 1]
-        to_low[pl.ds(64, 8), :] = passive[0].astype(jnp.float32)
-        to_high[pl.ds(40, 8), :] = passive[NXL - 1].astype(jnp.float32)
-        for base, first, out in ((72, 0, to_low), (48, NXL - 2, to_high)):
-            for kind in range(9):
-                out[pl.ds(base + 2 * kind, 2), :] = y_high[pl.ds(NXL * kind + first, 2), :]
-            for kind in range(6):
-                out[pl.ds(base + 18 + 2 * kind, 2), :] = y_low[pl.ds(NXL * kind + first, 2), :]
-            out[pl.ds(base + 30, 2), :] = jnp.zeros((2, NZ), jnp.float32)
-        to_high[pl.ds(80, 24), :] = jnp.zeros((24, NZ), jnp.float32)
-
-    odd_x = is_odd("gx")
-    pl.when(odd_x)(lambda: fill(send_b, send_a))
-    pl.when(jnp.logical_not(odd_x))(lambda: fill(send_a, send_b))
+    low_rows = pl.ds(0, 6 * NXL)
+    y_low[...] = jnp.where(odd, received_b[low_rows, :], received_a[low_rows, :])
+    by_parity(
+        "gx",
+        lambda low: x_planes(density, displacement, passive, y_high, y_low, send_a, low),
+        False,
+    )
 
 
 def lane_ends(height):
@@ -171,10 +185,11 @@
     )
 
 
-def interior_energy(displacement, energy, inverse, weights, factors):
-    start_y = lax.axis_index("gy") * NYL
-    total_y = lax.axis_size("gy") * NYL
-    first, last = lane_ends(NYL)
+def interior_energy(density, displacement, passive, energy, send_b):
+    by_parity(
+        "gy", lambda low: y_rows(density, displacement, passive, send_b, low), True
+    )
+    _, last = lane_ends(NYL)
 
     def nodes(plane):
         here = []
@@ -190,6 +205,13 @@
 
     lax.fori_loop(0, NXL - 1, plane_energy, nodes(0))
     energy[NXL - 1] = jnp.zeros((NYL, NZ), jnp.float32)
+
+
+def tables(after, inverse, weights, factors):
+    del after
+    start_y = lax.axis_index("gy") * NYL
+    total_y = lax.axis_size("gy") * NYL
+    first, last = lane_ends(NYL)
     trial = lax.broadcasted_iota(jnp.int32, (SLOTS, NZ), 0).astype(jnp.float32)
     factors[...] = jnp.exp(-0.5 * (-BRACKET + STEP * (trial + 1.0)))
 
@@ -254,8 +276,8 @@
 
 
 def middle(
-    factors,
     density,
+    displacement,
     passive,
     own_energy,
     inverse,
@@ -264,15 +286,20 @@
     y_low,
     sent_a,
     sent_b,
+    send_b,
     spread,
     sensitivity,
     scaled,
     lower,
     upper,
-    partial,
     dens,
     energy,
 ):
+    by_parity(
+        "gx",
+        lambda low: x_planes(density, displacement, passive, y_high, y_low, send_b, low),
+        True,
+    )
     def rows(ref, kind):
         return ref[pl.ds(kind * NXL, NXL), :]
 
@@ -356,6 +383,9 @@
     fixed = jnp.where(kind == 1, 1.0, 0.0)
     lower[...] = jnp.where(kind == 0, jnp.maximum(here - MOVE_LIMIT, 0.0), fixed)
     upper[...] = jnp.where(kind == 0, jnp.minimum(here + MOVE_LIMIT, 1.0), fixed)
+
+
+def middle_volumes(factors, scaled, lower, upper, partial):
     add_volumes(
         [(x, x) for x in range(2, NXL - 2)], factors, scaled, lower, upper, None, partial
     )
@@ -618,14 +648,13 @@
     count_x, count_y = lax.axis_size("gx"), lax.axis_size("gy")
     assert density.shape == (NXL, NYL, NZ)
     block = (NXL, NYL, NZ)
-    density, displacement, passive, sent_a, sent_b = call(
+    density, displacement, passive, sent_a = call(
         pack_y,
         (
             near(*block),
             near(3, *block),
             near(*block, dtype=jnp.int32),
             near(9 * NXL, NZ),
-            near(9 * NXL, NZ),
         ),
         (far(density), far(displacement), far(passive)),
         [pltpu.SemaphoreType.DMA((3,))],
@@ -633,27 +662,32 @@
         cost=1000,
     )
     received_a = held(swapped(sent_a, "gy", 1))
+    own_energy, sent_b = call(
+        interior_energy,
+        (near(*block), near(9 * NXL, NZ)),
+        (density, displacement, passive),
+        cost=1000,
+    )
     received_b = held(swapped(sent_b, "gy", 0))
-    own_energy, inverse, weights, factors = call(
-        interior_energy,
-        (near(*block), near(2, 16, NZ), near(4, NYL, NZ), near(SLOTS, NZ)),
-        (displacement,),
+    inverse, weights, factors = call(
+        tables,
+        (near(2, 16, NZ), near(4, NYL, NZ), near(SLOTS, NZ)),
+        (own_energy,),
         cost=1000,
     )
-    y_high, y_low, to_a, to_b = call(
+    y_high, y_low, to_a = call(
         pack_x,
-        (near(9 * NXL, NZ), near(6 * NXL, NZ), near(104, NZ), near(104, NZ)),
+        (near(9 * NXL, NZ), near(6 * NXL, NZ), near(104, NZ)),
         (density, displacement, passive, received_a, received_b, weights),
         cost=500,
     )
     received_a = held(swapped(to_a, "gx", 1))
-    received_b = held(swapped(to_b, "gx", 0))
-    spread, sensitivity, scaled, lower, upper, partial = call(
+    to_b, spread, sensitivity, scaled, lower, upper = call(
         middle,
-        (near(NXL, 24, NZ),) + (near(*block),) * 4 + (near(8 * SLOTS, NZ),),
+        (near(104, NZ), near(NXL, 24, NZ)) + (near(*block),) * 4,
         (
-            factors,
             density,
+            displacement,
             passive,
             own_energy,
             inverse,
@@ -664,7 +698,11 @@
             sent_b,
         ),
         [pltpu.VMEM((NXL, 24, NZ), jnp.float32), pltpu.VMEM(block, jnp.float32)],
-        cost=5000,
+        cost=3000,
+    )
+    received_b = held(swapped(to_b, "gx", 0))
+    partial = call(
+        middle_volumes, near(8 * SLOTS, NZ), (factors, scaled, lower, upper), cost=3000
     )
     across, along = reduction_groups(count_x, count_y)
     first_group, second_group = len(across[0]), len(along[0])

time: 63.6 us -> 65.1 us (1.024)
  waiting for transfers between devices: 0.18 us -> 1.59 us
    ppermute x4, waiting for transfers between devices: 0.18 us -> 1.59 us  [swapped(): return lax.ppermute(block, axis, pairs + [(j, i) for i, j in pairs])]
    pallas_call x7 -> x9, Pallas kernels: 8.08 us -> 8.15 us  [call(): pl.pallas_call(kernel, out_shape=outputs, in_specs=specs or [VMEM] * len(...]
where the time goes in v7:
time: 65.1 us; the launch traced here: 64.8 us
  blocking collectives  39.8 us (61%)
  starting transfers between devices  14.6 us (22%)
  Pallas kernels  8.15 us (13%)
  waiting for transfers between devices  1.59 us (2%)
  between operations  0.73 us (1%)
    all_to_all x1, blocking collectives, per_device(): lax.all_to_all(volumes, ('gx', 'gy'), 0, 0, axis_index_groups=along)  28.6 us
    ppermute x4, starting transfers between devices, swapped(): return lax.ppermute(block, axis, pairs + [(j, i) for i, j in pairs])  14.6 us
    all_to_all x1, blocking collectives, per_device(): lax.all_to_all(volumes, ('gx', 'gy'), 0, 0, axis_index_groups=across)  11.2 us
    pallas_call x9, Pallas kernels, call(): pl.pallas_call(kernel, out_shape=outputs, in_specs=specs or [VMEM] * len(...  8.15 us
    ppermute x4, waiting for transfers between devices, swapped(): return lax.ppermute(block, axis, pairs + [(j, i) for i, j in pairs])  1.59 us
  transfers between devices with their start and end apart: 4, of which 1 were waited for; matrix products, arithmetic and copies ran while one was open for 0% of the time, Pallas kernels for 8%

profile of v7, /device:TPU:1, one launch (start us, length us, event | category | flops | bytes accessed | tf_op | source)
XLA Modules:
  0.0 64.8 jit_solution(7106380061705346162)
XLA Ops:
  0.6 1.0 %shard_map.50 = (f32[16,8,128]{2,1,0:T(8,128)S(1)}, f32[3,16,8,128]{3,2,1,0:T(8,128)S(1)}, s32[16,8,128]{2,1,0:T(8,128)S(1)}, f32[144,128]{1,0:T(8,128)S(1)}) custom-call(f32[16,8,128]{2,1,0:T(8,128)} %density_far.1, f32[3,16,8,128]{3,2,1,0:T(8,128)} %displacement_far.1, s32[16,8,128]{2,1,0:T(8,128)} %passive_far.1), custom_call_target="tpu_custom_call" | custom-call | flops 4000000 | bytes 1000000 | tf_op jit(solution)/shard_map/pallas_call | solution.py:617
  1.7 0.7 %collective-permute-start = (f32[144,128]{1,0:T(8,128)S(1)}, f32[144,128]{1,0:T(8,128)S(1)}, u32[]{:S(2)}, u32[]{:S(2)}) collective-permute-start(f32[144,128]{1,0:T(8,128)S(1)} %get-tuple-element.28.sent_a), channel_id=1, source_target_pairs={{1,2},{3,4},{5,6},{7,8},{9,10},{11,12},{13,14},{2,1},{4,3},{6,5},{... | collective-permute-start | bytes 221192 | tf_op jit(solution)/shard_map/ppermute | solution.py:632
  2.3 1.5 %shard_map.51 = (f32[16,8,128]{2,1,0:T(8,128)S(1)}, f32[144,128]{1,0:T(8,128)S(1)}) custom-call(f32[16,8,128]{2,1,0:T(8,128)S(1)} %get-tuple-element.23.density, f32[3,16,8,128]{3,2,1,0:T(8,128)S(1)} %get-tuple-element.24.displacement, s32[16,8,128]{2,1,0:T(8,128)S(1)} %get-tuple-element.25.passive), custom_call_target="tpu_custom_call" | custom-call | flops 4000000 | bytes 1000000 | tf_op jit(solution)/shard_map/pallas_call | solution.py:617
  3.8 6.6 %collective-permute-start.1 = (f32[144,128]{1,0:T(8,128)S(1)}, f32[144,128]{1,0:T(8,128)S(1)}, u32[]{:S(2)}, u32[]{:S(2)}) collective-permute-start(f32[144,128]{1,0:T(8,128)S(1)} %get-tuple-element.29.sent_b), channel_id=1, source_target_pairs={{0,1},{2,3},{4,5},{6,7},{8,9},{10,11},{12,13},{14,15},{1,0},{3,2},... | collective-permute-start | bytes 221192 | tf_op jit(solution)/shard_map/ppermute | solution.py:632
  10.4 0.1 shard_map.52
  10.5 0.0 collective-permute-done.received_a
  10.6 1.6 %collective-permute-done.1.received_b = f32[144,128]{1,0:T(8,128)S(1)} collective-permute-done((f32[144,128]{1,0:T(8,128)S(1)}, f32[144,128]{1,0:T(8,128)S(1)}, u32[]{:S(2)}, u32[]{:S(2)}) %collective-permute-start.1) | collective-permute-done | bytes 73760 | tf_op jit(solution)/shard_map/ppermute | solution.py:632
  12.2 5.3 %collective-permute-start.2 = (f32[104,128]{1,0:T(8,128)S(1)}, f32[104,128]{1,0:T(8,128)S(1)}, u32[]{:S(2)}, u32[]{:S(2)}) collective-permute-start(f32[104,128]{1,0:T(8,128)S(1)} %get-tuple-element.33), channel_id=1, source_target_pairs={{16,32},{48,64},{80,96},{112,128},{144,160},{176,192},{208,224},{2... | collective-permute-start | bytes 159752 | tf_op jit(solution)/shard_map/ppermute | solution.py:632
  17.4 1.5 %shard_map.54 = (f32[104,128]{1,0:T(8,128)S(1)}, f32[16,24,128]{2,1,0:T(8,128)S(1)}, f32[16,8,128]{2,1,0:T(8,128)S(1)}, f32[16,8,128]{2,1,0:T(8,128)S(1)}, f32[1...) custom-call(f32[16,8,128]{2,1,0:T(8,128)S(1)} %get-tuple-element.23.density, ...), custom_call_target="tpu_custom_call" | custom-call | flops 12000000 | bytes 3000000 | tf_op jit(solution)/shard_map/pallas_call | solution.py:617
  18.9 2.1 %collective-permute-start.3 = (f32[104,128]{1,0:T(8,128)S(1)}, f32[104,128]{1,0:T(8,128)S(1)}, u32[]{:S(2)}, u32[]{:S(2)}) collective-permute-start(f32[104,128]{1,0:T(8,128)S(1)} %get-tuple-element.35), channel_id=1, source_target_pairs={{0,16},{32,48},{64,80},{96,112},{128,144},{160,176},{192,208},{224... | collective-permute-start | bytes 159752 | tf_op jit(solution)/shard_map/ppermute | solution.py:632
  21.0 1.8 %shard_map.55.start = f32[2048,128]{1,0:T(8,128)S(1)} custom-call(f32[256,128]{1,0:T(8,128)S(1)} %get-tuple-element.27.factors, f32[16,8,128]{2,1,0:T(8,128)S(1)} %get-tuple-element.40.scaled, f32[16,8,128]{2,1,0:T(8,128)S(1)} %get-tuple-element.38.lower, f32[16,8,128]{2,1,0:T(8,128)S(1)} %get-tuple-element.39.upper), custom_call_target="tpu_custom_call" | custom-call | flops 12000000 | bytes 3000000 | tf_op jit(solution)/shard_map/pallas_call | solution.py:617
  22.8 0.0 collective-permute-done.2.received_a
  22.8 0.0 collective-permute-done.3.received_b
  22.8 1.4 %shard_map.56 = (f32[16,8,128]{2,1,0:T(8,128)S(1)}, f32[4,8,128]{2,1,0:T(8,128)S(1)}, f32[16,2,128]{2,1,0:T(2,128)S(1)}) custom-call(f32[256,128]{1,0:T(8,128)S(1)} %get-tuple-element.27.factors, f32[16,8,128]{2,1,0:T(8,128)S(1)} %get-tuple-element.23.density, f32[3,16,8,128]{3,2,1,0:T(8,128)S(1)} %get-tuple-element.24.displacement, ...), custom_call_target="tpu_custom_call" | custom-call | flops 12000000 | bytes 3000000 | tf_op jit(solution)/shard_map/pallas_call | solution.py:617
  24.2 11.2 %all_to_all.10.received = f32[16,2,128]{2,1,0:T(2,128)S(1)} all-to-all(f32[16,2,128]{2,1,0:T(2,128)S(1)} %get-tuple-element.41), channel_id=1, replica_groups={{0,1,2,3,4,5,6,7,16,17,18,19,20,21,22,23},{8,9,10,11,12,13,14,15,24,25,..., dimensions={0} | all-to-all | bytes 32768 | tf_op jit(solution)/shard_map/all_to_all | solution.py:741
  35.4 28.6 %all_to_all.11.received = f32[32,2,128]{2,1,0:T(2,128)S(1)} all-to-all(f32[32,2,128]{2,1,0:T(2,128)S(1)} %shard_map.57), channel_id=1, replica_groups={{0,12,32,44,64,76,96,108,128,140,160,172,192,204,224,236,256,268,288,30..., dimensions={0} | all-to-all | bytes 65536 | tf_op jit(solution)/shard_map/all_to_all | solution.py:748
  64.0 0.8 %shard_map.58 = (f32[16,8,128]{2,1,0:T(8,128)}, f32[16,8,128]{2,1,0:T(8,128)}) custom-call(f32[32,2,128]{2,1,0:T(2,128)S(1)} %all_to_all.11.received, f32[16,8,128]{2,1,0:T(8,128)S(1)} %get-tuple-element.40.scaled, f32[4,8,128]{2,1,0:T(8,128)S(1)} %get-tuple-element.42.scaled_edge, f32[16,8,128]{2,1,0:T(8,128)S(1)} %get-tuple-element.38.lower, ...), custom_call_target="tpu_custom_call" | custom-call | flops 2000000 | bytes 500000 | tf_op jit(solution)/shard_map/pallas_call | solution.py:617
  (2 shorter events, 0.1 us)
Async XLA Ops:
  1.7 8.9 %collective-permute-start = (f32[144,128]{1,0:T(8,128)S(1)}, f32[144,128]{1,0:T(8,128)S(1)}, u32[]{:S(2)}, u32[]{:S(2)}) collective-permute-start(f32[144,128]{1,0:T(8,128)S(1)} %get-tuple-element.28.sent_a), channel_id=1, source_target_pairs={{1,2},{3,4},{5,6},{7,8},{9,10},{11,12},{13,14},{2,1},{4,3},{6,5},{... | collective-permute-start | bytes 221192 | tf_op jit(solution)/shard_map/ppermute | solution.py:632
  3.8 8.3 %collective-permute-start.1 = (f32[144,128]{1,0:T(8,128)S(1)}, f32[144,128]{1,0:T(8,128)S(1)}, u32[]{:S(2)}, u32[]{:S(2)}) collective-permute-start(f32[144,128]{1,0:T(8,128)S(1)} %get-tuple-element.29.sent_b), channel_id=1, source_target_pairs={{0,1},{2,3},{4,5},{6,7},{8,9},{10,11},{12,13},{14,15},{1,0},{3,2},... | collective-permute-start | bytes 221192 | tf_op jit(solution)/shard_map/ppermute | solution.py:632
  12.2 10.6 %collective-permute-start.2 = (f32[104,128]{1,0:T(8,128)S(1)}, f32[104,128]{1,0:T(8,128)S(1)}, u32[]{:S(2)}, u32[]{:S(2)}) collective-permute-start(f32[104,128]{1,0:T(8,128)S(1)} %get-tuple-element.33), channel_id=1, source_target_pairs={{16,32},{48,64},{80,96},{112,128},{144,160},{176,192},{208,224},{2... | collective-permute-start | bytes 159752 | tf_op jit(solution)/shard_map/ppermute | solution.py:632
  18.9 3.9 %collective-permute-start.3 = (f32[104,128]{1,0:T(8,128)S(1)}, f32[104,128]{1,0:T(8,128)S(1)}, u32[]{:S(2)}, u32[]{:S(2)}) collective-permute-start(f32[104,128]{1,0:T(8,128)S(1)} %get-tuple-element.35), channel_id=1, source_target_pairs={{0,16},{32,48},{64,80},{96,112},{128,144},{160,176},{192,208},{224... | collective-permute-start | bytes 159752 | tf_op jit(solution)/shard_map/ppermute | solution.py:632

commit v8 on v6

--- a/solution.py
+++ b/solution.py
@@ -188,7 +188,9 @@
         energy[x] = element_energy(before, after)
         return after
 
-    lax.fori_loop(0, NXL - 1, plane_energy, nodes(0))
+    before = nodes(0)
+    for x in range(NXL - 1):
+        before = plane_energy(x, before)
     energy[NXL - 1] = jnp.zeros((NYL, NZ), jnp.float32)
     trial = lax.broadcasted_iota(jnp.int32, (SLOTS, NZ), 0).astype(jnp.float32)
     factors[...] = jnp.exp(-0.5 * (-BRACKET + STEP * (trial + 1.0)))
@@ -332,9 +334,9 @@
         return side_here, side_after, rest_after
 
     side_0, _ = around(dens, 0, first, last)
-    lax.fori_loop(
-        1, NXL - 1, spread_plane, (side_0,) + around(dens, 1, first, last), unroll=2
-    )
+    carry = (side_0,) + around(dens, 1, first, last)
+    for x in range(1, NXL - 1):
+        carry = spread_plane(x, carry)
 
     scale = 1.0 / (weights[1] + 2.0 * weights[0])
 
@@ -347,9 +349,9 @@
         return side_here, side_after, rest_after
 
     side_1, _ = around(spread, 1, first, last)
-    lax.fori_loop(
-        2, NXL - 2, out_plane, (side_1,) + around(spread, 2, first, last), unroll=2
-    )
+    carry = (side_1,) + around(spread, 2, first, last)
+    for x in range(2, NXL - 2):
+        carry = out_plane(x, carry)
 
     here = density[...]
     kind = passive[...]
@@ -609,8 +611,8 @@
         for gy in range(count_y):
             device = gx * count_y + gy
             x, y = gy // SIDE, gy % SIDE
-            across.setdefault((gx // 2, x // 2), []).append(device)
-            along.setdefault((gx % 2, y, min(x, chips_x - 1 - x)), []).append(device)
+            across.setdefault((gx // 2, min(x, chips_x - 1 - x)), []).append(device)
+            along.setdefault((gx % 2, y, x // 2), []).append(device)
     return list(across.values()), list(along.values())
 
 

time: 63.6 us -> 62.5 us (0.983)
  Pallas kernels: 8.08 us -> 5.81 us
  waiting for transfers between devices: 0.18 us -> 1.4 us
    pallas_call x7, Pallas kernels: 8.08 us -> 5.81 us  [call(): pl.pallas_call(kernel, out_shape=outputs, in_specs=specs or [VMEM] * len(...]
    all_to_all x1, blocking collectives: 28.6 us -> 26.4 us  [per_device(): lax.all_to_all(volumes, ('gx', 'gy'), 0, 0, axis_index_groups=along)]
    all_to_all x1, blocking collectives: 11.2 us -> 13.3 us  [per_device(): lax.all_to_all(volumes, ('gx', 'gy'), 0, 0, axis_index_groups=across)]
    ppermute x4, waiting for transfers between devices: 0.18 us -> 1.4 us  [swapped(): return lax.ppermute(block, axis, pairs + [(j, i) for i, j in pairs])]
  transfers between devices with their start and end apart: 4 -> 4, of which waited for: 1 -> 1; matrix products, arithmetic and copies ran while one was open for 0% -> 0% of each run, Pallas kernels for 8% -> 4%
where the time goes in v8:
time: 62.5 us; the launch traced here: 62.2 us
  blocking collectives  39.7 us (64%)
  starting transfers between devices  14.6 us (23%)
  Pallas kernels  5.81 us (9%)
  waiting for transfers between devices  1.4 us (2%)
  between operations  0.72 us (1%)
    all_to_all x1, blocking collectives, per_device(): lax.all_to_all(volumes, ('gx', 'gy'), 0, 0, axis_index_groups=along)  26.4 us
    ppermute x4, starting transfers between devices, swapped(): return lax.ppermute(block, axis, pairs + [(j, i) for i, j in pairs])  14.6 us
    all_to_all x1, blocking collectives, per_device(): lax.all_to_all(volumes, ('gx', 'gy'), 0, 0, axis_index_groups=across)  13.3 us
    pallas_call x7, Pallas kernels, call(): pl.pallas_call(kernel, out_shape=outputs, in_specs=specs or [VMEM] * len(...  5.81 us
    ppermute x4, waiting for transfers between devices, swapped(): return lax.ppermute(block, axis, pairs + [(j, i) for i, j in pairs])  1.4 us
  transfers between devices with their start and end apart: 4, of which 1 were waited for; matrix products, arithmetic and copies ran while one was open for 0% of the time, Pallas kernels for 4%

profile of v8, /device:TPU:1, one launch (start us, length us, event | category | flops | bytes accessed | tf_op | source)
XLA Modules:
  0.0 62.2 jit_solution(2293574461578737761)
XLA Ops:
  0.6 1.1 %shard_map.50 = (f32[16,8,128]{2,1,0:T(8,128)S(1)}, f32[3,16,8,128]{3,2,1,0:T(8,128)S(1)}, s32[16,8,128]{2,1,0:T(8,128)S(1)}, f32[144,128]{1,0:T(8,128)S(1)}, f32[144,128]{1,0:T(8,128)S(1)}) custom-call(f32[16,8,128]{2,1,0:T(8,128)} %density_far.1, f32[3,16,8,128]{3,2,1,0:T(8,128)} %displacement_far.1, s32[16,8,128]{2,1,0:T(8,128)} %passive_far.1), custom_call_target="tpu_custom_call" | custom-call | flops 4000000 | bytes 1000000 | tf_op jit(solution)/shard_map/pallas_call | solution.py:589
  1.7 0.7 %collective-permute-start = (f32[144,128]{1,0:T(8,128)S(1)}, f32[144,128]{1,0:T(8,128)S(1)}, u32[]{:S(2)}, u32[]{:S(2)}) collective-permute-start(f32[144,128]{1,0:T(8,128)S(1)} %get-tuple-element.28.sent_a), channel_id=1, source_target_pairs={{1,2},{3,4},{5,6},{7,8},{9,10},{11,12},{13,14},{2,1},{4,3},{6,5},{... | collective-permute-start | bytes 221192 | tf_op jit(solution)/shard_map/ppermute | solution.py:604
  2.4 6.6 %collective-permute-start.1 = (f32[144,128]{1,0:T(8,128)S(1)}, f32[144,128]{1,0:T(8,128)S(1)}, u32[]{:S(2)}, u32[]{:S(2)}) collective-permute-start(f32[144,128]{1,0:T(8,128)S(1)} %get-tuple-element.29.sent_b), channel_id=1, source_target_pairs={{0,1},{2,3},{4,5},{6,7},{8,9},{10,11},{12,13},{14,15},{1,0},{3,2},... | collective-permute-start | bytes 221192 | tf_op jit(solution)/shard_map/ppermute | solution.py:604
  8.9 0.3 shard_map.51
  9.3 0.0 collective-permute-done.received_a
  9.3 1.4 %collective-permute-done.1.received_b = f32[144,128]{1,0:T(8,128)S(1)} collective-permute-done((f32[144,128]{1,0:T(8,128)S(1)}, f32[144,128]{1,0:T(8,128)S(1)}, u32[]{:S(2)}, u32[]{:S(2)}) %collective-permute-start.1) | collective-permute-done | bytes 73760 | tf_op jit(solution)/shard_map/ppermute | solution.py:604
  10.7 5.3 %collective-permute-start.2 = (f32[104,128]{1,0:T(8,128)S(1)}, f32[104,128]{1,0:T(8,128)S(1)}, u32[]{:S(2)}, u32[]{:S(2)}) collective-permute-start(f32[104,128]{1,0:T(8,128)S(1)} %get-tuple-element.33), channel_id=1, source_target_pairs={{16,32},{48,64},{80,96},{112,128},{144,160},{176,192},{208,224},{2... | collective-permute-start | bytes 159752 | tf_op jit(solution)/shard_map/ppermute | solution.py:604
  16.0 2.1 %collective-permute-start.3 = (f32[104,128]{1,0:T(8,128)S(1)}, f32[104,128]{1,0:T(8,128)S(1)}, u32[]{:S(2)}, u32[]{:S(2)}) collective-permute-start(f32[104,128]{1,0:T(8,128)S(1)} %get-tuple-element.34), channel_id=1, source_target_pairs={{0,16},{32,48},{64,80},{96,112},{128,144},{160,176},{192,208},{224... | collective-permute-start | bytes 159752 | tf_op jit(solution)/shard_map/ppermute | solution.py:604
  18.1 2.2 %shard_map.53 = (f32[16,24,128]{2,1,0:T(8,128)S(1)}, f32[16,8,128]{2,1,0:T(8,128)S(1)}, f32[16,8,128]{2,1,0:T(8,128)S(1)}, f32[16,8,128]{2,1,0:T(8,128)S(1)}, f3...) custom-call(f32[256,128]{1,0:T(8,128)S(1)} %get-tuple-element.25.factors, f32[16,8,128]{2,1,0:T(8,128)S(1)} %get-tuple-element.26.density, ...), custom_call_target="tpu_custom_call" | custom-call | flops 20000000 | bytes 5000000 | tf_op jit(solution)/shard_map/pallas_call | solution.py:589
  20.3 0.0 collective-permute-done.2.received_a
  20.3 0.0 collective-permute-done.3.received_b
  20.3 1.4 %shard_map.54 = (f32[16,8,128]{2,1,0:T(8,128)S(1)}, f32[4,8,128]{2,1,0:T(8,128)S(1)}, f32[16,2,128]{2,1,0:T(2,128)S(1)}) custom-call(f32[256,128]{1,0:T(8,128)S(1)} %get-tuple-element.25.factors, f32[16,8,128]{2,1,0:T(8,128)S(1)} %get-tuple-element.26.density, f32[3,16,8,128]{3,2,1,0:T(8,128)S(1)} %get-tuple-element.24.displacement, ...), custom_call_target="tpu_custom_call" | custom-call | flops 12000000 | bytes 3000000 | tf_op jit(solution)/shard_map/pallas_call | solution.py:589
  21.7 13.3 %all_to_all.10.received = f32[16,2,128]{2,1,0:T(2,128)S(1)} all-to-all(f32[16,2,128]{2,1,0:T(2,128)S(1)} %get-tuple-element.42), channel_id=1, replica_groups={{0,1,2,3,12,13,14,15,16,17,18,19,28,29,30,31},{4,5,6,7,8,9,10,11,20,21,..., dimensions={0} | all-to-all | bytes 32768 | tf_op jit(solution)/shard_map/all_to_all | solution.py:705
  35.0 26.4 %all_to_all.11.received = f32[32,2,128]{2,1,0:T(2,128)S(1)} all-to-all(f32[32,2,128]{2,1,0:T(2,128)S(1)} %shard_map.55), channel_id=1, replica_groups={{0,4,32,36,64,68,96,100,128,132,160,164,192,196,224,228,256,260,288,292..., dimensions={0} | all-to-all | bytes 65536 | tf_op jit(solution)/shard_map/all_to_all | solution.py:712
  61.4 0.8 %shard_map.56 = (f32[16,8,128]{2,1,0:T(8,128)}, f32[16,8,128]{2,1,0:T(8,128)}) custom-call(f32[32,2,128]{2,1,0:T(2,128)S(1)} %all_to_all.11.received, f32[16,8,128]{2,1,0:T(8,128)S(1)} %get-tuple-element.43.scaled, f32[4,8,128]{2,1,0:T(8,128)S(1)} %get-tuple-element.44.scaled_edge, f32[16,8,128]{2,1,0:T(8,128)S(1)} %get-tuple-element.39.lower, ...), custom_call_target="tpu_custom_call" | custom-call | flops 2000000 | bytes 500000 | tf_op jit(solution)/shard_map/pallas_call | solution.py:589
  (2 shorter events, 0.1 us)
Async XLA Ops:
  1.7 7.6 %collective-permute-start = (f32[144,128]{1,0:T(8,128)S(1)}, f32[144,128]{1,0:T(8,128)S(1)}, u32[]{:S(2)}, u32[]{:S(2)}) collective-permute-start(f32[144,128]{1,0:T(8,128)S(1)} %get-tuple-element.28.sent_a), channel_id=1, source_target_pairs={{1,2},{3,4},{5,6},{7,8},{9,10},{11,12},{13,14},{2,1},{4,3},{6,5},{... | collective-permute-start | bytes 221192 | tf_op jit(solution)/shard_map/ppermute | solution.py:604
  2.4 8.3 %collective-permute-start.1 = (f32[144,128]{1,0:T(8,128)S(1)}, f32[144,128]{1,0:T(8,128)S(1)}, u32[]{:S(2)}, u32[]{:S(2)}) collective-permute-start(f32[144,128]{1,0:T(8,128)S(1)} %get-tuple-element.29.sent_b), channel_id=1, source_target_pairs={{0,1},{2,3},{4,5},{6,7},{8,9},{10,11},{12,13},{14,15},{1,0},{3,2},... | collective-permute-start | bytes 221192 | tf_op jit(solution)/shard_map/ppermute | solution.py:604
  10.7 9.6 %collective-permute-start.2 = (f32[104,128]{1,0:T(8,128)S(1)}, f32[104,128]{1,0:T(8,128)S(1)}, u32[]{:S(2)}, u32[]{:S(2)}) collective-permute-start(f32[104,128]{1,0:T(8,128)S(1)} %get-tuple-element.33), channel_id=1, source_target_pairs={{16,32},{48,64},{80,96},{112,128},{144,160},{176,192},{208,224},{2... | collective-permute-start | bytes 159752 | tf_op jit(solution)/shard_map/ppermute | solution.py:604
  16.0 4.3 %collective-permute-start.3 = (f32[104,128]{1,0:T(8,128)S(1)}, f32[104,128]{1,0:T(8,128)S(1)}, u32[]{:S(2)}, u32[]{:S(2)}) collective-permute-start(f32[104,128]{1,0:T(8,128)S(1)} %get-tuple-element.34), channel_id=1, source_target_pairs={{0,16},{32,48},{64,80},{96,112},{128,144},{160,176},{192,208},{224... | collective-permute-start | bytes 159752 | tf_op jit(solution)/shard_map/ppermute | solution.py:604

commit v9 on v8

--- a/solution.py
+++ b/solution.py
@@ -25,6 +25,7 @@
 SLOTS = TRIALS + 1
 STEP = 2.0 * BRACKET / 2 ** BISECT
 GROUP = 16
+PAIRS = NXL // 2 - 2
 SIDE = 4
 
 VMEM = pl.BlockSpec(memory_space=pltpu.VMEM)
@@ -171,7 +172,22 @@
     )
 
 
-def interior_energy(displacement, energy, inverse, weights, factors):
+def interior(
+    density,
+    displacement,
+    passive,
+    energy,
+    inverse,
+    weights,
+    factors,
+    lower,
+    upper,
+    lower_outer,
+    upper_outer,
+    partial,
+    own_spread,
+    inner,
+):
     start_y = lax.axis_index("gy") * NYL
     total_y = lax.axis_size("gy") * NYL
     first, last = lane_ends(NYL)
@@ -217,11 +233,59 @@
         weights[2 * slot] = side
         weights[2 * slot + 1] = rest
 
+    here = density[...]
+    kind = passive[...]
+    fixed = jnp.where(kind == 1, 1.0, 0.0)
+    lower[...] = jnp.where(kind == 0, jnp.maximum(here - MOVE_LIMIT, 0.0), fixed)
+    upper[...] = jnp.where(kind == 0, jnp.minimum(here + MOVE_LIMIT, 1.0), fixed)
+
+    def rolled_terms(f):
+        return filter_terms(pltpu.roll(f, 1, 0), f, pltpu.roll(f, NYL - 1, 0), first, last)
+
+    weight = inverse[0, pl.ds(1, 8), :]
+    before, here = rolled_terms(density[0]), rolled_terms(density[1])
+    for x in range(1, NXL - 1):
+        after = rolled_terms(density[x + 1])
+        own_spread[x] = spread_of(
+            here[1] + before[0] + after[0], weight, passive[x].astype(jnp.float32), energy[x]
+        )
+        before, here = here, after
+    scale = 1.0 / (weights[1] + 2.0 * weights[0])
+    before, here = rolled_terms(own_spread[1]), rolled_terms(own_spread[2])
+    values = []
+    for x in range(2, NXL - 2):
+        after = rolled_terms(own_spread[x + 1])
+        sens = here[1] + before[0] + after[0]
+        values.append(density[x] * jnp.sqrt(-sens * scale))
+        before, here = here, after
+    for p in range(PAIRS):
+        x = 2 + 2 * p
+        inner[0, p] = row_pack(values[2 * p], values[2 * p + 1], True)
+        for i, (limit, outer) in enumerate(((lower, lower_outer), (upper, upper_outer))):
+            inner[1 + i, p] = row_pack(limit[x], limit[x + 1], True)
+            outer[p] = row_pack(limit[x], limit[x + 1], False)
+    add_volumes(
+        [(p, p) for p in range(PAIRS)],
+        factors,
+        inner.at[0],
+        inner.at[1],
+        inner.at[2],
+        None,
+        partial,
+    )
+
 
 def spread_of(filtered, weight, kind, energy):
     physical = filtered * weight
     physical = jnp.where(kind == 1.0, 1.0, jnp.where(kind == 2.0, 0.0, physical))
     return -DERIVATIVE * physical * physical * energy * weight
+
+
+def row_pack(one, two, inner):
+    row = lax.broadcasted_iota(jnp.int32, (NYL, NZ), 0)
+    mid = (row >= 2) & (row < 6)
+    turned = pltpu.roll(two, 4, 0)
+    return jnp.where(mid, one, turned) if inner else jnp.where(mid, turned, one)
 
 
 def around(ref, plane, first, last):
@@ -266,14 +330,16 @@
     y_low,
     sent_a,
     sent_b,
+    lower_outer,
+    upper_outer,
+    start,
     spread,
     sensitivity,
     scaled,
-    lower,
-    upper,
     partial,
     dens,
     energy,
+    outer,
 ):
     def rows(ref, kind):
         return ref[pl.ds(kind * NXL, NXL), :]
@@ -353,13 +419,16 @@
     for x in range(2, NXL - 2):
         carry = out_plane(x, carry)
 
-    here = density[...]
-    kind = passive[...]
-    fixed = jnp.where(kind == 1, 1.0, 0.0)
-    lower[...] = jnp.where(kind == 0, jnp.maximum(here - MOVE_LIMIT, 0.0), fixed)
-    upper[...] = jnp.where(kind == 0, jnp.minimum(here + MOVE_LIMIT, 1.0), fixed)
+    for p in range(PAIRS):
+        outer[p] = row_pack(scaled[2 + 2 * p], scaled[3 + 2 * p], False)
     add_volumes(
-        [(x, x) for x in range(2, NXL - 2)], factors, scaled, lower, upper, None, partial
+        [(p, p) for p in range(PAIRS)],
+        factors,
+        outer,
+        lower_outer,
+        upper_outer,
+        start,
+        partial,
     )
 
 
@@ -636,10 +705,27 @@
     )
     received_a = held(swapped(sent_a, "gy", 1))
     received_b = held(swapped(sent_b, "gy", 0))
-    own_energy, inverse, weights, factors = call(
-        interior_energy,
-        (near(*block), near(2, 16, NZ), near(4, NYL, NZ), near(SLOTS, NZ)),
-        (displacement,),
+    (
+        own_energy,
+        inverse,
+        weights,
+        factors,
+        lower,
+        upper,
+        lower_outer,
+        upper_outer,
+        start,
+    ) = call(
+        interior,
+        (near(*block), near(2, 16, NZ), near(4, NYL, NZ), near(SLOTS, NZ))
+        + (near(*block),) * 2
+        + (near(PAIRS, NYL, NZ),) * 2
+        + (near(8 * SLOTS, NZ),),
+        (density, displacement, passive),
+        [
+            pltpu.VMEM(block, jnp.float32),
+            pltpu.VMEM((3, PAIRS, NYL, NZ), jnp.float32),
+        ],
         cost=1000,
     )
     y_high, y_low, to_a, to_b = call(
@@ -650,9 +736,9 @@
     )
     received_a = held(swapped(to_a, "gx", 1))
     received_b = held(swapped(to_b, "gx", 0))
-    spread, sensitivity, scaled, lower, upper, partial = call(
+    spread, sensitivity, scaled, partial = call(
         middle,
-        (near(NXL, 24, NZ),) + (near(*block),) * 4 + (near(8 * SLOTS, NZ),),
+        (near(NXL, 24, NZ),) + (near(*block),) * 2 + (near(8 * SLOTS, NZ),),
         (
             factors,
             density,
@@ -664,8 +750,15 @@
             y_low,
             sent_a,
             sent_b,
+            lower_outer,
+            upper_outer,
+            start,
         ),
-        [pltpu.VMEM((NXL, 24, NZ), jnp.float32), pltpu.VMEM(block, jnp.float32)],
+        [
+            pltpu.VMEM((NXL, 24, NZ), jnp.float32),
+            pltpu.VMEM(block, jnp.float32),
+            pltpu.VMEM((PAIRS, NYL, NZ), jnp.float32),
+        ],
         cost=5000,
     )
     across, along = reduction_groups(count_x, count_y)

time: 62.5 us -> 62 us (level)
  waiting for transfers between devices: 1.4 us -> 0.31 us
    ppermute x4, waiting for transfers between devices: 1.4 us -> 0.31 us  [swapped(): return lax.ppermute(block, axis, pairs + [(j, i) for i, j in pairs])]
where the time goes in v9:
time: 62 us; the launch traced here: 61.7 us
  blocking collectives  40 us (65%)
  starting transfers between devices  14.6 us (24%)
  Pallas kernels  6.08 us (10%)
  between operations  0.72 us (1%)
    all_to_all x1, blocking collectives, per_device(): lax.all_to_all(volumes, ('gx', 'gy'), 0, 0, axis_index_groups=along)  26.7 us
    ppermute x4, starting transfers between devices, swapped(): return lax.ppermute(block, axis, pairs + [(j, i) for i, j in pairs])  14.6 us
    all_to_all x1, blocking collectives, per_device(): lax.all_to_all(volumes, ('gx', 'gy'), 0, 0, axis_index_groups=across)  13.3 us
    pallas_call x7, Pallas kernels, call(): pl.pallas_call(kernel, out_shape=outputs, in_specs=specs or [VMEM] * len(...  6.08 us
  transfers between devices with their start and end apart: 4, of which 1 were waited for; matrix products, arithmetic and copies ran while one was open for 0% of the time, Pallas kernels for 4%

profile of v9, /device:TPU:1, one launch (start us, length us, event | category | flops | bytes accessed | tf_op | source)
XLA Modules:
  0.0 61.7 jit_solution(15771569590285569596)
XLA Ops:
  0.6 1.1 %shard_map.50 = (f32[16,8,128]{2,1,0:T(8,128)S(1)}, f32[3,16,8,128]{3,2,1,0:T(8,128)S(1)}, s32[16,8,128]{2,1,0:T(8,128)S(1)}, f32[144,128]{1,0:T(8,128)S(1)}, f32[144,128]{1,0:T(8,128)S(1)}) custom-call(f32[16,8,128]{2,1,0:T(8,128)} %density_far.1, f32[3,16,8,128]{3,2,1,0:T(8,128)} %displacement_far.1, s32[16,8,128]{2,1,0:T(8,128)} %passive_far.1), custom_call_target="tpu_custom_call" | custom-call | flops 4000000 | bytes 1000000 | tf_op jit(solution)/shard_map/pallas_call | solution.py:658
  1.7 0.7 %collective-permute-start = (f32[144,128]{1,0:T(8,128)S(1)}, f32[144,128]{1,0:T(8,128)S(1)}, u32[]{:S(2)}, u32[]{:S(2)}) collective-permute-start(f32[144,128]{1,0:T(8,128)S(1)} %get-tuple-element.31.sent_a), channel_id=1, source_target_pairs={{1,2},{3,4},{5,6},{7,8},{9,10},{11,12},{13,14},{2,1},{4,3},{6,5},{... | collective-permute-start | bytes 221192 | tf_op jit(solution)/shard_map/ppermute | solution.py:673
  2.4 6.6 %collective-permute-start.1 = (f32[144,128]{1,0:T(8,128)S(1)}, f32[144,128]{1,0:T(8,128)S(1)}, u32[]{:S(2)}, u32[]{:S(2)}) collective-permute-start(f32[144,128]{1,0:T(8,128)S(1)} %get-tuple-element.32.sent_b), channel_id=1, source_target_pairs={{0,1},{2,3},{4,5},{6,7},{8,9},{10,11},{12,13},{14,15},{1,0},{3,2},... | collective-permute-start | bytes 221192 | tf_op jit(solution)/shard_map/ppermute | solution.py:673
  8.9 1.4 %shard_map.51 = (f32[16,8,128]{2,1,0:T(8,128)S(1)}, f32[2,16,128]{2,1,0:T(8,128)S(1)}, f32[4,8,128]{2,1,0:T(8,128)S(1)}, f32[256,128]{1,0:T(8,128)S(1)}, f32[16,...) custom-call(f32[16,8,128]{2,1,0:T(8,128)S(1)} %get-tuple-element.27., ...), custom_call_target="tpu_custom_call" | custom-call | flops 4000000 | bytes 1000000 | tf_op jit(solution)/shard_map/pallas_call | solution.py:658
  10.4 0.0 collective-permute-done.received_a
  10.4 0.3 collective-permute-done.1.received_b
  10.7 5.3 %collective-permute-start.2 = (f32[104,128]{1,0:T(8,128)S(1)}, f32[104,128]{1,0:T(8,128)S(1)}, u32[]{:S(2)}, u32[]{:S(2)}) collective-permute-start(f32[104,128]{1,0:T(8,128)S(1)} %get-tuple-element.36), channel_id=1, source_target_pairs={{16,32},{48,64},{80,96},{112,128},{144,160},{176,192},{208,224},{2... | collective-permute-start | bytes 159752 | tf_op jit(solution)/shard_map/ppermute | solution.py:673
  16.0 2.1 %collective-permute-start.3 = (f32[104,128]{1,0:T(8,128)S(1)}, f32[104,128]{1,0:T(8,128)S(1)}, u32[]{:S(2)}, u32[]{:S(2)}) collective-permute-start(f32[104,128]{1,0:T(8,128)S(1)} %get-tuple-element.37), channel_id=1, source_target_pairs={{0,16},{32,48},{64,80},{96,112},{128,144},{160,176},{192,208},{224... | collective-permute-start | bytes 159752 | tf_op jit(solution)/shard_map/ppermute | solution.py:673
  18.1 1.4 %shard_map.53 = (f32[16,24,128]{2,1,0:T(8,128)S(1)}, f32[16,8,128]{2,1,0:T(8,128)S(1)}, f32[16,8,128]{2,1,0:T(8,128)S(1)}, f32[2048,128]{1,0:T(8,128)S(1)}) custom-call(f32[256,128]{1,0:T(8,128)S(1)} %get-tuple-element.30.factors, f32[16,8,128]{2,1,0:T(8,128)S(1)} %get-tuple-element.27.density, s32[16,8,128]{2,1,0:T(8,128)S(1)} %get-tuple-element.29.passive, ...), custom_call_target="tpu_custom_call" | custom-call | flops 20000000 | bytes 5000000 | tf_op jit(solution)/shard_map/pallas_call | solution.py:658
  19.5 0.0 collective-permute-done.2.received_a
  19.5 0.0 collective-permute-done.3.received_b
  19.5 1.4 %shard_map.54 = (f32[16,8,128]{2,1,0:T(8,128)S(1)}, f32[4,8,128]{2,1,0:T(8,128)S(1)}, f32[16,2,128]{2,1,0:T(2,128)S(1)}) custom-call(f32[256,128]{1,0:T(8,128)S(1)} %get-tuple-element.30.factors, f32[16,8,128]{2,1,0:T(8,128)S(1)} %get-tuple-element.27.density, f32[3,16,8,128]{3,2,1,0:T(8,128)S(1)} %get-tuple-element.28.displacement, ...), custom_call_target="tpu_custom_call" | custom-call | flops 12000000 | bytes 3000000 | tf_op jit(solution)/shard_map/pallas_call | solution.py:658
  20.9 13.3 %all_to_all.10.received = f32[16,2,128]{2,1,0:T(2,128)S(1)} all-to-all(f32[16,2,128]{2,1,0:T(2,128)S(1)} %get-tuple-element.48), channel_id=1, replica_groups={{0,1,2,3,12,13,14,15,16,17,18,19,28,29,30,31},{4,5,6,7,8,9,10,11,20,21,..., dimensions={0} | all-to-all | bytes 32768 | tf_op jit(solution)/shard_map/all_to_all | solution.py:798
  34.2 26.7 %all_to_all.11.received = f32[32,2,128]{2,1,0:T(2,128)S(1)} all-to-all(f32[32,2,128]{2,1,0:T(2,128)S(1)} %shard_map.55), channel_id=1, replica_groups={{0,4,32,36,64,68,96,100,128,132,160,164,192,196,224,228,256,260,288,292..., dimensions={0} | all-to-all | bytes 65536 | tf_op jit(solution)/shard_map/all_to_all | solution.py:805
  60.9 0.8 %shard_map.56 = (f32[16,8,128]{2,1,0:T(8,128)}, f32[16,8,128]{2,1,0:T(8,128)}) custom-call(f32[32,2,128]{2,1,0:T(2,128)S(1)} %all_to_all.11.received, f32[16,8,128]{2,1,0:T(8,128)S(1)} %get-tuple-element.49.scaled, f32[4,8,128]{2,1,0:T(8,128)S(1)} %get-tuple-element.50.scaled_edge, f32[16,8,128]{2,1,0:T(8,128)S(1)} %get-tuple-element.45.lower, ...), custom_call_target="tpu_custom_call" | custom-call | flops 2000000 | bytes 500000 | tf_op jit(solution)/shard_map/pallas_call | solution.py:658
  (2 shorter events, 0.1 us)
Async XLA Ops:
  1.7 8.7 %collective-permute-start = (f32[144,128]{1,0:T(8,128)S(1)}, f32[144,128]{1,0:T(8,128)S(1)}, u32[]{:S(2)}, u32[]{:S(2)}) collective-permute-start(f32[144,128]{1,0:T(8,128)S(1)} %get-tuple-element.31.sent_a), channel_id=1, source_target_pairs={{1,2},{3,4},{5,6},{7,8},{9,10},{11,12},{13,14},{2,1},{4,3},{6,5},{... | collective-permute-start | bytes 221192 | tf_op jit(solution)/shard_map/ppermute | solution.py:673
  2.4 8.3 %collective-permute-start.1 = (f32[144,128]{1,0:T(8,128)S(1)}, f32[144,128]{1,0:T(8,128)S(1)}, u32[]{:S(2)}, u32[]{:S(2)}) collective-permute-start(f32[144,128]{1,0:T(8,128)S(1)} %get-tuple-element.32.sent_b), channel_id=1, source_target_pairs={{0,1},{2,3},{4,5},{6,7},{8,9},{10,11},{12,13},{14,15},{1,0},{3,2},... | collective-permute-start | bytes 221192 | tf_op jit(solution)/shard_map/ppermute | solution.py:673
  10.7 8.7 %collective-permute-start.2 = (f32[104,128]{1,0:T(8,128)S(1)}, f32[104,128]{1,0:T(8,128)S(1)}, u32[]{:S(2)}, u32[]{:S(2)}) collective-permute-start(f32[104,128]{1,0:T(8,128)S(1)} %get-tuple-element.36), channel_id=1, source_target_pairs={{16,32},{48,64},{80,96},{112,128},{144,160},{176,192},{208,224},{2... | collective-permute-start | bytes 159752 | tf_op jit(solution)/shard_map/ppermute | solution.py:673
  16.0 3.5 %collective-permute-start.3 = (f32[104,128]{1,0:T(8,128)S(1)}, f32[104,128]{1,0:T(8,128)S(1)}, u32[]{:S(2)}, u32[]{:S(2)}) collective-permute-start(f32[104,128]{1,0:T(8,128)S(1)} %get-tuple-element.37), channel_id=1, source_target_pairs={{0,16},{32,48},{64,80},{96,112},{128,144},{160,176},{192,208},{224... | collective-permute-start | bytes 159752 | tf_op jit(solution)/shard_map/ppermute | solution.py:673

commit v10 on v9

--- a/solution.py
+++ b/solution.py
@@ -316,7 +316,7 @@
             partial[pl.ds(base + 8 * k, 8), :] = totals[k]
         return carry
 
-    lax.fori_loop(0, SLOTS // GROUP, volume_group, 0)
+    lax.fori_loop(0, SLOTS // GROUP, volume_group, 0, unroll=4)
 
 
 def middle(

time: 62 us -> 61.9 us (level)
  no operation moved by 1% of the time
where the time goes in v10:
time: 61.9 us; the launch traced here: 61.6 us
  blocking collectives  40.1 us (65%)
  starting transfers between devices  14.6 us (24%)
  Pallas kernels  5.81 us (9%)
  between operations  0.72 us (1%)
    all_to_all x1, blocking collectives, per_device(): lax.all_to_all(volumes, ('gx', 'gy'), 0, 0, axis_index_groups=along)  26.8 us
    ppermute x4, starting transfers between devices, swapped(): return lax.ppermute(block, axis, pairs + [(j, i) for i, j in pairs])  14.6 us
    all_to_all x1, blocking collectives, per_device(): lax.all_to_all(volumes, ('gx', 'gy'), 0, 0, axis_index_groups=across)  13.3 us
    pallas_call x7, Pallas kernels, call(): pl.pallas_call(kernel, out_shape=outputs, in_specs=specs or [VMEM] * len(...  5.81 us
  transfers between devices with their start and end apart: 4, of which 1 were waited for; matrix products, arithmetic and copies ran while one was open for 0% of the time, Pallas kernels for 4%

profile of v10, /device:TPU:1, one launch (start us, length us, event | category | flops | bytes accessed | tf_op | source)
XLA Modules:
  0.0 61.6 jit_solution(2936197099839071612)
XLA Ops:
  0.6 1.1 %shard_map.50 = (f32[16,8,128]{2,1,0:T(8,128)S(1)}, f32[3,16,8,128]{3,2,1,0:T(8,128)S(1)}, s32[16,8,128]{2,1,0:T(8,128)S(1)}, f32[144,128]{1,0:T(8,128)S(1)}, f32[144,128]{1,0:T(8,128)S(1)}) custom-call(f32[16,8,128]{2,1,0:T(8,128)} %density_far.1, f32[3,16,8,128]{3,2,1,0:T(8,128)} %displacement_far.1, s32[16,8,128]{2,1,0:T(8,128)} %passive_far.1), custom_call_target="tpu_custom_call" | custom-call | flops 4000000 | bytes 1000000 | tf_op jit(solution)/shard_map/pallas_call | solution.py:658
  1.7 0.7 %collective-permute-start = (f32[144,128]{1,0:T(8,128)S(1)}, f32[144,128]{1,0:T(8,128)S(1)}, u32[]{:S(2)}, u32[]{:S(2)}) collective-permute-start(f32[144,128]{1,0:T(8,128)S(1)} %get-tuple-element.31.sent_a), channel_id=1, source_target_pairs={{1,2},{3,4},{5,6},{7,8},{9,10},{11,12},{13,14},{2,1},{4,3},{6,5},{... | collective-permute-start | bytes 221192 | tf_op jit(solution)/shard_map/ppermute | solution.py:673
  2.4 6.6 %collective-permute-start.1 = (f32[144,128]{1,0:T(8,128)S(1)}, f32[144,128]{1,0:T(8,128)S(1)}, u32[]{:S(2)}, u32[]{:S(2)}) collective-permute-start(f32[144,128]{1,0:T(8,128)S(1)} %get-tuple-element.32.sent_b), channel_id=1, source_target_pairs={{0,1},{2,3},{4,5},{6,7},{8,9},{10,11},{12,13},{14,15},{1,0},{3,2},... | collective-permute-start | bytes 221192 | tf_op jit(solution)/shard_map/ppermute | solution.py:673
  8.9 1.3 %shard_map.51 = (f32[16,8,128]{2,1,0:T(8,128)S(1)}, f32[2,16,128]{2,1,0:T(8,128)S(1)}, f32[4,8,128]{2,1,0:T(8,128)S(1)}, f32[256,128]{1,0:T(8,128)S(1)}, f32[16,...) custom-call(f32[16,8,128]{2,1,0:T(8,128)S(1)} %get-tuple-element.27., ...), custom_call_target="tpu_custom_call" | custom-call | flops 4000000 | bytes 1000000 | tf_op jit(solution)/shard_map/pallas_call | solution.py:658
  10.3 0.0 collective-permute-done.received_a
  10.3 0.4 collective-permute-done.1.received_b
  10.7 5.3 %collective-permute-start.2 = (f32[104,128]{1,0:T(8,128)S(1)}, f32[104,128]{1,0:T(8,128)S(1)}, u32[]{:S(2)}, u32[]{:S(2)}) collective-permute-start(f32[104,128]{1,0:T(8,128)S(1)} %get-tuple-element.36), channel_id=1, source_target_pairs={{16,32},{48,64},{80,96},{112,128},{144,160},{176,192},{208,224},{2... | collective-permute-start | bytes 159752 | tf_op jit(solution)/shard_map/ppermute | solution.py:673
  16.0 2.1 %collective-permute-start.3 = (f32[104,128]{1,0:T(8,128)S(1)}, f32[104,128]{1,0:T(8,128)S(1)}, u32[]{:S(2)}, u32[]{:S(2)}) collective-permute-start(f32[104,128]{1,0:T(8,128)S(1)} %get-tuple-element.37), channel_id=1, source_target_pairs={{0,16},{32,48},{64,80},{96,112},{128,144},{160,176},{192,208},{224... | collective-permute-start | bytes 159752 | tf_op jit(solution)/shard_map/ppermute | solution.py:673
  18.1 1.3 %shard_map.53 = (f32[16,24,128]{2,1,0:T(8,128)S(1)}, f32[16,8,128]{2,1,0:T(8,128)S(1)}, f32[16,8,128]{2,1,0:T(8,128)S(1)}, f32[2048,128]{1,0:T(8,128)S(1)}) custom-call(f32[256,128]{1,0:T(8,128)S(1)} %get-tuple-element.30.factors, f32[16,8,128]{2,1,0:T(8,128)S(1)} %get-tuple-element.27.density, s32[16,8,128]{2,1,0:T(8,128)S(1)} %get-tuple-element.29.passive, ...), custom_call_target="tpu_custom_call" | custom-call | flops 20000000 | bytes 5000000 | tf_op jit(solution)/shard_map/pallas_call | solution.py:658
  19.4 0.0 collective-permute-done.2.received_a
  19.4 0.0 collective-permute-done.3.received_b
  19.4 1.3 %shard_map.54 = (f32[16,8,128]{2,1,0:T(8,128)S(1)}, f32[4,8,128]{2,1,0:T(8,128)S(1)}, f32[16,2,128]{2,1,0:T(2,128)S(1)}) custom-call(f32[256,128]{1,0:T(8,128)S(1)} %get-tuple-element.30.factors, f32[16,8,128]{2,1,0:T(8,128)S(1)} %get-tuple-element.27.density, f32[3,16,8,128]{3,2,1,0:T(8,128)S(1)} %get-tuple-element.28.displacement, ...), custom_call_target="tpu_custom_call" | custom-call | flops 12000000 | bytes 3000000 | tf_op jit(solution)/shard_map/pallas_call | solution.py:658
  20.7 13.3 %all_to_all.10.received = f32[16,2,128]{2,1,0:T(2,128)S(1)} all-to-all(f32[16,2,128]{2,1,0:T(2,128)S(1)} %get-tuple-element.48), channel_id=1, replica_groups={{0,1,2,3,12,13,14,15,16,17,18,19,28,29,30,31},{4,5,6,7,8,9,10,11,20,21,..., dimensions={0} | all-to-all | bytes 32768 | tf_op jit(solution)/shard_map/all_to_all | solution.py:798
  34.0 26.8 %all_to_all.11.received = f32[32,2,128]{2,1,0:T(2,128)S(1)} all-to-all(f32[32,2,128]{2,1,0:T(2,128)S(1)} %shard_map.55), channel_id=1, replica_groups={{0,4,32,36,64,68,96,100,128,132,160,164,192,196,224,228,256,260,288,292..., dimensions={0} | all-to-all | bytes 65536 | tf_op jit(solution)/shard_map/all_to_all | solution.py:805
  60.8 0.8 %shard_map.56 = (f32[16,8,128]{2,1,0:T(8,128)}, f32[16,8,128]{2,1,0:T(8,128)}) custom-call(f32[32,2,128]{2,1,0:T(2,128)S(1)} %all_to_all.11.received, f32[16,8,128]{2,1,0:T(8,128)S(1)} %get-tuple-element.49.scaled, f32[4,8,128]{2,1,0:T(8,128)S(1)} %get-tuple-element.50.scaled_edge, f32[16,8,128]{2,1,0:T(8,128)S(1)} %get-tuple-element.45.lower, ...), custom_call_target="tpu_custom_call" | custom-call | flops 2000000 | bytes 500000 | tf_op jit(solution)/shard_map/pallas_call | solution.py:658
  (2 shorter events, 0.1 us)
Async XLA Ops:
  1.7 8.6 %collective-permute-start = (f32[144,128]{1,0:T(8,128)S(1)}, f32[144,128]{1,0:T(8,128)S(1)}, u32[]{:S(2)}, u32[]{:S(2)}) collective-permute-start(f32[144,128]{1,0:T(8,128)S(1)} %get-tuple-element.31.sent_a), channel_id=1, source_target_pairs={{1,2},{3,4},{5,6},{7,8},{9,10},{11,12},{13,14},{2,1},{4,3},{6,5},{... | collective-permute-start | bytes 221192 | tf_op jit(solution)/shard_map/ppermute | solution.py:673
  2.4 8.3 %collective-permute-start.1 = (f32[144,128]{1,0:T(8,128)S(1)}, f32[144,128]{1,0:T(8,128)S(1)}, u32[]{:S(2)}, u32[]{:S(2)}) collective-permute-start(f32[144,128]{1,0:T(8,128)S(1)} %get-tuple-element.32.sent_b), channel_id=1, source_target_pairs={{0,1},{2,3},{4,5},{6,7},{8,9},{10,11},{12,13},{14,15},{1,0},{3,2},... | collective-permute-start | bytes 221192 | tf_op jit(solution)/shard_map/ppermute | solution.py:673
  10.7 8.6 %collective-permute-start.2 = (f32[104,128]{1,0:T(8,128)S(1)}, f32[104,128]{1,0:T(8,128)S(1)}, u32[]{:S(2)}, u32[]{:S(2)}) collective-permute-start(f32[104,128]{1,0:T(8,128)S(1)} %get-tuple-element.36), channel_id=1, source_target_pairs={{16,32},{48,64},{80,96},{112,128},{144,160},{176,192},{208,224},{2... | collective-permute-start | bytes 159752 | tf_op jit(solution)/shard_map/ppermute | solution.py:673
  16.0 3.4 %collective-permute-start.3 = (f32[104,128]{1,0:T(8,128)S(1)}, f32[104,128]{1,0:T(8,128)S(1)}, u32[]{:S(2)}, u32[]{:S(2)}) collective-permute-start(f32[104,128]{1,0:T(8,128)S(1)} %get-tuple-element.37), channel_id=1, source_target_pairs={{0,16},{32,48},{64,80},{96,112},{128,144},{160,176},{192,208},{224... | collective-permute-start | bytes 159752 | tf_op jit(solution)/shard_map/ppermute | solution.py:673
